TPU v7x, 32 devices: a whole 2x2x4 slice. The times are simulated.
32 devices in a mesh: ctx: 8 (over z, core), hid: 4 (over y, x).
Axes of the slice: x: 2, y: 2, z: 4, core: 2. Of those that a mesh axis runs over, the one named last changes fastest.
Arguments:
- tokens: bfloat16 [1, 32768, 4096], P(None, 'ctx', 'hid'), may hold values from -40 to 40
- seq_inner: bfloat16 [256, 256], replicated, may hold values from -0.375 to 0.375
- seq_outer: bfloat16 [128, 128], replicated, may hold values from -0.5 to 0.5
- inv_outer: bfloat16 [128, 128], replicated, may hold values from -0.5 to 0.5
- inv_inner: bfloat16 [256, 256], replicated, may hold values from -0.375 to 0.375
- twiddle_in: float32 [128, 256], P('ctx'), may hold values from -1.7 to 1.7
- twiddle_out: float32 [128, 256], P(None, 'ctx'), may hold values from -1.7 to 1.7
- freq_kernel: bfloat16 [128, 256, 4096], P('ctx', None, 'hid'), may hold values from -4 to 4
- first_gain: float32 [4096], P('hid'), may hold values from 0.25 to 1.75
- second_gain: float32 [4096], P('hid'), may hold values from 0.25 to 1.75
- right_up: bfloat16 [64, 64, 64], P('hid'), may hold values from -0.75 to 0.75
- left_up: bfloat16 [64, 64, 128], P('hid'), may hold values from -0.75 to 0.75
- right_down: bfloat16 [64, 128, 64], P('hid'), may hold values from -0.5 to 0.5
- left_down: bfloat16 [64, 64, 64], P('hid'), may hold values from -0.75 to 0.75
Outputs:
- block_out: bfloat16 [1, 32768, 4096], P(None, 'ctx', 'hid')
All inputs are finite; a program needn't handle non-finite values.
Results may differ from a plain program's by a relative error of at most 0.0085.
Values may be sent and summed in bfloat16 or wider, within the bound.
No kernel may reach another device: no remote copies, remote signals or barrier semaphores. Data moves between devices by JAX's collectives and lax.ppermute only.
A program may use at most 192 MiB of HBM per device.

v0:
```python
import jax
import jax.numpy as jnp
from jax import lax
from jax.sharding import PartitionSpec as P

SB = 256
NB = 64
D = 4096


EPS = 1e-06


def shards(
    tokens,
    seq_inner,
    seq_outer,
    inv_outer,
    inv_inner,
    twiddle_in,
    twiddle_out,
    freq_kernel,
    first_gain,
    second_gain,
    right_up,
    left_up,
    right_down,
    left_down,
):
    seq_count, tok_count, chan_local = tokens.shape
    sa_local = tok_count // SB
    wide = tokens.astype(jnp.float32)
    first_sums = lax.psum(jnp.sum(wide * wide, axis=2), "hid")
    normed = (wide * (first_gain * lax.rsqrt(first_sums[:, :, None] / D + EPS))).astype(
        jnp.bfloat16
    )
    grid = normed.reshape(seq_count, sa_local, SB, chan_local)
    inner_mix = jnp.einsum("qb,sabc->saqc", seq_inner, grid, preferred_element_type=jnp.float32)
    inner_mix = (inner_mix * twiddle_in[None, :, :, None]).astype(jnp.bfloat16)
    spread = lax.all_to_all(inner_mix, "ctx", split_axis=2, concat_axis=1, tiled=True)
    outer_mix = jnp.einsum(
        "pa,saqc->spqc", seq_outer, spread, preferred_element_type=jnp.float32
    ).astype(jnp.bfloat16)
    at_rows = lax.all_to_all(outer_mix, "ctx", split_axis=1, concat_axis=2, tiled=True)
    scaled = (at_rows.astype(jnp.float32) * freq_kernel[None].astype(jnp.float32)).astype(
        jnp.bfloat16
    )
    filtered = lax.all_to_all(scaled, "ctx", split_axis=2, concat_axis=1, tiled=True)
    backed = jnp.einsum("rp,spqc->srqc", inv_outer, filtered, preferred_element_type=jnp.float32)
    backed = (backed * twiddle_out[None, :, :, None]).astype(jnp.bfloat16)
    home = lax.all_to_all(backed, "ctx", split_axis=1, concat_axis=2, tiled=True)
    conv = jnp.einsum("eq,srqc->srec", inv_inner, home, preferred_element_type=jnp.float32)
    conv = conv.reshape(seq_count, tok_count, chan_local)
    mixed = wide + conv * jax.nn.silu(normed.astype(jnp.float32))
    second_sums = lax.psum(jnp.sum(mixed * mixed, axis=2), "hid")
    normed_two = (mixed * (second_gain * lax.rsqrt(second_sums[:, :, None] / D + EPS))).astype(
        jnp.bfloat16
    )
    block_local = right_up.shape[0]
    flat = normed_two.reshape(seq_count * tok_count, block_local, NB)
    projected = jnp.einsum(
        "tij,ijk->ikt", flat, right_up, preferred_element_type=jnp.float32
    ).astype(jnp.bfloat16)
    hidden = jnp.einsum(
        "ikt,kim->kmt",
        lax.all_to_all(projected, "hid", split_axis=1, concat_axis=0, tiled=True),
        left_up,
        preferred_element_type=jnp.float32,
    )
    active = jax.nn.gelu(hidden, approximate=True).astype(jnp.bfloat16)
    reduced = jnp.einsum(
        "kmt,kmq->kqt", active, right_down, preferred_element_type=jnp.float32
    ).astype(jnp.bfloat16)
    returned = lax.all_to_all(reduced, "hid", split_axis=1, concat_axis=0, tiled=True)
    result = jnp.einsum("kqt,qkr->tqr", returned, left_down, preferred_element_type=jnp.float32)
    return (mixed + result.reshape(seq_count, tok_count, chan_local)).astype(jnp.bfloat16)


def solution(mesh):
    return jax.shard_map(
        shards,
        mesh=mesh,
        in_specs=(
            P(None, "ctx", "hid"),
            P(),
            P(),
            P(),
            P(),
            P("ctx", None),
            P(None, "ctx"),
            P("ctx", None, "hid"),
            P("hid"),
            P("hid"),
            P("hid", None, None),
            P("hid", None, None),
            P("hid", None, None),
            P("hid", None, None),
        ),
        out_specs=P(None, "ctx", "hid"),
        check_vma=False,
    )
```

profile of v0, /device:TPU:0, one launch (start us, length us, event | category | flops | bytes accessed | tf_op | source)
XLA Modules:
  0.0 1358.4 jit_solution(6014883153161361301)
XLA Ops:
  0.0 0.0 copy-start
  0.0 12.0 copy.61
  12.0 5.1 fusion.12
  17.0 17.8 %psum.14 = f32[1,4096]{1,0:T(1,128)S(1)} all-reduce(f32[1,4096]{1,0:T(1,128)S(1)} %bitcast.121), channel_id=1, replica_groups=mesh['ctx'=8,'hid'=4] {'hid'}, use_global_device_ids=true, to_apply=%region_1.0 | all-reduce | flops 4096 | bytes 32768 | tf_op jit(solution)/shard_map/psum | solution.py:33
  34.8 0.0 copy-done.6
  34.8 10.1 fusion.13
  45.0 9.8 copy.88
  54.7 0.0 copy-done.11
  54.7 11.8 fusion.30
  66.5 12.4 copy.63
  78.9 189.9 %all_to_all.90 = bf16[1,16,256,1024]{3,1,0,2:T(8,128)(2,1)} all-to-all(bf16[1,16,256,1024]{3,1,0,2:T(8,128)(2,1)} %copy.63), channel_id=1, replica_groups=mesh['ctx'=8,'hid'=4] {'ctx'}, dimensions={2} | all-to-all | bytes 16777216 | tf_op jit(solution)/shard_map/all_to_all | solution.py:40
  268.7 11.3 copy.64
  280.0 8.5 copy.65
  288.5 22.3 %convert_bitcast_fusion.3 = bf16[1,128,32,1024]{1,3,2,0:T(8,128)(2,1)} fusion(bf16[128,32,1024]{2,1,0:T(8,128)(2,1)} %bitcast.107, bf16[128,128]{1,0:T(8,128)(2,1)S(1)} %copy-done.3), kind=kOutput, calls=%fused_computation.39 | convolution fusion | flops 1077936128 | bytes 16809984 | tf_op jit(solution)/shard_map/pa,saqc->spqc/dot_general | solution.py:41
  310.8 12.4 copy.67
  323.2 190.0 %all_to_all.91 = bf16[1,128,32,1024]{3,2,0,1:T(8,128)(2,1)} all-to-all(bf16[1,128,32,1024]{3,2,0,1:T(8,128)(2,1)} %copy.67), channel_id=1, replica_groups=mesh['ctx'=8,'hid'=4] {'ctx'}, dimensions={1} | all-to-all | bytes 16777216 | tf_op jit(solution)/shard_map/all_to_all | solution.py:44
  513.3 11.5 convert_bitcast_fusion
  524.8 7.1 copy.69
  531.9 0.0 slice-done
  531.9 0.0 slice-done.1
  531.9 5.4 fusion.21
  537.4 11.3 copy.70
  548.7 189.9 %all_to_all.92 = bf16[1,16,256,1024]{3,1,0,2:T(8,128)(2,1)} all-to-all(bf16[1,16,256,1024]{3,1,0,2:T(8,128)(2,1)} %copy.70), channel_id=1, replica_groups=mesh['ctx'=8,'hid'=4] {'ctx'}, dimensions={2} | all-to-all | bytes 16777216 | tf_op jit(solution)/shard_map/all_to_all | solution.py:48
  738.5 11.3 copy.71
  749.9 8.5 copy.72
  758.3 22.5 %fusion.15 = bf16[1,128,32,1024]{1,3,2,0:T(8,128)(2,1)} fusion(bf16[128,32,1024]{2,1,0:T(8,128)(2,1)} %bitcast.105, f32[128,32]{0,1:T(8,128)S(1)} %copy-done.5, bf16[128,128]{1,0:T(8,128)(2,1)S(1)} %copy-done.4), kind=kOutput, calls=%fused_computation.23 | convolution fusion | flops 1082130432 | bytes 16826368 | tf_op jit(solution)/shard_map/rp,spqc->srqc/dot_general | solution.py:49
  780.8 12.4 copy.74
  793.2 190.1 %all_to_all.93 = bf16[1,128,32,1024]{3,2,0,1:T(8,128)(2,1)} all-to-all(bf16[1,128,32,1024]{3,2,0,1:T(8,128)(2,1)} %copy.74), channel_id=1, replica_groups=mesh['ctx'=8,'hid'=4] {'ctx'}, dimensions={1} | all-to-all | bytes 16777216 | tf_op jit(solution)/shard_map/all_to_all | solution.py:51
  983.2 8.5 copy.75
  991.7 11.5 fusion.33
  1003.3 17.5 %copy.76 = f32[1,4096,1024]{1,2,0:T(8,128)} copy(f32[1,4096,1024]{2,1,0:T(8,128)} %bitcast.100) | data formatting | bytes 33554432 | tf_op jit(solution)/shard_map/reshape | solution.py:53
  1020.7 16.7 %multiply_reduce_fusion = (f32[4096]{0:T(1024)S(1)}, f32[1,4096,1024]{1,2,0:T(8,128)}) fusion(f32[1,4096,1024]{1,2,0:T(8,128)} %copy.76, f32[4096]{0:T(1024)S(1)} %bitcast.118, f32[1024]{0:T(1024)S(1)} %copy-done.6, bf16[1,4096,1024]{1,2,0:T(8,128)(2,1)} %copy.61), kind=kLoop, calls=%fused_computation.28 | loop fusion | flops 54521856 | bytes 41979904 | tf_op jit(solution)/shard_map/reduce_sum | solution.py:55
  1037.5 14.0 %psum.15 = f32[1,4096]{1,0:T(1,128)S(1)} all-reduce(f32[1,4096]{1,0:T(1,128)S(1)} %bitcast.119), channel_id=1, replica_groups=mesh['ctx'=8,'hid'=4] {'hid'}, use_global_device_ids=true, to_apply=%region_3.4 | all-reduce | flops 4096 | bytes 32768 | tf_op jit(solution)/shard_map/psum | solution.py:55
  1051.5 0.0 copy-done.7
  1051.5 9.6 multiply_convert_fusion
  1061.0 0.0 copy-done
  1061.0 9.0 convert_bitcast_fusion.2
  1070.0 11.4 copy.78
  1081.4 97.2 %all_to_all.94 = bf16[16,64,4096]{2,0,1:T(8,128)(2,1)} all-to-all(bf16[16,64,4096]{2,0,1:T(8,128)(2,1)} %copy.78), channel_id=1, replica_groups=mesh['ctx'=8,'hid'=4] {'hid'}, dimensions={1} | all-to-all | bytes 16777216 | tf_op jit(solution)/shard_map/all_to_all | solution.py:66
  1178.6 7.9 copy.79
  1186.5 18.4 %convert_bitcast_fusion.1 = bf16[16,64,4096]{2,1,0:T(8,128)(2,1)} fusion(bf16[16,128,64]{1,2,0:T(8,128)(2,1)S(1)} %copy-done.8, bf16[64,16,4096]{2,0,1:T(8,128)(2,1)} %bitcast.114, bf16[16,64,128]{2,1,0:T(8,128)(2,1)S(1)} %copy-done.9), kind=kOutput, calls=%fused_computation.37 | convolution fusion | flops 2227175424 | bytes 17301504 | tf_op jit(solution)/shard_map/kmt,kmq->kqt/dot_general | solution.py:71
  1205.0 11.4 copy.81
  1216.3 95.6 %all_to_all.95 = bf16[16,64,4096]{2,0,1:T(8,128)(2,1)} all-to-all(bf16[16,64,4096]{2,0,1:T(8,128)(2,1)} %copy.81), channel_id=1, replica_groups=mesh['ctx'=8,'hid'=4] {'hid'}, dimensions={1} | all-to-all | bytes 16777216 | tf_op jit(solution)/shard_map/all_to_all | solution.py:74
  1311.9 7.9 copy.82
  1319.9 0.0 copy-done.1
  1319.9 11.5 fusion.42
  1331.3 14.9 %fusion.14 = bf16[1,4096,1024]{1,2,0:T(8,128)(2,1)} fusion(f32[1,4096,1024]{1,2,0:T(8,128)} %get-tuple-element.6, f32[1,4096,1024]{1,2,0:T(8,128)} %bitcast.98), kind=kLoop, calls=%fused_computation.21 | loop fusion | flops 8388608 | bytes 41943040 | tf_op jit(solution)/shard_map/convert_element_type | solution.py:76
  1346.3 11.9 copy.84
  (23 shorter events, 0.1 us)
Async XLA Ops:
  0.0 1061.0 %copy-start = (bf16[16,64,64]{2,1,0:T(8,128)(2,1)S(1)}, bf16[16,64,64]{2,1,0:T(8,128)(2,1)}, u32[]{:S(2)}) copy-start(bf16[16,64,64]{2,1,0:T(8,128)(2,1)} %param.24) | copy-start | bytes 393220
  12.0 22.9 %copy-start.6 = (f32[1024]{0:T(1024)S(1)}, f32[1024]{0:T(1024)}, u32[]{:S(2)}) copy-start(f32[1024]{0:T(1024)} %param.22) | copy-start | bytes 12292
  45.0 9.8 copy-start.10
  45.0 9.8 copy-start.11
  280.0 8.5 copy-start.3
  513.3 18.7 %slice-start = ((s8[8388608]{0:T(1024)(128)(4,1)}), s8[4194304]{0:T(1024)(128)(4,1)S(1)}, s32[]{:S(2)}) async-start(s8[8388608]{0:T(1024)(128)(4,1)} %bitcast.115), calls=%async_computation.6 | async-start | bytes 8388608
  524.8 7.1 slice-start.1
  749.9 8.5 copy-start.4
  749.9 8.5 copy-start.5
  983.2 8.5 copy-start.2
  1020.7 30.7 %copy-start.7 = (f32[1024]{0:T(1024)S(1)}, f32[1024]{0:T(1024)}, u32[]{:S(2)}) copy-start(f32[1024]{0:T(1024)} %param.23) | copy-start | bytes 12292
  1178.6 8.0 copy-start.8
  1178.6 8.0 copy-start.9
  1311.9 7.9 copy-start.1
where the time goes:
time: 1360 us
  blocking collectives  984 us (72%)
  local copies, waits for them, and re-layouts  193 us (14%)
  matrix products  107 us (8%)
  other arithmetic  73.4 us (5%)
    all_to_all x1, blocking collectives, shards(): lax.all_to_all(backed, 'ctx', split_axis=1, concat_axis=2, tiled=True)  190 us
    all_to_all x1, blocking collectives, shards(): lax.all_to_all(outer_mix, 'ctx', split_axis=1, concat_axis=2, tiled=True)  190 us
    all_to_all x1, blocking collectives, shards(): lax.all_to_all(inner_mix, 'ctx', split_axis=2, concat_axis=1, tiled=True)  190 us
    all_to_all x1, blocking collectives, shards(): lax.all_to_all(scaled, 'ctx', split_axis=2, concat_axis=1, tiled=True)  190 us
    all_to_all x1, blocking collectives, shards(): lax.all_to_all(projected, 'hid', split_axis=1, concat_axis=0, tiled=True)  97.2 us
    all_to_all x1, blocking collectives, shards(): lax.all_to_all(reduced, 'hid', split_axis=1, concat_axis=0, tiled=True)  95.6 us

commit v1 on v0

v1 whole, which is shorter than its diff:
```python
import math

import jax
import jax.numpy as jnp
from jax import lax
from jax.experimental import pallas as pl
from jax.experimental.pallas import tpu as pltpu
from jax.sharding import PartitionSpec as P

EPS = 1e-06
G = 16
ROWS = 256
BF = jnp.bfloat16
F32 = jnp.float32

RETURN_SPLIT = (4, 4, 4, 2, 2)
CHANNEL_SPLIT = (3, 1)


def cost(flops, moved, exps=0):
    return pl.CostEstimate(flops=int(flops), bytes_accessed=int(moved), transcendentals=int(exps))


def dot(a, b):
    return jnp.dot(a, b, preferred_element_type=F32)


def whole(shape):
    zeros = (0,) * len(shape)
    return pl.BlockSpec(shape, lambda *_: zeros, pipeline_mode=pl.Buffered(1))


def xor_blocks(x, axis, me, parts):
    size = x.shape[axis] // parts
    return jnp.concatenate(
        [lax.dynamic_slice_in_dim(x, (me ^ d) * size, size, axis) for d in range(parts)], axis
    )


def swap(x, name, size, d):
    return lax.ppermute(x, name, [(i, i ^ d) for i in range(size)])


def exchange(pieces, name, size):
    order = sorted(range(1, size), key=lambda d: -d)
    got = {d: swap(pieces[d], name, size, d) for d in order}
    return [pieces[0]] + [got[d] for d in range(1, size)]


def inner_kernel(parts, splits, tok, scale, gain, mix, twiddle, *outs):
    normed = (tok[...].astype(F32) * (gain[...] * scale[...])).astype(BF)
    mixed = (dot(mix[...], normed) * twiddle[0]).astype(BF)
    rows = mixed.shape[0] // parts
    for d in range(parts):
        start = 0
        for f, width in enumerate(splits):
            outs[f * parts + d][0] = mixed[d * rows : (d + 1) * rows, start : start + width]
            start += width


def inner(tokens, scale, gain, mix, twiddle, parts, splits):
    count, chans = tokens.shape
    block = mix.shape[0]
    rows = count // block
    ql = block // parts
    return pl.pallas_call(
        lambda *refs: inner_kernel(parts, splits, *refs),
        grid=(rows,),
        in_specs=[
            pl.BlockSpec((block, chans), lambda a: (a, 0)),
            pl.BlockSpec((block, 1), lambda a: (a, 0)),
            whole((1, chans)),
            whole((block, block)),
            pl.BlockSpec((1, block, 1), lambda a: (a, 0, 0)),
        ],
        out_specs=[
            pl.BlockSpec((1, ql, width), lambda a: (a, 0, 0)) for width in splits for _ in range(parts)
        ],
        out_shape=[
            jax.ShapeDtypeStruct((rows, ql, width), BF) for width in splits for _ in range(parts)
        ],
        cost_estimate=cost(2 * count * block * chans, 4 * count * chans),
        name="inner_mix",
    )(tokens, scale, gain, mix, twiddle)


def outer_kernel(parts, sizes, *refs):
    pieces = refs[:parts]
    kern, fwd, back, twiddle = refs[parts : parts + 4]
    outs = refs[-parts * len(sizes) :]
    width = kern.shape[-1]
    x = jnp.concatenate([p[...].reshape(-1, width) for p in pieces], axis=0)
    mixed = dot(fwd[...], x).astype(BF)
    filtered = (mixed.astype(F32) * kern[...].reshape(-1, width).astype(F32)).astype(BF)
    backed = (dot(back[...], filtered) * twiddle[0]).astype(BF)
    row = 0
    for d in range(parts):
        for j, size in enumerate(sizes):
            outs[j * parts + d][...] = backed[row * G : (row + size) * G].reshape(size, G, width)
            row += size


def outer(pieces, kern, fwd, back, twiddle, sizes, start, carried):
    parts = len(pieces)
    rows, ql, width = pieces[0].shape
    chans = kern.shape[-1]
    side = fwd.shape[0]
    cb = math.gcd(math.gcd(width, start), 256)
    first = start // cb
    aliases = {} if carried is None else {parts + 4 + i: i for i in range(len(carried))}
    extra = [] if carried is None else list(carried)
    return pl.pallas_call(
        lambda *refs: outer_kernel(parts, sizes, *refs),
        grid=(width // cb, ql // G),
        in_specs=[pl.BlockSpec((rows, G, cb), lambda c, q: (0, q, c)) for _ in range(parts)]
        + [
            pl.BlockSpec((parts, rows, G, cb), lambda c, q: (0, 0, q, c + first)),
            whole((side, side)),
            whole((side, side)),
            pl.BlockSpec((1, side, 1), lambda c, q: (q, 0, 0)),
        ]
        + [pl.BlockSpec(memory_space=pl.ANY) for _ in extra],
        out_specs=[
            pl.BlockSpec((size, G, cb), lambda c, q: (0, q, c + first)) for size in sizes for _ in range(parts)
        ],
        out_shape=[jax.ShapeDtypeStruct((size, ql, chans), BF) for size in sizes for _ in range(parts)],
        input_output_aliases=aliases,
        cost_estimate=cost(4 * side * side * ql // G * width, 6 * side * ql // G * width),
        name="outer_mix",
    )(*pieces, kern, fwd, back, twiddle, *extra)


def mix_kernel(parts, groups, *refs):
    pieces = refs[:parts]
    tok, scale, gain, gain_two, back, up = refs[parts : parts + 6]
    mixed_out = refs[parts + 6]
    outs = refs[parts + 7 :]
    home = jnp.concatenate([p[0] for p in pieces], axis=0)
    conv = dot(back[...], home)
    wide = tok[...].astype(F32)
    normed = (wide * (gain[...] * scale[...])).astype(BF).astype(F32)
    mixed = wide + conv * (normed / (1.0 + jnp.exp(-normed)))
    mixed_out[...] = mixed
    sums = jnp.sum(mixed * mixed, axis=1, keepdims=True)
    high = sums.astype(BF)
    rest = sums - high.astype(F32)
    mid = rest.astype(BF)
    low = rest - mid.astype(F32)
    lane = lax.broadcasted_iota(jnp.int32, (mixed.shape[0], 128), 1)
    tail = jnp.where(
        lane == 0,
        high.astype(F32),
        jnp.where(lane == 1, mid.astype(F32), jnp.where(lane == 2, low, 0.0)),
    ).astype(BF)
    projected = dot((mixed * gain_two[...]).astype(BF), up[...]).astype(BF)
    width = projected.shape[1] // groups
    for d in range(groups):
        outs[d][:, :width] = projected[:, d * width : (d + 1) * width]
        outs[d][:, width:] = tail


def mix(pieces, tokens, scale, gain, gain_two, back, up, row, groups):
    parts = len(pieces)
    size, ql, chans = pieces[0].shape
    block = ql * parts
    count = size * block
    width = up.shape[1] // groups
    return pl.pallas_call(
        lambda *refs: mix_kernel(parts, groups, *refs),
        grid=(size,),
        in_specs=[pl.BlockSpec((1, ql, chans), lambda r: (r, 0, 0)) for _ in range(parts)]
        + [
            pl.BlockSpec((block, chans), lambda r: (r + row, 0)),
            pl.BlockSpec((block, 1), lambda r: (r + row, 0)),
            whole((1, chans)),
            whole((1, chans)),
            whole((block, block)),
            whole(up.shape),
        ],
        out_specs=[pl.BlockSpec((block, chans), lambda r: (r, 0))]
        + [pl.BlockSpec((block, width + 128), lambda r: (r, 0)) for _ in range(groups)],
        out_shape=[jax.ShapeDtypeStruct((count, chans), F32)]
        + [jax.ShapeDtypeStruct((count, width + 128), BF) for _ in range(groups)],
        cost_estimate=cost(2 * count * chans * (block + up.shape[1]), 11 * count * chans, count * chans),
        name="mix_tokens",
    )(*pieces, tokens, scale, gain, gain_two, back, up)


def hidden_kernel(groups, total, *refs):
    pieces = refs[:groups]
    up, down = refs[groups : groups + 2]
    outs = refs[groups + 2 :]
    width = up.shape[0] // groups
    sums = sum(jnp.sum(p[:, width:].astype(F32), axis=1, keepdims=True) for p in pieces)
    scale = lax.rsqrt(sums / total + EPS)
    x = jnp.concatenate([p[:, :width] for p in pieces], axis=1)
    v = dot(x, up[...]) * scale
    active = (0.5 * v * (1.0 + jnp.tanh(0.7978845608 * (v + 0.044715 * (v * v * v))))).astype(BF)
    reduced = dot(active, down[...]).astype(BF)
    step = reduced.shape[1] // groups
    for d in range(groups):
        outs[d][...] = reduced[:, d * step : (d + 1) * step]


def hidden(pieces, up, down, total):
    groups = len(pieces)
    count, wide = pieces[0].shape
    step = down.shape[1] // groups
    tb = min(ROWS, count)
    return pl.pallas_call(
        lambda *refs: hidden_kernel(groups, total, *refs),
        grid=(count // tb,),
        in_specs=[pl.BlockSpec((tb, wide), lambda t: (t, 0)) for _ in range(groups)]
        + [whole(up.shape), whole(down.shape)],
        out_specs=[pl.BlockSpec((tb, step), lambda t: (t, 0)) for _ in range(groups)],
        out_shape=[jax.ShapeDtypeStruct((count, step), BF) for _ in range(groups)],
        cost_estimate=cost(
            2 * count * up.shape[1] * (up.shape[0] + down.shape[1]),
            2 * groups * count * (wide + step),
            count * up.shape[1],
        ),
        name="hidden_units",
    )(*pieces, up, down)


def final_kernel(groups, *refs):
    pieces = refs[:groups]
    mixed, left = refs[groups : groups + 2]
    out = refs[-1]
    x = jnp.concatenate([p[...] for p in pieces], axis=1)
    out[...] = (mixed[...] + dot(x, left[...])).astype(BF)


def final(pieces, mixed, left, row, count_all, carried):
    groups = len(pieces)
    count, step = pieces[0].shape
    chans = mixed.shape[1]
    tb = min(ROWS, count)
    first = row // tb
    extra = [] if carried is None else [carried]
    return pl.pallas_call(
        lambda *refs: final_kernel(groups, *refs),
        grid=(count // tb,),
        in_specs=[pl.BlockSpec((tb, step), lambda t: (t, 0)) for _ in range(groups)]
        + [pl.BlockSpec((tb, chans), lambda t: (t, 0)), whole(left.shape)]
        + [pl.BlockSpec(memory_space=pl.ANY) for _ in extra],
        out_specs=pl.BlockSpec((tb, chans), lambda t: (t + first, 0)),
        out_shape=jax.ShapeDtypeStruct((count_all, chans), BF),
        input_output_aliases={groups + 2: 0} if extra else {},
        cost_estimate=cost(2 * count * groups * step * chans, 8 * count * chans),
        name="block_out",
    )(*pieces, mixed, left, *extra)


def iota(shape, axis):
    return lax.broadcasted_iota(jnp.int32, shape, axis)


def pick(rows, cols, of_col):
    return (iota((rows, cols), 0) == of_col(iota((rows, cols), 1))).astype(BF)


def masked(x, keep):
    rows, cols = iota(x.shape, 0), iota(x.shape, 1)
    return jnp.where(keep(rows, cols), x, 0.0).astype(BF)


def spread_pairs(x):
    rows, cols = x.shape
    wide = dot(x, pick(cols, cols * G, lambda c: c // G))
    tall = jnp.broadcast_to(wide[:, None, :], (rows, G, cols * G)).reshape(rows * G, cols * G)
    return masked(tall, lambda r, c: r % G == c % G)


def expand_factors(right_up, left_up, right_down, left_down, me, groups):
    il, nj, nk = right_up.shape
    kl, ni, nm = left_up.shape
    nq = right_down.shape[2]
    ql, _, nr = left_down.shape
    lk, lr = kl * il, ql * kl
    up_one = masked(
        dot(
            right_up.reshape(il * nj, nk),
            pick(nk, groups * lk, lambda c: (me ^ (c // lk)) * kl + c % lk // il),
        ),
        lambda r, c: r // nj == c % il,
    )
    rows = groups * lk

    def source(r):
        return (r % lk // il) * ni + (me ^ (r // lk)) * il + r % il

    pick_rows = (source(iota((rows, kl * ni), 0)) == iota((rows, kl * ni), 1)).astype(BF)
    taken = dot(pick_rows, left_up.reshape(kl * ni, nm))
    tiled = jnp.broadcast_to(taken[:, None, :], (rows, kl, nm)).reshape(rows, kl * nm)
    up_two = masked(tiled, lambda r, c: c // nm == r % lk // il)
    down_one = masked(
        dot(
            right_down.reshape(kl * nm, nq),
            pick(nq, groups * lr, lambda c: (me ^ (c // lr)) * ql + c % lr // kl),
        ),
        lambda r, c: r // nm == c % kl,
    )
    rows = groups * lr
    nkk = left_down.shape[1]

    def source_two(r):
        return (r % lr // kl) * nkk + (me ^ (r // lr)) * kl + r % kl

    pick_rows = (source_two(iota((rows, ql * nkk), 0)) == iota((rows, ql * nkk), 1)).astype(BF)
    taken = dot(pick_rows, left_down.reshape(ql * nkk, nr)).astype(BF)
    down_two = masked(
        dot(taken, pick(nr, ql * nr, lambda c: c % nr)),
        lambda r, c: c // nr == r % lr // kl,
    )
    return up_one, up_two, down_one, down_two


def splits_of(total, shares):
    unit = total // sum(shares)
    if unit * sum(shares) != total:
        return [total]
    return [unit * share for share in shares]


def make_shards(parts, groups):
    def shards(
        tokens,
        seq_inner,
        seq_outer,
        inv_outer,
        inv_inner,
        twiddle_in,
        twiddle_out,
        freq_kernel,
        first_gain,
        second_gain,
        right_up,
        left_up,
        right_down,
        left_down,
    ):
        _, count, chans = tokens.shape
        total = chans * groups
        block = seq_inner.shape[0]
        ql = block // parts
        al = count // block
        at = lax.axis_index("ctx")
        me = lax.axis_index("hid")
        tok = tokens.reshape(count, chans)

        sent = freq_kernel.reshape(al, parts, ql, chans).transpose(1, 0, 2, 3)
        kern = lax.all_to_all(sent, "ctx", split_axis=0, concat_axis=0, tiled=True)

        wide = tok.astype(F32)
        sums = lax.psum(jnp.sum(wide * wide, axis=1), "hid")
        scale = lax.rsqrt(sums / total + EPS).reshape(count, 1)
        gain = first_gain.reshape(1, chans)
        gain_two = second_gain.reshape(1, chans)

        chan_splits = splits_of(chans, CHANNEL_SPLIT)
        mixes = inner(
            tok,
            scale,
            gain,
            xor_blocks(seq_inner, 0, at, parts),
            xor_blocks(twiddle_in, 1, at, parts).reshape(al, block, 1),
            parts,
            chan_splits,
        )

        fwd = spread_pairs(xor_blocks(seq_outer, 1, at, parts))
        back = spread_pairs(xor_blocks(inv_outer, 0, at, parts))
        side = fwd.shape[0]
        turn = xor_blocks(twiddle_out, 0, at, parts)
        turn = turn.reshape(side // G, ql // G, G).transpose(1, 0, 2).reshape(ql // G, side, 1)
        sizes = splits_of(al, RETURN_SPLIT)

        backed = None
        start = 0
        for f, width in enumerate(chan_splits):
            pieces = exchange(mixes[f * parts : (f + 1) * parts], "ctx", parts)
            backed = outer(pieces, kern, fwd, back, turn, sizes, start, backed)
            start += width

        up_one, up_two, down_one, down_two = expand_factors(
            right_up, left_up, right_down, left_down, me, groups
        )
        last = xor_blocks(inv_inner, 1, at, parts)
        out = None
        row = 0
        for j, size in enumerate(sizes):
            home = exchange(backed[j * parts : (j + 1) * parts], "ctx", parts)
            mixed, *pieces = mix(home, tok, scale, gain, gain_two, last, up_one, row, groups)
            pieces = exchange(pieces, "hid", groups)
            pieces = hidden(pieces, up_two, down_one, total)
            pieces = exchange(pieces, "hid", groups)
            out = final(pieces, mixed, down_two, row * block, count, out)
            row += size
        return out.reshape(1, count, chans)

    return shards


def solution(mesh):
    return jax.shard_map(
        make_shards(mesh.shape["ctx"], mesh.shape["hid"]),
        mesh=mesh,
        in_specs=(
            P(None, "ctx", "hid"),
            P(),
            P(),
            P(),
            P(),
            P("ctx", None),
            P(None, "ctx"),
            P("ctx", None, "hid"),
            P("hid"),
            P("hid"),
            P("hid", None, None),
            P("hid", None, None),
            P("hid", None, None),
            P("hid", None, None),
        ),
        out_specs=P(None, "ctx", "hid"),
        check_vma=False,
    )
```

time: 1360 us -> 851 us (0.63)
  blocking collectives: 984 us -> 16.2 us
  waiting for transfers between devices: 0 us -> 379 us
  Pallas kernels: 0 us -> 237 us
  local copies, waits for them, and re-layouts: 193 us -> 25.6 us
  starting transfers between devices: 0 us -> 150 us
  matrix products: 107 us -> 17.2 us
  other arithmetic: 73.4 us -> 17 us
    all_to_all x6 -> x0, blocking collectives: 953 us -> none  [the longest x1 190 us: shards(): lax.all_to_all(backed, 'ctx', split_axis=1, concat_axis=2, tiled=True)]
    ppermute x0 -> x79, waiting for transfers between devices: none -> 379 us  [swap(): return lax.ppermute(x, name, [(i, i ^ d) for i in range(size)])]
    pallas_call x0 -> x18, Pallas kernels: none -> 237 us  [the longest x2 87.1 us: outer(): pl.pallas_call(lambda *refs: outer_kernel(parts, sizes, *refs), grid=(wid...]
    ppermute x0 -> x79, starting transfers between devices: none -> 143 us  [swap(): return lax.ppermute(x, name, [(i, i ^ d) for i in range(size)])]
    convert_element_type x8 -> x0, local copies, waits for them, and re-layouts: 90.2 us -> none  [the longest x1 12.4 us: shards(): inner_mix = (inner_mix * twiddle_in[None, :, :, None]).astype(jnp.bfloat16)]
    dot_general x7 -> x6, matrix products: 107 us -> 17.2 us  [dot(): return jnp.dot(a, b, preferred_element_type=F32)]
    all_to_all x7 -> x0, local copies, waits for them, and re-layouts: 64 us -> none  [the longest x2 19.8 us: shards(): lax.all_to_all(scaled, 'ctx', split_axis=2, concat_axis=1, tiled=True)]
    convert_element_type x5 -> x2, other arithmetic: 51.6 us -> 11.8 us  [masked(): return jnp.where(keep(rows, cols), x, 0.0).astype(BF)]
  transfers between devices with their start and end apart: 0 -> 80, of which waited for: 0 -> 22; matrix products, arithmetic and copies ran while one was open for 0% -> 5% of each run, Pallas kernels for 0% -> 24%
where the time goes in v1:
time: 851 us; the launch traced here: 843 us
  waiting for transfers between devices  379 us (45%)
  Pallas kernels  237 us (28%)
  starting transfers between devices  150 us (18%)
  local copies, waits for them, and re-layouts  25.6 us (3%)
  matrix products  17.2 us (2%)
  other arithmetic  17 us (2%)
  blocking collectives  16.2 us (2%)
    ppermute x79, waiting for transfers between devices, swap(): return lax.ppermute(x, name, [(i, i ^ d) for i in range(size)])  379 us
    ppermute x79, starting transfers between devices, swap(): return lax.ppermute(x, name, [(i, i ^ d) for i in range(size)])  143 us
    pallas_call x2, Pallas kernels, outer(): pl.pallas_call(lambda *refs: outer_kernel(parts, sizes, *refs), grid=(wid...  87.1 us
    pallas_call x5, Pallas kernels, hidden(): pl.pallas_call(lambda *refs: hidden_kernel(groups, total, *refs), grid=(c...  65.1 us
    pallas_call x5, Pallas kernels, mix(): pl.pallas_call(lambda *refs: mix_kernel(parts, groups, *refs), grid=(size...  39.1 us
    pallas_call x5, Pallas kernels, final(): pl.pallas_call(lambda *refs: final_kernel(groups, *refs), grid=(count //...  30.2 us
    dot_general x6, matrix products, dot(): return jnp.dot(a, b, preferred_element_type=F32)  17.2 us
  transfers between devices with their start and end apart: 80, of which 22 were waited for; matrix products, arithmetic and copies ran while one was open for 5% of the time, Pallas kernels for 24%

profile of v1, /device:TPU:0, one launch (start us, length us, event | category | flops | bytes accessed | tf_op | source)
XLA Modules:
  0.0 843.3 jit_solution(13729272699749952924)
XLA Ops:
  0.0 8.7 %copy.86 = bf16[16,8,32,1024]{3,2,0,1:T(8,128)(2,1)} copy(bf16[16,8,32,1024]{3,2,1,0:T(8,128)(2,1)} %bitcast.57) | data formatting | bytes 16777216 | tf_op jit(solution)/shard_map/reshape | solution.py:352
  8.7 6.5 all-to-all-start
  17.4 5.1 multiply_reduce_fusion
  22.6 16.2 %psum.7 = f32[4096]{0:T(1024)S(1)} all-reduce(f32[4096]{0:T(1024)S(1)} %multiply_reduce_fusion), channel_id=1, replica_groups=mesh['ctx'=8,'hid'=4] {'hid'}, use_global_device_ids=true, to_apply=%region_1.0 | all-reduce | flops 4096 | bytes 32768 | tf_op jit(solution)/shard_map/psum | solution.py:356
  41.6 15.1 %inner_mix.1 = (bf16[16,32,768]{2,1,0:T(8,128)(2,1)}, bf16[16,32,768]{2,1,0:T(8,128)(2,1)}, bf16[16,32,768]{2,1,0:T(8,128)(2,1)}, bf16[16,32,768]{2,1,0:T(8,128)...) custom-call(bf16[4096,1024]{1,0:T(8,128)(2,1)} %bitcast.49, ...), custom_call_target="tpu_custom_call" | custom-call | flops 2147483648 | bytes 16777216 | tf_op jit(solution)/shard_map/inner_mix/pallas_call | solution.py:66
  67.9 139.7 %collective-permute-done.1.refs_2_ = bf16[16,32,256]{2,1,0:T(8,128)(2,1)S(1)} collective-permute-done((bf16[16,32,256]{2,1,0:T(8,128)(2,1)}, bf16[16,32,256]{2,1,0:T(8,128)(2,1)S(1)}, u32[]{:S(2)}, u32[]{:S(2)}) %collective-permute-start.1) | collective-permute-done | bytes 262176 | tf_op jit(solution)/shard_map/ppermute | solution.py:41
  207.6 76.2 %collective-permute-done.10.refs_4_ = bf16[16,32,768]{2,1,0:T(8,128)(2,1)S(1)} collective-permute-done((bf16[16,32,768]{2,1,0:T(8,128)(2,1)}, bf16[16,32,768]{2,1,0:T(8,128)(2,1)S(1)}, u32[]{:S(2)}, u32[]{:S(2)}) %collective-permute-start.10) | collective-permute-done | bytes 786464 | tf_op jit(solution)/shard_map/ppermute | solution.py:41
  283.8 16.0 %collective-permute-done.11.refs_5_ = bf16[16,32,768]{2,1,0:T(8,128)(2,1)S(1)} collective-permute-done((bf16[16,32,768]{2,1,0:T(8,128)(2,1)}, bf16[16,32,768]{2,1,0:T(8,128)(2,1)S(1)}, u32[]{:S(2)}, u32[]{:S(2)}) %collective-permute-start.11) | collective-permute-done | bytes 786464 | tf_op jit(solution)/shard_map/ppermute | solution.py:41
  300.7 7.9 fusion
  308.8 8.2 collective-permute-start.2
  317.0 17.4 %collective-permute-start.3 = (bf16[16,32,256]{2,1,0:T(8,128)(2,1)}, bf16[16,32,256]{2,1,0:T(8,128)(2,1)S(1)}, u32[]{:S(2)}, u32[]{:S(2)}) collective-permute-start(bf16[16,32,256]{2,1,0:T(8,128)(2,1)} %get-tuple-element.150), channel_id=1, source_target_pairs={{0,16},{4,20},{8,24},{12,28},{16,0},{20,4},{24,8},{28,12},{1,17},{... | collective-permute-start | bytes 786440 | tf_op jit(solution)/shard_map/ppermute | solution.py:41
  337.6 61.4 %outer_mix.2 = (bf16[4,32,1024]{2,1,0:T(8,128)(2,1)}, bf16[4,32,1024]{2,1,0:T(8,128)(2,1)}, bf16[4,32,1024]{2,1,0:T(8,128)(2,1)}, bf16[4,32,1024]{2,1,0:T(8,128)...) custom-call(bf16[16,32,768]{2,1,0:T(8,128)(2,1)} %get-tuple-element., ...), custom_call_target="tpu_custom_call" | custom-call | flops 25769803776 | bytes 18874368 | tf_op jit(solution)/shard_map/outer_mix/pallas_call | solution.py:112
  400.1 25.7 %outer_mix.3 = (bf16[4,32,1024]{2,1,0:T(8,128)(2,1)}, bf16[4,32,1024]{2,1,0:T(8,128)(2,1)}, bf16[4,32,1024]{2,1,0:T(8,128)(2,1)}, bf16[4,32,1024]{2,1,0:T(8,128)...) custom-call(bf16[16,32,256]{2,1,0:T(8,128)(2,1)} %get-tuple-element., ...), custom_call_target="tpu_custom_call", output_to_operand_aliasing={{0}: (12, {}), {1}: (13, {}), {2}: (14, {}), {3}: (15, {}),... | custom-call | flops 8589934592 | bytes 6291456 | tf_op jit(solution)/shard_map/outer_mix/pallas_call | solution.py:112
  431.1 3.6 fusion.61
  439.6 9.6 %collective-permute-done.31.refs_5_ = bf16[2,32,1024]{2,1,0:T(8,128)(2,1)S(1)} collective-permute-done((bf16[2,32,1024]{2,1,0:T(8,128)(2,1)}, bf16[2,32,1024]{2,1,0:T(8,128)(2,1)S(1)}, u32[]{:S(2)}, u32[]{:S(2)}) %collective-permute-start.31) | collective-permute-done | bytes 131104 | tf_op jit(solution)/shard_map/ppermute | solution.py:41
  449.7 5.7 collective-permute-start.67
  459.2 3.9 fusion.7.refs_4_
  463.1 7.4 collective-permute-done.17.refs_4_
  473.5 4.5 collective-permute-done.19.refs_6_
  477.9 6.5 collective-permute-start.69
  491.4 6.2 select_convert_fusion.refs_5_
  497.6 16.8 %collective-permute-done.69.refs_4_ = bf16[4,32,1024]{2,1,0:T(8,128)(2,1)S(1)} collective-permute-done((bf16[4,32,1024]{2,1,0:T(8,128)(2,1)S(1)}, bf16[4,32,1024]{2,1,0:T(8,128)(2,1)S(1)}, u32[]{:S(2)}, u32[]{:S(2)}) %collective-permute-start.69) | collective-permute-done | bytes 262176 | tf_op jit(solution)/shard_map/ppermute | solution.py:41
  514.4 5.5 collective-permute-done.70.refs_5_
  520.0 6.6 collective-permute-start.56
  526.6 10.7 %collective-permute-start.57 = (bf16[4,32,1024]{2,1,0:T(8,128)(2,1)S(1)}, bf16[4,32,1024]{2,1,0:T(8,128)(2,1)S(1)}, u32[]{:S(2)}, u32[]{:S(2)}) collective-permute-start(bf16[4,32,1024]{2,1,0:T(8,128)(2,1)S(1)} %copy-done.42), channel_id=1, source_target_pairs={{0,20},{4,16},{8,28},{12,24},{16,4},{20,0},{24,12},{28,8},{1,21},{... | collective-permute-start | bytes 786440 | tf_op jit(solution)/shard_map/ppermute | solution.py:41
  545.4 6.0 mix_tokens.6
  553.8 11.1 %collective-permute-done.57.refs_5_ = bf16[4,32,1024]{2,1,0:T(8,128)(2,1)S(1)} collective-permute-done((bf16[4,32,1024]{2,1,0:T(8,128)(2,1)S(1)}, bf16[4,32,1024]{2,1,0:T(8,128)(2,1)S(1)}, u32[]{:S(2)}, u32[]{:S(2)}) %collective-permute-start.57) | collective-permute-done | bytes 262176 | tf_op jit(solution)/shard_map/ppermute | solution.py:41
  570.3 6.6 collective-permute-start.43
  580.3 5.9 mix_tokens.5
  586.3 9.0 %mix_tokens.9 = (f32[1024,1024]{1,0:T(8,128)}, bf16[1024,384]{1,0:T(8,128)(2,1)}, bf16[1024,384]{1,0:T(8,128)(2,1)}, bf16[1024,384]{1,0:T(8,128)(2,1)}, bf16[1024,384]{1,0:T(8,128)(2,1)}) custom-call(bf16[4,32,1024]{2,1,0:T(8,128)(2,1)} %get-tuple-element.270.refs_0_, bf16[4,32,1024]{2,1,0:T(8,128)(2,1)} %copy-done.13, bf16[4,32,1024]{2,1,0:T(8,128)(2,1)} %copy-done.14, ...), custom_call_target="tpu_custom_call" | custom-call | flops 2684354560 | bytes 11534336 | tf_op jit(solution)/shard_map/mix_tokens/pallas_call | solution.py:168
  595.3 11.1 %collective-permute-done.43.refs_4_ = bf16[4,32,1024]{2,1,0:T(8,128)(2,1)S(1)} collective-permute-done((bf16[4,32,1024]{2,1,0:T(8,128)(2,1)S(1)}, bf16[4,32,1024]{2,1,0:T(8,128)(2,1)S(1)}, u32[]{:S(2)}, u32[]{:S(2)}) %collective-permute-start.43) | collective-permute-done | bytes 262176 | tf_op jit(solution)/shard_map/ppermute | solution.py:41
  617.5 9.0 %mix_tokens.8 = (f32[1024,1024]{1,0:T(8,128)}, bf16[1024,384]{1,0:T(8,128)(2,1)}, bf16[1024,384]{1,0:T(8,128)(2,1)}, bf16[1024,384]{1,0:T(8,128)(2,1)}, bf16[1024,384]{1,0:T(8,128)(2,1)}) custom-call(bf16[4,32,1024]{2,1,0:T(8,128)(2,1)} %get-tuple-element.253.refs_0_, bf16[4,32,1024]{2,1,0:T(8,128)(2,1)} %copy-done.16, bf16[4,32,1024]{2,1,0:T(8,128)(2,1)} %copy-done.17, ...), custom_call_target="tpu_custom_call" | custom-call | flops 2684354560 | bytes 11534336 | tf_op jit(solution)/shard_map/mix_tokens/pallas_call | solution.py:168
  626.5 9.1 %mix_tokens.7 = (f32[1024,1024]{1,0:T(8,128)}, bf16[1024,384]{1,0:T(8,128)(2,1)}, bf16[1024,384]{1,0:T(8,128)(2,1)}, bf16[1024,384]{1,0:T(8,128)(2,1)}, bf16[1024,384]{1,0:T(8,128)(2,1)}) custom-call(bf16[4,32,1024]{2,1,0:T(8,128)(2,1)} %get-tuple-element.236.refs_0_, bf16[4,32,1024]{2,1,0:T(8,128)(2,1)} %copy-done.27, bf16[4,32,1024]{2,1,0:T(8,128)(2,1)} %copy-done.30, ...), custom_call_target="tpu_custom_call" | custom-call | flops 2684354560 | bytes 11534336 | tf_op jit(solution)/shard_map/mix_tokens/pallas_call | solution.py:168
  637.0 9.9 %hidden_units.6 = (bf16[512,256]{1,0:T(8,128)(2,1)}, bf16[512,256]{1,0:T(8,128)(2,1)}, bf16[512,256]{1,0:T(8,128)(2,1)}, bf16[512,256]{1,0:T(8,128)(2,1)}) custom-call(bf16[512,384]{1,0:T(8,128)(2,1)} %get-tuple-element.227.refs_0_, bf16[512,384]{1,0:T(8,128)(2,1)} %collective-permute-done.34.refs_1_, bf16[512,384]{1,0:T(8,128)(2,1)} %copy-done.111, ...), custom_call_target="tpu_custom_call" | custom-call | flops 4294967296 | bytes 2621440 | tf_op jit(solution)/shard_map/hidden_units/pallas_call | solution.py:210
  648.4 12.3 %collective-permute-done.74.refs_2_ = bf16[1024,384]{1,0:T(8,128)(2,1)} collective-permute-done((bf16[1024,384]{1,0:T(8,128)(2,1)}, bf16[1024,384]{1,0:T(8,128)(2,1)}, u32[]{:S(2)}, u32[]{:S(2)}) %collective-permute-start.74) | collective-permute-done | bytes 786464 | tf_op jit(solution)/shard_map/ppermute | solution.py:41
  663.7 15.1 %hidden_units.9 = (bf16[1024,256]{1,0:T(8,128)(2,1)}, bf16[1024,256]{1,0:T(8,128)(2,1)}, bf16[1024,256]{1,0:T(8,128)(2,1)}, bf16[1024,256]{1,0:T(8,128)(2,1)}) custom-call(bf16[1024,384]{1,0:T(8,128)(2,1)} %get-tuple-element.278.refs_0_, bf16[1024,384]{1,0:T(8,128)(2,1)} %collective-permute-done.73.refs_1_, ...), custom_call_target="tpu_custom_call" | custom-call | flops 8589934592 | bytes 5242880 | tf_op jit(solution)/shard_map/hidden_units/pallas_call | solution.py:210
  685.1 24.8 %collective-permute-done.61.refs_2_ = bf16[1024,384]{1,0:T(8,128)(2,1)} collective-permute-done((bf16[1024,384]{1,0:T(8,128)(2,1)}, bf16[1024,384]{1,0:T(8,128)(2,1)}, u32[]{:S(2)}, u32[]{:S(2)}) %collective-permute-start.61) | collective-permute-done | bytes 786464 | tf_op jit(solution)/shard_map/ppermute | solution.py:41
  714.1 15.1 %hidden_units.8 = (bf16[1024,256]{1,0:T(8,128)(2,1)}, bf16[1024,256]{1,0:T(8,128)(2,1)}, bf16[1024,256]{1,0:T(8,128)(2,1)}, bf16[1024,256]{1,0:T(8,128)(2,1)}) custom-call(bf16[1024,384]{1,0:T(8,128)(2,1)} %get-tuple-element.261.refs_0_, bf16[1024,384]{1,0:T(8,128)(2,1)} %collective-permute-done.60.refs_1_, ...), custom_call_target="tpu_custom_call" | custom-call | flops 8589934592 | bytes 5242880 | tf_op jit(solution)/shard_map/hidden_units/pallas_call | solution.py:210
  732.8 14.0 %collective-permute-done.48.refs_2_ = bf16[1024,384]{1,0:T(8,128)(2,1)} collective-permute-done((bf16[1024,384]{1,0:T(8,128)(2,1)S(1)}, bf16[1024,384]{1,0:T(8,128)(2,1)}, u32[]{:S(2)}, u32[]{:S(2)}) %collective-permute-start.48) | collective-permute-done | bytes 786464 | tf_op jit(solution)/shard_map/ppermute | solution.py:41
  749.8 15.0 %hidden_units.7 = (bf16[1024,256]{1,0:T(8,128)(2,1)}, bf16[1024,256]{1,0:T(8,128)(2,1)}, bf16[1024,256]{1,0:T(8,128)(2,1)}, bf16[1024,256]{1,0:T(8,128)(2,1)}) custom-call(bf16[1024,384]{1,0:T(8,128)(2,1)} %get-tuple-element.244.refs_0_, bf16[1024,384]{1,0:T(8,128)(2,1)} %collective-permute-done.47.refs_1_, ...), custom_call_target="tpu_custom_call" | custom-call | flops 8589934592 | bytes 5242880 | tf_op jit(solution)/shard_map/hidden_units/pallas_call | solution.py:210
  772.2 9.8 %collective-permute-done.63.refs_1_ = bf16[1024,256]{1,0:T(8,128)(2,1)S(1)} collective-permute-done((bf16[1024,256]{1,0:T(8,128)(2,1)}, bf16[1024,256]{1,0:T(8,128)(2,1)S(1)}, u32[]{:S(2)}, u32[]{:S(2)}) %collective-permute-start.63) | collective-permute-done | bytes 524320 | tf_op jit(solution)/shard_map/ppermute | solution.py:41
  783.4 10.0 %hidden_units.5 = (bf16[512,256]{1,0:T(8,128)(2,1)}, bf16[512,256]{1,0:T(8,128)(2,1)}, bf16[512,256]{1,0:T(8,128)(2,1)}, bf16[512,256]{1,0:T(8,128)(2,1)}) custom-call(bf16[512,384]{1,0:T(8,128)(2,1)} %get-tuple-element.210.refs_0_, bf16[512,384]{1,0:T(8,128)(2,1)} %collective-permute-done.21.refs_1_, bf16[512,384]{1,0:T(8,128)(2,1)} %collective-permute-done.22.refs_2_, ...), custom_call_target="tpu_custom_call" | custom-call | flops 4294967296 | bytes 2621440 | tf_op jit(solution)/shard_map/hidden_units/pallas_call | solution.py:210
  793.5 7.1 block_out.5.refs_6_
  802.7 7.0 block_out.6.refs_6_
  818.3 7.0 block_out.7.refs_6_
  827.7 4.5 block_out.8.refs_6_
  832.2 5.3 collective-permute-done.25.refs_2_
  838.3 4.6 block_out.9
  (420 shorter events, 120.9 us)
Async XLA Ops:
  8.7 328.9 %all-to-all-start = ((bf16[8,16,32,1024]{3,2,1,0:T(8,128)(2,1)}), bf16[8,16,32,1024]{3,2,1,0:T(8,128)(2,1)}, u32[]{:S(2)}, u32[]{:S(2)}) async-start(bf16[8,16,32,1024]{3,2,1,0:T(8,128)(2,1)} %bitcast.55), calls=%async_computation | async-start | bytes 16777216 | tf_op jit(solution)/shard_map/all_to_all | solution.py:353
  56.7 227.0 %collective-permute-start.10 = (bf16[16,32,768]{2,1,0:T(8,128)(2,1)}, bf16[16,32,768]{2,1,0:T(8,128)(2,1)S(1)}, u32[]{:S(2)}, u32[]{:S(2)}) collective-permute-start(bf16[16,32,768]{2,1,0:T(8,128)(2,1)} %get-tuple-element.158), channel_id=1, source_target_pairs={{0,16},{4,20},{8,24},{12,28},{16,0},{20,4},{24,8},{28,12},{1,17},{... | collective-permute-start | bytes 2359304 | tf_op jit(solution)/shard_map/ppermute | solution.py:41
  59.5 240.2 %collective-permute-start.11 = (bf16[16,32,768]{2,1,0:T(8,128)(2,1)}, bf16[16,32,768]{2,1,0:T(8,128)(2,1)S(1)}, u32[]{:S(2)}, u32[]{:S(2)}) collective-permute-start(bf16[16,32,768]{2,1,0:T(8,128)(2,1)} %get-tuple-element.159), channel_id=1, source_target_pairs={{0,20},{4,16},{8,28},{12,24},{16,4},{20,0},{24,12},{28,8},{1,21},{... | collective-permute-start | bytes 2359304 | tf_op jit(solution)/shard_map/ppermute | solution.py:41
  59.5 249.2 %collective-permute-start.12 = (bf16[16,32,768]{2,1,0:T(8,128)(2,1)}, bf16[16,32,768]{2,1,0:T(8,128)(2,1)}, u32[]{:S(2)}, u32[]{:S(2)}) collective-permute-start(bf16[16,32,768]{2,1,0:T(8,128)(2,1)} %get-tuple-element.160), channel_id=1, source_target_pairs={{0,24},{4,28},{8,16},{12,20},{16,8},{20,12},{24,0},{28,4},{1,25},{... | collective-permute-start | bytes 2359304 | tf_op jit(solution)/shard_map/ppermute | solution.py:41
  63.2 144.4 %collective-permute-start.1 = (bf16[16,32,256]{2,1,0:T(8,128)(2,1)}, bf16[16,32,256]{2,1,0:T(8,128)(2,1)S(1)}, u32[]{:S(2)}, u32[]{:S(2)}) collective-permute-start(bf16[16,32,256]{2,1,0:T(8,128)(2,1)} %get-tuple-element.148), channel_id=1, source_target_pairs={{0,8},{4,12},{8,0},{12,4},{16,24},{20,28},{24,16},{28,20},{1,9},{5... | collective-permute-start | bytes 786440 | tf_op jit(solution)/shard_map/ppermute | solution.py:41
  67.2 249.7 %collective-permute-start.13 = (bf16[16,32,768]{2,1,0:T(8,128)(2,1)}, bf16[16,32,768]{2,1,0:T(8,128)(2,1)}, u32[]{:S(2)}, u32[]{:S(2)}) collective-permute-start(bf16[16,32,768]{2,1,0:T(8,128)(2,1)} %get-tuple-element.161), channel_id=1, source_target_pairs={{0,28},{4,24},{8,20},{12,16},{16,12},{20,8},{24,4},{28,0},{1,29},{... | collective-permute-start | bytes 2359304 | tf_op jit(solution)/shard_map/ppermute | solution.py:41
  207.6 126.7 %collective-permute-start.7 = (bf16[16,32,768]{2,1,0:T(8,128)(2,1)}, bf16[16,32,768]{2,1,0:T(8,128)(2,1)}, u32[]{:S(2)}, u32[]{:S(2)}) collective-permute-start(bf16[16,32,768]{2,1,0:T(8,128)(2,1)} %get-tuple-element.155), channel_id=1, source_target_pairs={{0,4},{4,0},{8,12},{12,8},{16,20},{20,16},{24,28},{28,24},{1,5},{5... | collective-permute-start | bytes 2359304 | tf_op jit(solution)/shard_map/ppermute | solution.py:41
  283.8 50.6 %collective-permute-start.8 = (bf16[16,32,768]{2,1,0:T(8,128)(2,1)}, bf16[16,32,768]{2,1,0:T(8,128)(2,1)}, u32[]{:S(2)}, u32[]{:S(2)}) collective-permute-start(bf16[16,32,768]{2,1,0:T(8,128)(2,1)} %get-tuple-element.156), channel_id=1, source_target_pairs={{0,8},{4,12},{8,0},{12,4},{16,24},{20,28},{24,16},{28,20},{1,9},{5... | collective-permute-start | bytes 2359304 | tf_op jit(solution)/shard_map/ppermute | solution.py:41
  299.8 36.8 %collective-permute-start.9 = (bf16[16,32,768]{2,1,0:T(8,128)(2,1)}, bf16[16,32,768]{2,1,0:T(8,128)(2,1)}, u32[]{:S(2)}, u32[]{:S(2)}) collective-permute-start(bf16[16,32,768]{2,1,0:T(8,128)(2,1)} %get-tuple-element.157), channel_id=1, source_target_pairs={{0,12},{4,8},{8,4},{12,0},{16,28},{20,24},{24,20},{28,16},{1,13},{... | collective-permute-start | bytes 2359304 | tf_op jit(solution)/shard_map/ppermute | solution.py:41
  308.8 90.3 %collective-permute-start.2 = (bf16[16,32,256]{2,1,0:T(8,128)(2,1)}, bf16[16,32,256]{2,1,0:T(8,128)(2,1)S(1)}, u32[]{:S(2)}, u32[]{:S(2)}) collective-permute-start(bf16[16,32,256]{2,1,0:T(8,128)(2,1)} %get-tuple-element.149), channel_id=1, source_target_pairs={{0,12},{4,8},{8,4},{12,0},{16,28},{20,24},{24,20},{28,16},{1,13},{... | collective-permute-start | bytes 786440 | tf_op jit(solution)/shard_map/ppermute | solution.py:41
  317.0 82.1 %collective-permute-start.3 = (bf16[16,32,256]{2,1,0:T(8,128)(2,1)}, bf16[16,32,256]{2,1,0:T(8,128)(2,1)S(1)}, u32[]{:S(2)}, u32[]{:S(2)}) collective-permute-start(bf16[16,32,256]{2,1,0:T(8,128)(2,1)} %get-tuple-element.150), channel_id=1, source_target_pairs={{0,16},{4,20},{8,24},{12,28},{16,0},{20,4},{24,8},{28,12},{1,17},{... | collective-permute-start | bytes 786440 | tf_op jit(solution)/shard_map/ppermute | solution.py:41
  334.3 64.7 %collective-permute-start.4 = (bf16[16,32,256]{2,1,0:T(8,128)(2,1)}, bf16[16,32,256]{2,1,0:T(8,128)(2,1)S(1)}, u32[]{:S(2)}, u32[]{:S(2)}) collective-permute-start(bf16[16,32,256]{2,1,0:T(8,128)(2,1)} %get-tuple-element.151), channel_id=1, source_target_pairs={{0,20},{4,16},{8,28},{12,24},{16,4},{20,0},{24,12},{28,8},{1,21},{... | collective-permute-start | bytes 786440 | tf_op jit(solution)/shard_map/ppermute | solution.py:41
  334.3 64.8 %collective-permute-start.5 = (bf16[16,32,256]{2,1,0:T(8,128)(2,1)}, bf16[16,32,256]{2,1,0:T(8,128)(2,1)S(1)}, u32[]{:S(2)}, u32[]{:S(2)}) collective-permute-start(bf16[16,32,256]{2,1,0:T(8,128)(2,1)} %get-tuple-element.152), channel_id=1, source_target_pairs={{0,24},{4,28},{8,16},{12,20},{16,8},{20,12},{24,0},{28,4},{1,25},{... | collective-permute-start | bytes 786440 | tf_op jit(solution)/shard_map/ppermute | solution.py:41
  336.5 62.6 %collective-permute-start.6 = (bf16[16,32,256]{2,1,0:T(8,128)(2,1)}, bf16[16,32,256]{2,1,0:T(8,128)(2,1)S(1)}, u32[]{:S(2)}, u32[]{:S(2)}) collective-permute-start(bf16[16,32,256]{2,1,0:T(8,128)(2,1)} %get-tuple-element.153), channel_id=1, source_target_pairs={{0,28},{4,24},{8,20},{12,16},{16,12},{20,8},{24,4},{28,0},{1,29},{... | collective-permute-start | bytes 786440 | tf_op jit(solution)/shard_map/ppermute | solution.py:41
  449.4 38.0 %collective-permute-start.66 = (bf16[4,32,1024]{2,1,0:T(8,128)(2,1)S(1)}, bf16[4,32,1024]{2,1,0:T(8,128)(2,1)S(1)}, u32[]{:S(2)}, u32[]{:S(2)}) collective-permute-start(bf16[4,32,1024]{2,1,0:T(8,128)(2,1)S(1)} %copy-done.36), channel_id=1, source_target_pairs={{0,4},{4,0},{8,12},{12,8},{16,20},{20,16},{24,28},{28,24},{1,5},{5... | collective-permute-start | bytes 786440 | tf_op jit(solution)/shard_map/ppermute | solution.py:41
  449.7 39.8 %collective-permute-start.67 = (bf16[4,32,1024]{2,1,0:T(8,128)(2,1)S(1)}, bf16[4,32,1024]{2,1,0:T(8,128)(2,1)S(1)}, u32[]{:S(2)}, u32[]{:S(2)}) collective-permute-start(bf16[4,32,1024]{2,1,0:T(8,128)(2,1)S(1)} %copy-done.37), channel_id=1, source_target_pairs={{0,8},{4,12},{8,0},{12,4},{16,24},{20,28},{24,16},{28,20},{1,9},{5... | collective-permute-start | bytes 786440 | tf_op jit(solution)/shard_map/ppermute | solution.py:41
  455.4 35.6 %collective-permute-start.68 = (bf16[4,32,1024]{2,1,0:T(8,128)(2,1)S(1)}, bf16[4,32,1024]{2,1,0:T(8,128)(2,1)S(1)}, u32[]{:S(2)}, u32[]{:S(2)}) collective-permute-start(bf16[4,32,1024]{2,1,0:T(8,128)(2,1)S(1)} %copy-done.38), channel_id=1, source_target_pairs={{0,12},{4,8},{8,4},{12,0},{16,28},{20,24},{24,20},{28,16},{1,13},{... | collective-permute-start | bytes 786440 | tf_op jit(solution)/shard_map/ppermute | solution.py:41
  477.9 36.5 %collective-permute-start.69 = (bf16[4,32,1024]{2,1,0:T(8,128)(2,1)S(1)}, bf16[4,32,1024]{2,1,0:T(8,128)(2,1)S(1)}, u32[]{:S(2)}, u32[]{:S(2)}) collective-permute-start(bf16[4,32,1024]{2,1,0:T(8,128)(2,1)S(1)} %copy-done.39), channel_id=1, source_target_pairs={{0,16},{4,20},{8,24},{12,28},{16,0},{20,4},{24,8},{28,12},{1,17},{... | collective-permute-start | bytes 786440 | tf_op jit(solution)/shard_map/ppermute | solution.py:41
  485.1 34.8 %collective-permute-start.70 = (bf16[4,32,1024]{2,1,0:T(8,128)(2,1)S(1)}, bf16[4,32,1024]{2,1,0:T(8,128)(2,1)S(1)}, u32[]{:S(2)}, u32[]{:S(2)}) collective-permute-start(bf16[4,32,1024]{2,1,0:T(8,128)(2,1)S(1)} %copy-done.40), channel_id=1, source_target_pairs={{0,20},{4,16},{8,28},{12,24},{16,4},{20,0},{24,12},{28,8},{1,21},{... | collective-permute-start | bytes 786440 | tf_op jit(solution)/shard_map/ppermute | solution.py:41
  489.5 37.1 %collective-permute-start.72 = (bf16[4,32,1024]{2,1,0:T(8,128)(2,1)}, bf16[4,32,1024]{2,1,0:T(8,128)(2,1)S(1)}, u32[]{:S(2)}, u32[]{:S(2)}) collective-permute-start(bf16[4,32,1024]{2,1,0:T(8,128)(2,1)} %get-tuple-element.277), channel_id=1, source_target_pairs={{0,28},{4,24},{8,20},{12,16},{16,12},{20,8},{24,4},{28,0},{1,29},{... | collective-permute-start | bytes 786440 | tf_op jit(solution)/shard_map/ppermute | solution.py:41
  491.0 46.3 %collective-permute-start.53 = (bf16[4,32,1024]{2,1,0:T(8,128)(2,1)}, bf16[4,32,1024]{2,1,0:T(8,128)(2,1)S(1)}, u32[]{:S(2)}, u32[]{:S(2)}) collective-permute-start(bf16[4,32,1024]{2,1,0:T(8,128)(2,1)} %get-tuple-element.254), channel_id=1, source_target_pairs={{0,4},{4,0},{8,12},{12,8},{16,20},{20,16},{24,28},{28,24},{1,5},{5... | collective-permute-start | bytes 786440 | tf_op jit(solution)/shard_map/ppermute | solution.py:41
  514.4 37.0 %collective-permute-start.54 = (bf16[4,32,1024]{2,1,0:T(8,128)(2,1)}, bf16[4,32,1024]{2,1,0:T(8,128)(2,1)S(1)}, u32[]{:S(2)}, u32[]{:S(2)}) collective-permute-start(bf16[4,32,1024]{2,1,0:T(8,128)(2,1)} %get-tuple-element.255), channel_id=1, source_target_pairs={{0,8},{4,12},{8,0},{12,4},{16,24},{20,28},{24,16},{28,20},{1,9},{5... | collective-permute-start | bytes 786440 | tf_op jit(solution)/shard_map/ppermute | solution.py:41
  526.6 38.3 %collective-permute-start.57 = (bf16[4,32,1024]{2,1,0:T(8,128)(2,1)S(1)}, bf16[4,32,1024]{2,1,0:T(8,128)(2,1)S(1)}, u32[]{:S(2)}, u32[]{:S(2)}) collective-permute-start(bf16[4,32,1024]{2,1,0:T(8,128)(2,1)S(1)} %copy-done.42), channel_id=1, source_target_pairs={{0,20},{4,16},{8,28},{12,24},{16,4},{20,0},{24,12},{28,8},{1,21},{... | collective-permute-start | bytes 786440 | tf_op jit(solution)/shard_map/ppermute | solution.py:41
  565.0 50.1 %collective-permute-start.34 = (bf16[512,384]{1,0:T(8,128)(2,1)}, bf16[512,384]{1,0:T(8,128)(2,1)}, u32[]{:S(2)}, u32[]{:S(2)}) collective-permute-start(bf16[512,384]{1,0:T(8,128)(2,1)} %get-tuple-element.228), channel_id=1, source_target_pairs={{0,1},{1,0},{2,3},{3,2},{4,5},{5,4},{6,7},{7,6},{8,9},{9,8},{10,11... | collective-permute-start | bytes 1179656 | tf_op jit(solution)/shard_map/ppermute | solution.py:41
  570.3 36.2 %collective-permute-start.43 = (bf16[4,32,1024]{2,1,0:T(8,128)(2,1)S(1)}, bf16[4,32,1024]{2,1,0:T(8,128)(2,1)S(1)}, u32[]{:S(2)}, u32[]{:S(2)}) collective-permute-start(bf16[4,32,1024]{2,1,0:T(8,128)(2,1)S(1)} %copy-done.45), channel_id=1, source_target_pairs={{0,16},{4,20},{8,24},{12,28},{16,0},{20,4},{24,8},{28,12},{1,17},{... | collective-permute-start | bytes 786440 | tf_op jit(solution)/shard_map/ppermute | solution.py:41
  576.9 34.6 %collective-permute-start.44 = (bf16[4,32,1024]{2,1,0:T(8,128)(2,1)}, bf16[4,32,1024]{2,1,0:T(8,128)(2,1)S(1)}, u32[]{:S(2)}, u32[]{:S(2)}) collective-permute-start(bf16[4,32,1024]{2,1,0:T(8,128)(2,1)} %get-tuple-element.241), channel_id=1, source_target_pairs={{0,20},{4,16},{8,28},{12,24},{16,4},{20,0},{24,12},{28,8},{1,21},{... | collective-permute-start | bytes 786440 | tf_op jit(solution)/shard_map/ppermute | solution.py:41
  577.0 37.0 %collective-permute-start.45 = (bf16[4,32,1024]{2,1,0:T(8,128)(2,1)}, bf16[4,32,1024]{2,1,0:T(8,128)(2,1)S(1)}, u32[]{:S(2)}, u32[]{:S(2)}) collective-permute-start(bf16[4,32,1024]{2,1,0:T(8,128)(2,1)} %get-tuple-element.242), channel_id=1, source_target_pairs={{0,24},{4,28},{8,16},{12,20},{16,8},{20,12},{24,0},{28,4},{1,25},{... | collective-permute-start | bytes 786440 | tf_op jit(solution)/shard_map/ppermute | solution.py:41
  579.1 35.4 %collective-permute-start.46 = (bf16[4,32,1024]{2,1,0:T(8,128)(2,1)}, bf16[4,32,1024]{2,1,0:T(8,128)(2,1)S(1)}, u32[]{:S(2)}, u32[]{:S(2)}) collective-permute-start(bf16[4,32,1024]{2,1,0:T(8,128)(2,1)} %get-tuple-element.243), channel_id=1, source_target_pairs={{0,28},{4,24},{8,20},{12,16},{16,12},{20,8},{24,4},{28,0},{1,29},{... | collective-permute-start | bytes 786440 | tf_op jit(solution)/shard_map/ppermute | solution.py:41
  614.6 46.2 %collective-permute-start.74 = (bf16[1024,384]{1,0:T(8,128)(2,1)}, bf16[1024,384]{1,0:T(8,128)(2,1)}, u32[]{:S(2)}, u32[]{:S(2)}) collective-permute-start(bf16[1024,384]{1,0:T(8,128)(2,1)} %get-tuple-element.280), channel_id=1, source_target_pairs={{0,2},{1,3},{2,0},{3,1},{4,6},{5,7},{6,4},{7,5},{8,10},{9,11},{10,... | collective-permute-start | bytes 2359304 | tf_op jit(solution)/shard_map/ppermute | solution.py:41
  615.1 47.2 %collective-permute-start.75 = (bf16[1024,384]{1,0:T(8,128)(2,1)}, bf16[1024,384]{1,0:T(8,128)(2,1)}, u32[]{:S(2)}, u32[]{:S(2)}) collective-permute-start(bf16[1024,384]{1,0:T(8,128)(2,1)} %get-tuple-element.281), channel_id=1, source_target_pairs={{0,3},{1,2},{2,1},{3,0},{4,7},{5,6},{6,5},{7,4},{8,11},{9,10},{10,... | collective-permute-start | bytes 2359304 | tf_op jit(solution)/shard_map/ppermute | solution.py:41
  635.6 43.2 %collective-permute-start.21 = (bf16[512,384]{1,0:T(8,128)(2,1)}, bf16[512,384]{1,0:T(8,128)(2,1)}, u32[]{:S(2)}, u32[]{:S(2)}) collective-permute-start(bf16[512,384]{1,0:T(8,128)(2,1)} %get-tuple-element.211), channel_id=1, source_target_pairs={{0,1},{1,0},{2,3},{3,2},{4,5},{5,4},{6,7},{7,6},{8,9},{9,8},{10,11... | collective-permute-start | bytes 1179656 | tf_op jit(solution)/shard_map/ppermute | solution.py:41
  636.3 92.9 %collective-permute-start.22 = (bf16[512,384]{1,0:T(8,128)(2,1)}, bf16[512,384]{1,0:T(8,128)(2,1)}, u32[]{:S(2)}, u32[]{:S(2)}) collective-permute-start(bf16[512,384]{1,0:T(8,128)(2,1)} %get-tuple-element.212), channel_id=1, source_target_pairs={{0,2},{1,3},{2,0},{3,1},{4,6},{5,7},{6,4},{7,5},{8,10},{9,11},{10,... | collective-permute-start | bytes 1179656 | tf_op jit(solution)/shard_map/ppermute | solution.py:41
  646.9 36.7 %collective-permute-start.60 = (bf16[1024,384]{1,0:T(8,128)(2,1)}, bf16[1024,384]{1,0:T(8,128)(2,1)}, u32[]{:S(2)}, u32[]{:S(2)}) collective-permute-start(bf16[1024,384]{1,0:T(8,128)(2,1)} %get-tuple-element.262), channel_id=1, source_target_pairs={{0,1},{1,0},{2,3},{3,2},{4,5},{5,4},{6,7},{7,6},{8,9},{9,8},{10,11... | collective-permute-start | bytes 2359304 | tf_op jit(solution)/shard_map/ppermute | solution.py:41
  660.7 49.1 %collective-permute-start.61 = (bf16[1024,384]{1,0:T(8,128)(2,1)}, bf16[1024,384]{1,0:T(8,128)(2,1)}, u32[]{:S(2)}, u32[]{:S(2)}) collective-permute-start(bf16[1024,384]{1,0:T(8,128)(2,1)} %get-tuple-element.263), channel_id=1, source_target_pairs={{0,2},{1,3},{2,0},{3,1},{4,6},{5,7},{6,4},{7,5},{8,10},{9,11},{10,... | collective-permute-start | bytes 2359304 | tf_op jit(solution)/shard_map/ppermute | solution.py:41
  662.3 49.1 %collective-permute-start.62 = (bf16[1024,384]{1,0:T(8,128)(2,1)S(1)}, bf16[1024,384]{1,0:T(8,128)(2,1)}, u32[]{:S(2)}, u32[]{:S(2)}) collective-permute-start(bf16[1024,384]{1,0:T(8,128)(2,1)S(1)} %copy-done.106), channel_id=1, source_target_pairs={{0,3},{1,2},{2,1},{3,0},{4,7},{5,6},{6,5},{7,4},{8,11},{9,10},{10,... | collective-permute-start | bytes 2359304 | tf_op jit(solution)/shard_map/ppermute | solution.py:41
  678.8 50.5 %collective-permute-start.23 = (bf16[512,384]{1,0:T(8,128)(2,1)S(1)}, bf16[512,384]{1,0:T(8,128)(2,1)}, u32[]{:S(2)}, u32[]{:S(2)}) collective-permute-start(bf16[512,384]{1,0:T(8,128)(2,1)S(1)} %copy-done.109), channel_id=1, source_target_pairs={{0,3},{1,2},{2,1},{3,0},{4,7},{5,6},{6,5},{7,4},{8,11},{9,10},{10,... | collective-permute-start | bytes 1179656 | tf_op jit(solution)/shard_map/ppermute | solution.py:41
  683.6 47.7 %collective-permute-start.47 = (bf16[1024,384]{1,0:T(8,128)(2,1)S(1)}, bf16[1024,384]{1,0:T(8,128)(2,1)}, u32[]{:S(2)}, u32[]{:S(2)}) collective-permute-start(bf16[1024,384]{1,0:T(8,128)(2,1)S(1)} %copy-done.105), channel_id=1, source_target_pairs={{0,1},{1,0},{2,3},{3,2},{4,5},{5,4},{6,7},{7,6},{8,9},{9,8},{10,11... | collective-permute-start | bytes 2359304 | tf_op jit(solution)/shard_map/ppermute | solution.py:41
  709.9 37.0 %collective-permute-start.48 = (bf16[1024,384]{1,0:T(8,128)(2,1)S(1)}, bf16[1024,384]{1,0:T(8,128)(2,1)}, u32[]{:S(2)}, u32[]{:S(2)}) collective-permute-start(bf16[1024,384]{1,0:T(8,128)(2,1)S(1)} %copy-done.104), channel_id=1, source_target_pairs={{0,2},{1,3},{2,0},{3,1},{4,6},{5,7},{6,4},{7,5},{8,10},{9,11},{10,... | collective-permute-start | bytes 2359304 | tf_op jit(solution)/shard_map/ppermute | solution.py:41
  711.4 35.9 %collective-permute-start.49 = (bf16[1024,384]{1,0:T(8,128)(2,1)}, bf16[1024,384]{1,0:T(8,128)(2,1)}, u32[]{:S(2)}, u32[]{:S(2)}) collective-permute-start(bf16[1024,384]{1,0:T(8,128)(2,1)} %get-tuple-element.247), channel_id=1, source_target_pairs={{0,3},{1,2},{2,1},{3,0},{4,7},{5,6},{6,5},{7,4},{8,11},{9,10},{10,... | collective-permute-start | bytes 2359304 | tf_op jit(solution)/shard_map/ppermute | solution.py:41
  729.2 35.7 %collective-permute-start.37 = (bf16[512,256]{1,0:T(8,128)(2,1)}, bf16[512,256]{1,0:T(8,128)(2,1)S(1)}, u32[]{:S(2)}, u32[]{:S(2)}) collective-permute-start(bf16[512,256]{1,0:T(8,128)(2,1)} %get-tuple-element.232), channel_id=1, source_target_pairs={{0,1},{1,0},{2,3},{3,2},{4,5},{5,4},{6,7},{7,6},{8,9},{9,8},{10,11... | collective-permute-start | bytes 786440 | tf_op jit(solution)/shard_map/ppermute | solution.py:41
  729.4 36.1 %collective-permute-start.76 = (bf16[1024,256]{1,0:T(8,128)(2,1)}, bf16[1024,256]{1,0:T(8,128)(2,1)S(1)}, u32[]{:S(2)}, u32[]{:S(2)}) collective-permute-start(bf16[1024,256]{1,0:T(8,128)(2,1)} %get-tuple-element.283), channel_id=1, source_target_pairs={{0,1},{1,0},{2,3},{3,2},{4,5},{5,4},{6,7},{7,6},{8,9},{9,8},{10,11... | collective-permute-start | bytes 1572872 | tf_op jit(solution)/shard_map/ppermute | solution.py:41
  731.3 35.1 %collective-permute-start.77 = (bf16[1024,256]{1,0:T(8,128)(2,1)S(1)}, bf16[1024,256]{1,0:T(8,128)(2,1)S(1)}, u32[]{:S(2)}, u32[]{:S(2)}) collective-permute-start(bf16[1024,256]{1,0:T(8,128)(2,1)S(1)} %copy-done.107), channel_id=1, source_target_pairs={{0,2},{1,3},{2,0},{3,1},{4,6},{5,7},{6,4},{7,5},{8,10},{9,11},{10,... | collective-permute-start | bytes 1572872 | tf_op jit(solution)/shard_map/ppermute | solution.py:41
  747.3 34.7 %collective-permute-start.63 = (bf16[1024,256]{1,0:T(8,128)(2,1)}, bf16[1024,256]{1,0:T(8,128)(2,1)S(1)}, u32[]{:S(2)}, u32[]{:S(2)}) collective-permute-start(bf16[1024,256]{1,0:T(8,128)(2,1)} %get-tuple-element.266), channel_id=1, source_target_pairs={{0,1},{1,0},{2,3},{3,2},{4,5},{5,4},{6,7},{7,6},{8,9},{9,8},{10,11... | collective-permute-start | bytes 1572872 | tf_op jit(solution)/shard_map/ppermute | solution.py:41
  764.9 35.6 %collective-permute-start.64 = (bf16[1024,256]{1,0:T(8,128)(2,1)}, bf16[1024,256]{1,0:T(8,128)(2,1)}, u32[]{:S(2)}, u32[]{:S(2)}) collective-permute-start(bf16[1024,256]{1,0:T(8,128)(2,1)} %get-tuple-element.267), channel_id=1, source_target_pairs={{0,2},{1,3},{2,0},{3,1},{4,6},{5,7},{6,4},{7,5},{8,10},{9,11},{10,... | collective-permute-start | bytes 1572872 | tf_op jit(solution)/shard_map/ppermute | solution.py:41
  765.5 36.6 %collective-permute-start.65 = (bf16[1024,256]{1,0:T(8,128)(2,1)}, bf16[1024,256]{1,0:T(8,128)(2,1)}, u32[]{:S(2)}, u32[]{:S(2)}) collective-permute-start(bf16[1024,256]{1,0:T(8,128)(2,1)} %get-tuple-element.268), channel_id=1, source_target_pairs={{0,3},{1,2},{2,1},{3,0},{4,7},{5,6},{6,5},{7,4},{8,11},{9,10},{10,... | collective-permute-start | bytes 1572872 | tf_op jit(solution)/shard_map/ppermute | solution.py:41
  766.4 43.3 %collective-permute-start.50 = (bf16[1024,256]{1,0:T(8,128)(2,1)}, bf16[1024,256]{1,0:T(8,128)(2,1)S(1)}, u32[]{:S(2)}, u32[]{:S(2)}) collective-permute-start(bf16[1024,256]{1,0:T(8,128)(2,1)} %get-tuple-element.249), channel_id=1, source_target_pairs={{0,1},{1,0},{2,3},{3,2},{4,5},{5,4},{6,7},{7,6},{8,9},{9,8},{10,11... | collective-permute-start | bytes 1572872 | tf_op jit(solution)/shard_map/ppermute | solution.py:41
  770.7 40.5 %collective-permute-start.51 = (bf16[1024,256]{1,0:T(8,128)(2,1)}, bf16[1024,256]{1,0:T(8,128)(2,1)S(1)}, u32[]{:S(2)}, u32[]{:S(2)}) collective-permute-start(bf16[1024,256]{1,0:T(8,128)(2,1)} %get-tuple-element.250), channel_id=1, source_target_pairs={{0,2},{1,3},{2,0},{3,1},{4,6},{5,7},{6,4},{7,5},{8,10},{9,11},{10,... | collective-permute-start | bytes 1572872 | tf_op jit(solution)/shard_map/ppermute | solution.py:41
  782.0 33.9 %collective-permute-start.52 = (bf16[1024,256]{1,0:T(8,128)(2,1)}, bf16[1024,256]{1,0:T(8,128)(2,1)}, u32[]{:S(2)}, u32[]{:S(2)}) collective-permute-start(bf16[1024,256]{1,0:T(8,128)(2,1)} %get-tuple-element.251), channel_id=1, source_target_pairs={{0,3},{1,2},{2,1},{3,0},{4,7},{5,6},{6,5},{7,4},{8,11},{9,10},{10,... | collective-permute-start | bytes 1572872 | tf_op jit(solution)/shard_map/ppermute | solution.py:41
  (150 other events, 5027.8 us)

commit v2 on v1

v2 whole, which is shorter than its diff:
```python
import math

import jax
import jax.numpy as jnp
from jax import lax
from jax.experimental import pallas as pl
from jax.experimental.pallas import tpu as pltpu
from jax.sharding import PartitionSpec as P

EPS = 1e-06
G = 16
ROWS = 256
TAIL = 16
LANES = 128
BF = jnp.bfloat16
F32 = jnp.float32

RETURN_SPLIT = (2, 4, 4, 4, 2)


def cost(flops, moved, exps=0):
    return pl.CostEstimate(flops=int(flops), bytes_accessed=int(moved), transcendentals=int(exps))


def dot(a, b):
    return jnp.dot(a, b, preferred_element_type=F32)


def whole(shape):
    zeros = (0,) * len(shape)
    return pl.BlockSpec(shape, lambda *_: zeros, pipeline_mode=pl.Buffered(1))


def xor_blocks(x, axis, me, parts):
    size = x.shape[axis] // parts
    return jnp.concatenate(
        [lax.dynamic_slice_in_dim(x, (me ^ d) * size, size, axis) for d in range(parts)], axis
    )


def after(x, *needed):
    return lax.optimization_barrier((x, needed))[0]


def swap(x, name, size, d):
    return lax.ppermute(x, name, [(i, i ^ d) for i in range(size)])


def exchange(pieces, name, size):
    order = sorted(range(1, size), key=lambda d: -d)
    got = {d: swap(pieces[d], name, size, d) for d in order}
    return [pieces[0]] + [got[d] for d in range(1, size)]


def inner_kernel(parts, tok, scale, gain, mix, twiddle, *refs):
    outs, rows_of = refs[:parts], refs[parts]
    block = mix.shape[0]
    al = tok.shape[0] // block
    ql = block // parts
    for a in range(al):
        at = pl.ds(a * block, block)
        normed = (tok[at, :].astype(F32) * (gain[...] * scale[at, :])).astype(BF)
        rows_of[at, :] = dot(mix[...], normed) * twiddle[a]
    for d in range(parts):
        for q in range(ql):
            outs[d][q] = rows_of[pl.ds(d * ql + q, al, stride=block), :].astype(BF)


def inner(tokens, scale, gain, mix, twiddle, parts):
    count, chans = tokens.shape
    block = mix.shape[0]
    al = count // block
    ql = block // parts
    cb = LANES
    return pl.pallas_call(
        lambda *refs: inner_kernel(parts, *refs),
        grid=(chans // cb,),
        in_specs=[
            pl.BlockSpec((count, cb), lambda c: (0, c)),
            whole((count, 1)),
            pl.BlockSpec((1, cb), lambda c: (0, c)),
            whole((block, block)),
            whole((al, block, 1)),
        ],
        out_specs=[pl.BlockSpec((ql, al, cb), lambda c: (0, 0, c)) for _ in range(parts)],
        out_shape=[jax.ShapeDtypeStruct((ql, al, chans), BF) for _ in range(parts)],
        scratch_shapes=[pltpu.VMEM((count, cb), F32)],
        cost_estimate=cost(2 * count * block * chans, 4 * count * chans),
        name="inner_mix",
    )(tokens, scale, gain, mix, twiddle)


def outer_kernel(parts, sizes, *refs):
    pieces = refs[:parts]
    kern, fwd, back, twiddle = refs[parts : parts + 4]
    outs, rows_of = refs[parts + 4 : -1], refs[-1]
    width = kern.shape[-1]
    side = twiddle.shape[1]
    pair = fwd.shape[0] // side
    al = side // parts
    for q in range(0, G, pair):
        x = jnp.concatenate([p[q + i] for i in range(pair) for p in pieces], axis=0)
        k = jnp.concatenate([kern[:, q + i].reshape(side, width) for i in range(pair)], axis=0)
        mixed = dot(fwd[...], x).astype(BF)
        filtered = (mixed.astype(F32) * k.astype(F32)).astype(BF)
        backed = dot(back[...], filtered)
        for i in range(pair):
            turned = backed[i * side : (i + 1) * side] * twiddle[q + i]
            for c in range(width // LANES):
                rows_of[c, pl.ds((q + i) * side, side), :] = turned[:, c * LANES : (c + 1) * LANES]
    for d in range(parts):
        r = d * al
        for out, size in zip(outs, sizes, strict=True):
            for i in range(size):
                for c in range(width // LANES):
                    out[d, i, :, c * LANES : (c + 1) * LANES] = rows_of[
                        c, pl.ds(r, G, stride=side), :
                    ].astype(BF)
                r += 1


def outer(pieces, kern, fwd, back, twiddle, sizes):
    parts = len(pieces)
    ql, al, chans = pieces[0].shape
    side = parts * al
    cb = 256
    return pl.pallas_call(
        lambda *refs: outer_kernel(parts, sizes, *refs),
        grid=(chans // cb, ql // G),
        in_specs=[pl.BlockSpec((G, al, cb), lambda c, q: (q, 0, c)) for _ in range(parts)]
        + [
            pl.BlockSpec((parts, G, al, cb), lambda c, q: (0, q, 0, c)),
            whole(fwd.shape),
            whole(back.shape),
            pl.BlockSpec((G, side, 1), lambda c, q: (q, 0, 0)),
        ],
        out_specs=[pl.BlockSpec((parts, size, G, cb), lambda c, q: (0, 0, q, c)) for size in sizes],
        out_shape=[jax.ShapeDtypeStruct((parts, size, ql, chans), BF) for size in sizes],
        scratch_shapes=[pltpu.VMEM((cb // LANES, G * side, LANES), F32)],
        cost_estimate=cost(8 * side * side * ql * chans, 6 * side * ql * chans),
        name="outer_mix",
    )(*pieces, kern, fwd, back, twiddle)


def eye_at(rows, cols, first):
    return iota((rows, cols), 0) == iota((rows, cols), 1) + first


def mix_kernel(groups, pieces, tok, scale, gain, gain_two, back, up, mixed_out, *outs):
    block, chans = tok.shape
    conv = dot(back[...], pieces[...].reshape(block, chans))
    wide = tok[...].astype(F32)
    normed = (wide * (gain[...] * scale[...])).astype(BF).astype(F32)
    mixed = wide + conv * (normed / (1.0 + jnp.exp(-normed)))
    mixed_out[...] = mixed
    projected = dot((mixed * gain_two[...]).astype(BF), up[...]).astype(BF)
    width = projected.shape[1] // groups
    sums = jnp.sum(mixed * mixed, axis=1, keepdims=True)
    tail = jnp.zeros((TAIL, width), F32)
    line = iota((TAIL, width), 0)
    for u in range(block // width):
        row = jnp.sum(jnp.where(eye_at(block, width, u * width), sums, 0.0), axis=0, keepdims=True)
        for part in range(3):
            piece = row.astype(BF).astype(F32)
            tail = jnp.where(line == 3 * u + part, piece, tail)
            row = row - piece
    for d in range(groups):
        outs[d][0, :block] = projected[:, d * width : (d + 1) * width]
        outs[d][0, block:] = tail.astype(BF)


def mix(home, tokens, scale, gain, gain_two, back, up, row, groups):
    parts, size, ql, chans = home.shape
    block = ql * parts
    count = size * block
    width = up.shape[1] // groups
    return pl.pallas_call(
        lambda *refs: mix_kernel(groups, *refs),
        grid=(size,),
        in_specs=[
            pl.BlockSpec((parts, 1, ql, chans), lambda r: (0, r, 0, 0)),
            pl.BlockSpec((block, chans), lambda r: (r + row, 0)),
            pl.BlockSpec((block, 1), lambda r: (r + row, 0)),
            whole((1, chans)),
            whole((1, chans)),
            whole((block, block)),
            whole(up.shape),
        ],
        out_specs=[pl.BlockSpec((block, chans), lambda r: (r, 0))]
        + [pl.BlockSpec((1, block + TAIL, width), lambda r: (r, 0, 0)) for _ in range(groups)],
        out_shape=[jax.ShapeDtypeStruct((count, chans), F32)]
        + [jax.ShapeDtypeStruct((size, block + TAIL, width), BF) for _ in range(groups)],
        cost_estimate=cost(2 * count * chans * (block + up.shape[1]), 10 * count * chans, count * chans),
        name="mix_tokens",
    )(home, tokens, scale, gain, gain_two, back, up)


def hidden_kernel(groups, total, halves, *refs):
    pieces = refs[:groups]
    up, down = refs[groups : groups + 2]
    outs = refs[groups + 2 :]
    width = pieces[0].shape[2]
    block = pieces[0].shape[1] - TAIL
    tail = sum(p[0, block:].astype(F32) for p in pieces)
    sums = jnp.zeros((block, 1), F32)
    for u in range(block // width):
        row = tail[3 * u : 3 * u + 1] + tail[3 * u + 1 : 3 * u + 2] + tail[3 * u + 2 : 3 * u + 3]
        sums = sums + jnp.sum(jnp.where(eye_at(block, width, u * width), row, 0.0), axis=1, keepdims=True)
    scale = lax.rsqrt(sums / total + EPS)
    part = width // halves
    inside, middle = up.shape[0] // halves, up.shape[1] // halves
    outside = down.shape[1] // halves
    step = outside // groups
    for h in range(halves):
        x = jnp.concatenate([p[0, :block, h * part : (h + 1) * part] for p in pieces], axis=1)
        up_h = up[h * inside : (h + 1) * inside, h * middle : (h + 1) * middle]
        down_h = down[h * middle : (h + 1) * middle, h * outside : (h + 1) * outside]
        v = dot(x, up_h) * scale
        active = (0.5 * v * (1.0 + jnp.tanh(0.7978845608 * (v + 0.044715 * (v * v * v))))).astype(BF)
        reduced = dot(active, down_h).astype(BF)
        for d in range(groups):
            outs[d][:, h * step : (h + 1) * step] = reduced[:, d * step : (d + 1) * step]


def hidden(pieces, up, down, total, halves):
    groups = len(pieces)
    size, tall, width = pieces[0].shape
    block = tall - TAIL
    count = size * block
    step = down.shape[1] // groups
    return pl.pallas_call(
        lambda *refs: hidden_kernel(groups, total, halves, *refs),
        grid=(size,),
        in_specs=[pl.BlockSpec((1, tall, width), lambda t: (t, 0, 0)) for _ in range(groups)]
        + [whole(up.shape), whole(down.shape)],
        out_specs=[pl.BlockSpec((block, step), lambda t: (t, 0)) for _ in range(groups)],
        out_shape=[jax.ShapeDtypeStruct((count, step), BF) for _ in range(groups)],
        cost_estimate=cost(
            2 * count * up.shape[1] * (up.shape[0] + down.shape[1]) // halves,
            2 * groups * count * (width + step),
            count * up.shape[1],
        ),
        name="hidden_units",
    )(*pieces, up, down)


def final_kernel(groups, *refs):
    pieces = refs[:groups]
    mixed, left = refs[groups : groups + 2]
    out = refs[-1]
    x = jnp.concatenate([p[...] for p in pieces], axis=1)
    out[...] = (mixed[...] + dot(x, left[...])).astype(BF)


def final(pieces, mixed, left, row, count_all, carried):
    groups = len(pieces)
    count, step = pieces[0].shape
    chans = mixed.shape[1]
    tb = min(ROWS, count)
    first = row // tb
    extra = [] if carried is None else [carried]
    return pl.pallas_call(
        lambda *refs: final_kernel(groups, *refs),
        grid=(count // tb,),
        in_specs=[pl.BlockSpec((tb, step), lambda t: (t, 0)) for _ in range(groups)]
        + [pl.BlockSpec((tb, chans), lambda t: (t, 0)), whole(left.shape)]
        + [pl.BlockSpec(memory_space=pl.ANY) for _ in extra],
        out_specs=pl.BlockSpec((tb, chans), lambda t: (t + first, 0)),
        out_shape=jax.ShapeDtypeStruct((count_all, chans), BF),
        input_output_aliases={groups + 2: 0} if extra else {},
        cost_estimate=cost(2 * count * groups * step * chans, 8 * count * chans),
        name="block_out",
    )(*pieces, mixed, left, *extra)


def iota(shape, axis):
    return lax.broadcasted_iota(jnp.int32, shape, axis)


def pick(rows, cols, of_col):
    return (iota((rows, cols), 0) == of_col(iota((rows, cols), 1))).astype(BF)


def masked(x, keep):
    rows, cols = iota(x.shape, 0), iota(x.shape, 1)
    return jnp.where(keep(rows, cols), x, 0.0).astype(BF)


def repeat_block(x, times):
    rows, cols = x.shape
    return masked(
        jnp.tile(x.astype(F32), (times, times)), lambda r, c: r // rows == c // cols
    )


def expand_factors(right_up, left_up, right_down, left_down, me, groups, halves):
    il, nj, nk = right_up.shape
    kl, ni, nm = left_up.shape
    nq = right_down.shape[2]
    ql, nkk, nr = left_down.shape
    lk, lr = kl * il, ql * kl

    def place(at, lanes):
        part = lanes // halves
        half, rest = at // (groups * part), at % (groups * part)
        return rest // part, half * part + rest % part

    def up_two_source(r):
        d, lane = place(r, lk)
        return (lane // il) * ni + (me ^ d) * il + lane % il

    def down_one_source(c):
        d, lane = place(c, lr)
        return (me ^ d) * ql + lane % ql

    def down_two_source(r):
        lane = r % lr
        return (lane % ql) * nkk + (me ^ (r // lr)) * kl + lane // ql

    up_one = masked(
        dot(
            right_up.reshape(il * nj, nk),
            pick(nk, groups * lk, lambda c: (me ^ (c // lk)) * kl + c % lk // il),
        ),
        lambda r, c: r // nj == c % il,
    )
    rows = groups * lk
    taken = dot(pick(kl * ni, rows, up_two_source).T, left_up.reshape(kl * ni, nm))
    up_two = masked(
        jnp.tile(taken, (1, kl)), lambda r, c: c // nm == place(r, lk)[1] // il
    )
    down_one = masked(
        dot(right_down.reshape(kl * nm, nq), pick(nq, groups * lr, down_one_source)),
        lambda r, c: r // nm == place(c, lr)[1] // ql,
    )
    rows = groups * lr
    taken = dot(pick(ql * nkk, rows, down_two_source).T, left_down.reshape(ql * nkk, nr)).astype(BF)
    down_two = masked(
        dot(taken, pick(nr, ql * nr, lambda c: c % nr)),
        lambda r, c: c // nr == r % lr % ql,
    )
    return up_one, up_two, down_one, down_two


def splits_of(total, shares):
    unit = total // sum(shares)
    if unit * sum(shares) != total:
        return [total]
    return [unit * share for share in shares]


def make_shards(parts, groups):
    def shards(
        tokens,
        seq_inner,
        seq_outer,
        inv_outer,
        inv_inner,
        twiddle_in,
        twiddle_out,
        freq_kernel,
        first_gain,
        second_gain,
        right_up,
        left_up,
        right_down,
        left_down,
    ):
        _, count, chans = tokens.shape
        total = chans * groups
        block = seq_inner.shape[0]
        ql = block // parts
        al = count // block
        at = lax.axis_index("ctx")
        me = lax.axis_index("hid")
        tok = tokens.reshape(count, chans)

        sent = freq_kernel.reshape(al, parts, ql, chans).transpose(1, 2, 0, 3)
        kern = lax.all_to_all(sent, "ctx", split_axis=0, concat_axis=0, tiled=True)

        wide = tok.astype(F32)
        sums = lax.psum(jnp.sum(wide * wide, axis=1), "hid")
        scale = lax.rsqrt(sums / total + EPS).reshape(count, 1)
        gain = first_gain.reshape(1, chans)
        gain_two = second_gain.reshape(1, chans)

        pieces = inner(
            tok,
            scale,
            gain,
            xor_blocks(seq_inner, 0, at, parts),
            xor_blocks(twiddle_in, 1, at, parts).reshape(al, block, 1),
            parts,
        )
        fwd = repeat_block(xor_blocks(seq_outer, 1, at, parts), 2)
        back = repeat_block(inv_outer, 2)
        turn = twiddle_out.T.reshape(ql, al * parts, 1)
        sizes = splits_of(al, RETURN_SPLIT)
        pieces = exchange(pieces, "ctx", parts)

        lanes = right_up.shape[0] * left_up.shape[0]
        halves = lanes // 128 if lanes % 128 == 0 else 1
        up_one, up_two, down_one, down_two = expand_factors(
            right_up, left_up, right_down, left_down, me, groups, halves
        )
        kern = after(kern, up_one, up_two, down_one, down_two, turn)
        backed = outer(pieces, kern, fwd, back, turn, sizes)
        chunks = len(sizes)
        starts = [sum(sizes[:j]) for j in range(chunks)]
        mixed, ups, downs, done = {}, {}, {}, {}
        out = None

        def hide(j):
            downs[j] = hidden(ups[j], up_two, down_one, total, halves)
            done[j] = downs[j][0]
            downs[j] = exchange(downs[j], "hid", groups)

        def finish(j, out):
            return final(downs[j], mixed[j], down_two, starts[j] * block, count, out)

        for j in range(chunks):
            needed = []
            if j >= 2:
                needed.append(mixed[j - 2])
            if j >= 3:
                needed.append(done[j - 3])
            if j >= 4:
                needed.append(out)
            sent = after(backed[j], *needed) if needed else backed[j]
            home = lax.all_to_all(sent, "ctx", split_axis=0, concat_axis=0, tiled=True)
            mixed[j], *pieces = mix(
                home, tok, scale, gain, gain_two, inv_inner, up_one, starts[j], groups
            )
            ups[j] = exchange(pieces, "hid", groups)
            if j >= 1:
                hide(j - 1)
            if j >= 2:
                out = finish(j - 2, out)
        hide(chunks - 1)
        for j in range(max(chunks - 2, 0), chunks):
            out = finish(j, out)
        return out.reshape(1, count, chans)

    return shards


def solution(mesh):
    return jax.shard_map(
        make_shards(mesh.shape["ctx"], mesh.shape["hid"]),
        mesh=mesh,
        in_specs=(
            P(None, "ctx", "hid"),
            P(),
            P(),
            P(),
            P(),
            P("ctx", None),
            P(None, "ctx"),
            P("ctx", None, "hid"),
            P("hid"),
            P("hid"),
            P("hid", None, None),
            P("hid", None, None),
            P("hid", None, None),
            P("hid", None, None),
        ),
        out_specs=P(None, "ctx", "hid"),
        check_vma=False,
    )
```

time: 851 us -> 786 us (0.924)
  starting transfers between devices: 150 us -> 67.7 us
  blocking collectives: 16.2 us -> 90.2 us
  Pallas kernels: 237 us -> 167 us
  waiting for transfers between devices: 379 us -> 394 us
    ppermute x79 -> x37, starting transfers between devices: 143 us -> 44.9 us  [swap(): return lax.ppermute(x, name, [(i, i ^ d) for i in range(size)])]
    all_to_all x0 -> x1, blocking collectives: none -> 73.7 us  [shards(): home = lax.all_to_all(sent, 'ctx', split_axis=0, concat_axis=0, tiled=True)]
    pallas_call x13 -> x12, Pallas kernels: 206 us -> 137 us  [the longest x5 47.8 us: hidden(): pl.pallas_call(lambda *refs: hidden_kernel(groups, total, halves, *refs),...]
    ppermute x79 -> x37, waiting for transfers between devices: 379 us -> 316 us  [swap(): return lax.ppermute(x, name, [(i, i ^ d) for i in range(size)])]
    all_to_all x0 -> x4, waiting for transfers between devices: none -> 58.6 us  [shards(): home = lax.all_to_all(sent, 'ctx', split_axis=0, concat_axis=0, tiled=True)]
    all_to_all x1, waiting for transfers between devices: 0.01 us -> 19.5 us  [shards(): kern = lax.all_to_all(sent, 'ctx', split_axis=0, concat_axis=0, tiled=True)]
    unnamed x250 -> x116, local copies, waits for them, and re-layouts: 6.18 us -> 23.1 us
    all_to_all x0 -> x4, starting transfers between devices: none -> 16.3 us  [shards(): home = lax.all_to_all(sent, 'ctx', split_axis=0, concat_axis=0, tiled=True)]
  transfers between devices with their start and end apart: 80 -> 42, of which waited for: 22 -> 20; matrix products, arithmetic and copies ran while one was open for 5% -> 5% of each run, Pallas kernels for 24% -> 18%
where the time goes in v2:
time: 786 us; the launch traced here: 779 us
  waiting for transfers between devices  394 us (50%)
  Pallas kernels  167 us (21%)
  blocking collectives  90.2 us (11%)
  starting transfers between devices  67.7 us (9%)
  local copies, waits for them, and re-layouts  31.6 us (4%)
  other arithmetic  14.2 us (2%)
  matrix products  13.6 us (2%)
    ppermute x37, waiting for transfers between devices, swap(): return lax.ppermute(x, name, [(i, i ^ d) for i in range(size)])  316 us
    all_to_all x1, blocking collectives, shards(): home = lax.all_to_all(sent, 'ctx', split_axis=0, concat_axis=0, tiled=True)  73.7 us
    all_to_all x4, waiting for transfers between devices, shards(): home = lax.all_to_all(sent, 'ctx', split_axis=0, concat_axis=0, tiled=True)  58.6 us
    pallas_call x5, Pallas kernels, hidden(): pl.pallas_call(lambda *refs: hidden_kernel(groups, total, halves, *refs),...  47.8 us
    ppermute x37, starting transfers between devices, swap(): return lax.ppermute(x, name, [(i, i ^ d) for i in range(size)])  44.9 us
    pallas_call x5, Pallas kernels, mix(): pl.pallas_call(lambda *refs: mix_kernel(groups, *refs), grid=(size,), in_...  37.5 us
    pallas_call x5, Pallas kernels, final(): pl.pallas_call(lambda *refs: final_kernel(groups, *refs), grid=(count //...  30.1 us
    pallas_call x1, Pallas kernels, inner(): pl.pallas_call(lambda *refs: inner_kernel(parts, *refs), grid=(chans // c...  26.3 us
  transfers between devices with their start and end apart: 42, of which 20 were waited for; matrix products, arithmetic and copies ran while one was open for 5% of the time, Pallas kernels for 18%

profile of v2, /device:TPU:0, one launch (start us, length us, event | category | flops | bytes accessed | tf_op | source)
XLA Modules:
  0.0 778.9 jit_solution(17208022311837615263)
XLA Ops:
  0.0 11.5 %copy.24 = bf16[16,256,1024]{2,0,1:T(8,128)(2,1)} copy(bf16[16,256,1024]{2,1,0:T(8,128)(2,1)} %param.21) | data formatting | bytes 16777216 | tf_op args[7]
  11.5 6.5 all-to-all-start
  20.1 5.1 multiply_reduce_fusion
  25.3 16.5 %psum.7 = f32[4096]{0:T(1024)S(1)} all-reduce(f32[4096]{0:T(1024)S(1)} %multiply_reduce_fusion), channel_id=1, replica_groups=mesh['ctx'=8,'hid'=4] {'hid'}, use_global_device_ids=true, to_apply=%region_1.0 | all-reduce | flops 4096 | bytes 32768 | tf_op jit(solution)/shard_map/psum | solution.py:382
  44.5 26.3 %inner_mix.1 = (bf16[32,16,1024]{2,1,0:T(8,128)(2,1)}, bf16[32,16,1024]{2,1,0:T(8,128)(2,1)}, bf16[32,16,1024]{2,1,0:T(8,128)(2,1)}, bf16[32,16,1024]{2,1,0:T(8,...) custom-call(bf16[4096,1024]{1,0:T(8,128)(2,1)} %bitcast.51, ...), custom_call_target="tpu_custom_call" | custom-call | flops 2147483648 | bytes 16777216 | tf_op jit(solution)/shard_map/inner_mix/pallas_call | solution.py:75
  78.0 3.1 fusion.40
  81.1 3.7 fusion.9.refs_5_
  85.5 5.1 fusion.8.refs_4_
  96.0 3.1 fusion.31.refs_6_
  99.0 3.5 collective-permute-start.5
  102.5 74.2 %collective-permute-done.1.refs_2_ = bf16[32,16,1024]{2,1,0:T(8,128)(2,1)S(1)} collective-permute-done((bf16[32,16,1024]{2,1,0:T(8,128)(2,1)}, bf16[32,16,1024]{2,1,0:T(8,128)(2,1)S(1)}, u32[]{:S(2)}, u32[]{:S(2)}) %collective-permute-start.1) | collective-permute-done | bytes 1048608 | tf_op jit(solution)/shard_map/ppermute | solution.py:46
  179.3 3.7 select_convert_fusion.refs_5_
  183.0 19.5 %all-to-all-done.refs_8_ = bf16[8,32,16,1024]{3,2,1,0:T(8,128)(2,1)} async-done(((bf16[8,32,16,1024]{3,2,1,0:T(8,128)(2,1)}), bf16[8,32,16,1024]{3,2,1,0:T(8,128)(2,1)}, u32[]{:S(2)}, u32[]{:S(2)}) %all-to-all-start) | async-done | bytes 8388640 | tf_op jit(solution)/shard_map/all_to_all | solution.py:379
  202.5 112.3 %collective-permute-done.3.refs_4_ = bf16[32,16,1024]{2,1,0:T(8,128)(2,1)} collective-permute-done((bf16[32,16,1024]{2,1,0:T(8,128)(2,1)}, bf16[32,16,1024]{2,1,0:T(8,128)(2,1)}, u32[]{:S(2)}, u32[]{:S(2)}) %collective-permute-start.3) | collective-permute-done | bytes 1048608 | tf_op jit(solution)/shard_map/ppermute | solution.py:46
  314.8 21.5 %collective-permute-done.4.refs_5_ = bf16[32,16,1024]{2,1,0:T(8,128)(2,1)} collective-permute-done((bf16[32,16,1024]{2,1,0:T(8,128)(2,1)}, bf16[32,16,1024]{2,1,0:T(8,128)(2,1)}, u32[]{:S(2)}, u32[]{:S(2)}) %collective-permute-start.4) | collective-permute-done | bytes 1048608 | tf_op jit(solution)/shard_map/ppermute | solution.py:46
  336.3 24.9 %outer_mix.1 = (bf16[8,2,32,1024]{3,2,1,0:T(8,128)(2,1)}, bf16[8,4,32,1024]{3,2,1,0:T(8,128)(2,1)}, bf16[8,4,32,1024]{3,2,1,0:T(8,128)(2,1)}, bf16[8,4,32,1024]{3,2,1,0:T(8,128)(2,1)}, bf16[8,2,32,1024]{3,2,1,0:T(8,128)(2,1)}) custom-call(bf16[32,16,1024]{2,1,0:T(8,128)(2,1)} %get-tuple-element.67.refs_0_, bf16[32,16,1024]{2,1,0:T(8,128)(2,1)} %copy-done.6, ...), custom_call_target="tpu_custom_call" | custom-call | flops 4294967296 | bytes 25165824 | tf_op jit(solution)/shard_map/outer_mix/pallas_call | solution.py:127
  361.2 73.7 %all_to_all.30.refs_0_ = bf16[8,2,32,1024]{3,2,1,0:T(8,128)(2,1)} all-to-all(bf16[8,2,32,1024]{3,2,1,0:T(8,128)(2,1)} %get-tuple-element.78), channel_id=1, replica_groups=mesh['ctx'=8,'hid'=4] {'ctx'}, dimensions={0} | all-to-all | bytes 2097152 | tf_op jit(solution)/shard_map/all_to_all | solution.py:430
  435.0 3.6 all-to-all-start.3
  438.6 5.7 mix_tokens.5
  444.3 43.3 %all-to-all-done.3.refs_0_ = bf16[8,4,32,1024]{3,2,1,0:T(8,128)(2,1)S(1)} async-done(((bf16[8,4,32,1024]{3,2,1,0:T(8,128)(2,1)}), bf16[8,4,32,1024]{3,2,1,0:T(8,128)(2,1)S(1)}, u32[]{:S(2)}, u32[]{:S(2)}) %all-to-all-start.3) | async-done | bytes 2097184 | tf_op jit(solution)/shard_map/all_to_all | solution.py:430
  488.9 3.6 all-to-all-start.2
  496.1 6.2 collective-permute-done.13.refs_1_
  502.3 6.6 collective-permute-done.14.refs_2_
  509.7 7.7 hidden_units.6
  517.4 8.8 %mix_tokens.7 = (f32[1024,1024]{1,0:T(8,128)}, bf16[4,272,256]{2,1,0:T(8,128)(2,1)}, bf16[4,272,256]{2,1,0:T(8,128)(2,1)}, bf16[4,272,256]{2,1,0:T(8,128)(2,1)}, bf16[4,272,256]{2,1,0:T(8,128)(2,1)}) custom-call(bf16[8,4,32,1024]{3,2,1,0:T(8,128)(2,1)} %copy-done.3, bf16[4096,1024]{1,0:T(8,128)(2,1)} %bitcast.53, f32[4096,1]{1,0:T(8,128)} %copy.22.refs_1_.refs_2_, ...), custom_call_target="tpu_custom_call" | custom-call | flops 2684354560 | bytes 10485760 | tf_op jit(solution)/shard_map/mix_tokens/pallas_call | solution.py:177
  526.2 15.3 %all-to-all-done.2.refs_0_ = bf16[8,4,32,1024]{3,2,1,0:T(8,128)(2,1)S(1)} async-done(((bf16[8,4,32,1024]{3,2,1,0:T(8,128)(2,1)}), bf16[8,4,32,1024]{3,2,1,0:T(8,128)(2,1)S(1)}, u32[]{:S(2)}, u32[]{:S(2)}) %all-to-all-start.2) | async-done | bytes 2097184 | tf_op jit(solution)/shard_map/all_to_all | solution.py:430
  541.5 4.4 all-to-all-start.5
  550.9 10.7 %collective-permute-done.7.refs_1_ = bf16[4,272,256]{2,1,0:T(8,128)(2,1)S(1)} collective-permute-done((bf16[4,272,256]{2,1,0:T(8,128)(2,1)}, bf16[4,272,256]{2,1,0:T(8,128)(2,1)S(1)}, u32[]{:S(2)}, u32[]{:S(2)}) %collective-permute-start.7) | collective-permute-done | bytes 557088 | tf_op jit(solution)/shard_map/ppermute | solution.py:46
  561.6 11.4 %collective-permute-done.8.refs_2_ = bf16[4,272,256]{2,1,0:T(8,128)(2,1)S(1)} collective-permute-done((bf16[4,272,256]{2,1,0:T(8,128)(2,1)S(1)}, bf16[4,272,256]{2,1,0:T(8,128)(2,1)S(1)}, u32[]{:S(2)}, u32[]{:S(2)}) %collective-permute-start.8) | collective-permute-done | bytes 557088 | tf_op jit(solution)/shard_map/ppermute | solution.py:46
  575.3 10.8 %hidden_units.5 = (bf16[1024,256]{1,0:T(8,128)(2,1)}, bf16[1024,256]{1,0:T(8,128)(2,1)}, bf16[1024,256]{1,0:T(8,128)(2,1)}, bf16[1024,256]{1,0:T(8,128)(2,1)}) custom-call(bf16[4,272,256]{2,1,0:T(8,128)(2,1)} %get-tuple-element.83.refs_0_, bf16[4,272,256]{2,1,0:T(8,128)(2,1)} %copy-done.47, bf16[4,272,256]{2,1,0:T(8,128)(2,1)} %copy-done.48, ...), custom_call_target="tpu_custom_call" | custom-call | flops 4294967296 | bytes 4194304 | tf_op jit(solution)/shard_map/hidden_units/pallas_call | solution.py:231
  592.7 30.2 %collective-permute-done.17.refs_2_ = bf16[512,256]{1,0:T(8,128)(2,1)S(1)} collective-permute-done((bf16[512,256]{1,0:T(8,128)(2,1)S(1)}, bf16[512,256]{1,0:T(8,128)(2,1)S(1)}, u32[]{:S(2)}, u32[]{:S(2)}) %collective-permute-start.17) | collective-permute-done | bytes 262176 | tf_op jit(solution)/shard_map/ppermute | solution.py:46
  624.4 4.6 block_out.5.refs_6_
  630.1 7.0 block_out.6.refs_6_
  637.1 8.7 %mix_tokens.6 = (f32[1024,1024]{1,0:T(8,128)}, bf16[4,272,256]{2,1,0:T(8,128)(2,1)}, bf16[4,272,256]{2,1,0:T(8,128)(2,1)}, bf16[4,272,256]{2,1,0:T(8,128)(2,1)}, bf16[4,272,256]{2,1,0:T(8,128)(2,1)}) custom-call(bf16[8,4,32,1024]{3,2,1,0:T(8,128)(2,1)} %copy-done.2, bf16[4096,1024]{1,0:T(8,128)(2,1)} %bitcast.54, f32[4096,1]{1,0:T(8,128)} %copy.22.refs_1_.refs_2_, ...), custom_call_target="tpu_custom_call" | custom-call | flops 2684354560 | bytes 10485760 | tf_op jit(solution)/shard_map/mix_tokens/pallas_call | solution.py:177
  645.8 4.8 all-to-all-start.4
  654.0 8.7 %mix_tokens.9 = (f32[1024,1024]{1,0:T(8,128)}, bf16[4,272,256]{2,1,0:T(8,128)(2,1)}, bf16[4,272,256]{2,1,0:T(8,128)(2,1)}, bf16[4,272,256]{2,1,0:T(8,128)(2,1)}, bf16[4,272,256]{2,1,0:T(8,128)(2,1)}) custom-call(bf16[8,4,32,1024]{3,2,1,0:T(8,128)(2,1)} %all-to-all-done.5.refs_0_, bf16[4096,1024]{1,0:T(8,128)(2,1)} %bitcast.55, ...), custom_call_target="tpu_custom_call" | custom-call | flops 2684354560 | bytes 10485760 | tf_op jit(solution)/shard_map/mix_tokens/pallas_call | solution.py:177
  666.9 11.7 %collective-permute-done.32.refs_2_ = bf16[4,272,256]{2,1,0:T(8,128)(2,1)} collective-permute-done((bf16[4,272,256]{2,1,0:T(8,128)(2,1)}, bf16[4,272,256]{2,1,0:T(8,128)(2,1)}, u32[]{:S(2)}, u32[]{:S(2)}) %collective-permute-start.32) | collective-permute-done | bytes 557088 | tf_op jit(solution)/shard_map/ppermute | solution.py:46
  678.6 10.8 %hidden_units.9 = (bf16[1024,256]{1,0:T(8,128)(2,1)}, bf16[1024,256]{1,0:T(8,128)(2,1)}, bf16[1024,256]{1,0:T(8,128)(2,1)}, bf16[1024,256]{1,0:T(8,128)(2,1)}) custom-call(bf16[4,272,256]{2,1,0:T(8,128)(2,1)} %get-tuple-element.121.refs_0_, bf16[4,272,256]{2,1,0:T(8,128)(2,1)} %copy-done.44, bf16[4,272,256]{2,1,0:T(8,128)(2,1)} %collective-permute-done.32.refs_2_, ...), custom_call_target="tpu_custom_call" | custom-call | flops 4294967296 | bytes 4194304 | tf_op jit(solution)/shard_map/hidden_units/pallas_call | solution.py:231
  692.5 5.7 mix_tokens.8
  702.6 2.9 collective-permute-start.21
  705.5 10.8 %hidden_units.8 = (bf16[1024,256]{1,0:T(8,128)(2,1)}, bf16[1024,256]{1,0:T(8,128)(2,1)}, bf16[1024,256]{1,0:T(8,128)(2,1)}, bf16[1024,256]{1,0:T(8,128)(2,1)}) custom-call(bf16[4,272,256]{2,1,0:T(8,128)(2,1)} %get-tuple-element.112.refs_0_, bf16[4,272,256]{2,1,0:T(8,128)(2,1)} %copy-done.42, bf16[4,272,256]{2,1,0:T(8,128)(2,1)} %copy-done.43, ...), custom_call_target="tpu_custom_call" | custom-call | flops 4294967296 | bytes 4194304 | tf_op jit(solution)/shard_map/hidden_units/pallas_call | solution.py:231
  720.5 15.5 %collective-permute-done.20.refs_2_ = bf16[2,272,256]{2,1,0:T(8,128)(2,1)S(1)} collective-permute-done((bf16[2,272,256]{2,1,0:T(8,128)(2,1)}, bf16[2,272,256]{2,1,0:T(8,128)(2,1)S(1)}, u32[]{:S(2)}, u32[]{:S(2)}) %collective-permute-start.20) | collective-permute-done | bytes 278560 | tf_op jit(solution)/shard_map/ppermute | solution.py:46
  737.4 3.2 collective-permute-start.30
  740.6 7.7 hidden_units.7
  751.9 7.0 block_out.7.refs_6_
  758.9 4.0 collective-permute-done.29.refs_2_
  763.9 7.0 block_out.8.refs_6_
  773.9 4.6 block_out.9
  (206 shorter events, 71.0 us)
Async XLA Ops:
  11.5 190.9 %all-to-all-start = ((bf16[8,32,16,1024]{3,2,1,0:T(8,128)(2,1)}), bf16[8,32,16,1024]{3,2,1,0:T(8,128)(2,1)}, u32[]{:S(2)}, u32[]{:S(2)}) async-start(bf16[8,32,16,1024]{3,2,1,0:T(8,128)(2,1)} %bitcast.57), calls=%async_computation | async-start | bytes 16777216 | tf_op jit(solution)/shard_map/all_to_all | solution.py:379
  70.8 28.2 %collective-permute-start = (bf16[32,16,1024]{2,1,0:T(8,128)(2,1)}, bf16[32,16,1024]{2,1,0:T(8,128)(2,1)S(1)}, u32[]{:S(2)}, u32[]{:S(2)}) collective-permute-start(bf16[32,16,1024]{2,1,0:T(8,128)(2,1)} %get-tuple-element.68), channel_id=1, source_target_pairs={{0,4},{4,0},{8,12},{12,8},{16,20},{20,16},{24,28},{28,24},{1,5},{5... | collective-permute-start | bytes 3145736 | tf_op jit(solution)/shard_map/ppermute | solution.py:46
  70.9 105.8 %collective-permute-start.1 = (bf16[32,16,1024]{2,1,0:T(8,128)(2,1)}, bf16[32,16,1024]{2,1,0:T(8,128)(2,1)S(1)}, u32[]{:S(2)}, u32[]{:S(2)}) collective-permute-start(bf16[32,16,1024]{2,1,0:T(8,128)(2,1)} %get-tuple-element.69), channel_id=1, source_target_pairs={{0,8},{4,12},{8,0},{12,4},{16,24},{20,28},{24,16},{28,20},{1,9},{5... | collective-permute-start | bytes 3145736 | tf_op jit(solution)/shard_map/ppermute | solution.py:46
  72.8 129.7 %collective-permute-start.2 = (bf16[32,16,1024]{2,1,0:T(8,128)(2,1)}, bf16[32,16,1024]{2,1,0:T(8,128)(2,1)S(1)}, u32[]{:S(2)}, u32[]{:S(2)}) collective-permute-start(bf16[32,16,1024]{2,1,0:T(8,128)(2,1)} %get-tuple-element.70), channel_id=1, source_target_pairs={{0,12},{4,8},{8,4},{12,0},{16,28},{20,24},{24,20},{28,16},{1,13},{... | collective-permute-start | bytes 3145736 | tf_op jit(solution)/shard_map/ppermute | solution.py:46
  72.9 242.0 %collective-permute-start.3 = (bf16[32,16,1024]{2,1,0:T(8,128)(2,1)}, bf16[32,16,1024]{2,1,0:T(8,128)(2,1)}, u32[]{:S(2)}, u32[]{:S(2)}) collective-permute-start(bf16[32,16,1024]{2,1,0:T(8,128)(2,1)} %get-tuple-element.71), channel_id=1, source_target_pairs={{0,16},{4,20},{8,24},{12,28},{16,0},{20,4},{24,8},{28,12},{1,17},{... | collective-permute-start | bytes 3145736 | tf_op jit(solution)/shard_map/ppermute | solution.py:46
  75.5 260.8 %collective-permute-start.4 = (bf16[32,16,1024]{2,1,0:T(8,128)(2,1)}, bf16[32,16,1024]{2,1,0:T(8,128)(2,1)}, u32[]{:S(2)}, u32[]{:S(2)}) collective-permute-start(bf16[32,16,1024]{2,1,0:T(8,128)(2,1)} %get-tuple-element.72), channel_id=1, source_target_pairs={{0,20},{4,16},{8,28},{12,24},{16,4},{20,0},{24,12},{28,8},{1,21},{... | collective-permute-start | bytes 3145736 | tf_op jit(solution)/shard_map/ppermute | solution.py:46
  95.9 83.3 %copy-start.39 = (pred[1024]{0:T(1024)(128)(4,1)S(1)}, pred[1024]{0:T(1024)(128)(4,1)}, u32[]{:S(2)}) copy-start(pred[1024]{0:T(1024)(128)(4,1)} %get-tuple-element.149) | copy-start | bytes 3076
  95.9 83.3 %copy-start.40 = (pred[1024]{0:T(1024)(128)(4,1)S(1)}, pred[1024]{0:T(1024)(128)(4,1)}, u32[]{:S(2)}) copy-start(pred[1024]{0:T(1024)(128)(4,1)} %get-tuple-element.150) | copy-start | bytes 3076
  95.9 83.3 %copy-start.41 = (pred[1024]{0:T(1024)(128)(4,1)S(1)}, pred[1024]{0:T(1024)(128)(4,1)}, u32[]{:S(2)}) copy-start(pred[1024]{0:T(1024)(128)(4,1)} %get-tuple-element.151) | copy-start | bytes 3076
  96.0 83.3 %copy-start.51 = (bf16[16,64,64]{2,1,0:T(8,128)(2,1)S(1)}, bf16[16,64,64]{2,1,0:T(8,128)(2,1)}, u32[]{:S(2)}) copy-start(bf16[16,64,64]{2,1,0:T(8,128)(2,1)} %param.27) | copy-start | bytes 393220
  99.0 84.0 %copy-start.6 = (bf16[32,16,1024]{2,1,0:T(8,128)(2,1)}, bf16[32,16,1024]{2,1,0:T(8,128)(2,1)S(1)}, u32[]{:S(2)}) copy-start(bf16[32,16,1024]{2,1,0:T(8,128)(2,1)S(1)} %collective-permute-done.refs_1_) | copy-start | bytes 3145732
  99.0 237.3 %collective-permute-start.5 = (bf16[32,16,1024]{2,1,0:T(8,128)(2,1)}, bf16[32,16,1024]{2,1,0:T(8,128)(2,1)}, u32[]{:S(2)}, u32[]{:S(2)}) collective-permute-start(bf16[32,16,1024]{2,1,0:T(8,128)(2,1)} %get-tuple-element.73), channel_id=1, source_target_pairs={{0,24},{4,28},{8,16},{12,20},{16,8},{20,12},{24,0},{28,4},{1,25},{... | collective-permute-start | bytes 3145736 | tf_op jit(solution)/shard_map/ppermute | solution.py:46
  176.7 159.6 %collective-permute-start.6 = (bf16[32,16,1024]{2,1,0:T(8,128)(2,1)}, bf16[32,16,1024]{2,1,0:T(8,128)(2,1)}, u32[]{:S(2)}, u32[]{:S(2)}) collective-permute-start(bf16[32,16,1024]{2,1,0:T(8,128)(2,1)} %get-tuple-element.74), channel_id=1, source_target_pairs={{0,28},{4,24},{8,20},{12,16},{16,12},{20,8},{24,4},{28,0},{1,29},{... | collective-permute-start | bytes 3145736 | tf_op jit(solution)/shard_map/ppermute | solution.py:46
  202.5 133.9 %copy-start.8 = (bf16[32,16,1024]{2,1,0:T(8,128)(2,1)}, bf16[32,16,1024]{2,1,0:T(8,128)(2,1)S(1)}, u32[]{:S(2)}) copy-start(bf16[32,16,1024]{2,1,0:T(8,128)(2,1)S(1)} %collective-permute-done.2.refs_3_) | copy-start | bytes 3145732
  435.0 52.6 %all-to-all-start.3 = ((bf16[8,4,32,1024]{3,2,1,0:T(8,128)(2,1)}), bf16[8,4,32,1024]{3,2,1,0:T(8,128)(2,1)S(1)}, u32[]{:S(2)}, u32[]{:S(2)}) async-start(bf16[8,4,32,1024]{3,2,1,0:T(8,128)(2,1)} %get-tuple-element.82), calls=%async_computation.3 | async-start | bytes 4194304 | tf_op jit(solution)/shard_map/all_to_all | solution.py:430
  488.9 52.6 %all-to-all-start.2 = ((bf16[8,4,32,1024]{3,2,1,0:T(8,128)(2,1)}), bf16[8,4,32,1024]{3,2,1,0:T(8,128)(2,1)S(1)}, u32[]{:S(2)}, u32[]{:S(2)}) async-start(bf16[8,4,32,1024]{3,2,1,0:T(8,128)(2,1)} %get-tuple-element.80), calls=%async_computation.2 | async-start | bytes 4194304 | tf_op jit(solution)/shard_map/all_to_all | solution.py:430
  492.5 9.8 %collective-permute-start.13 = (bf16[2,272,256]{2,1,0:T(8,128)(2,1)}, bf16[2,272,256]{2,1,0:T(8,128)(2,1)S(1)}, u32[]{:S(2)}, u32[]{:S(2)}) collective-permute-start(bf16[2,272,256]{2,1,0:T(8,128)(2,1)} %get-tuple-element.93), channel_id=1, source_target_pairs={{0,1},{1,0},{2,3},{3,2},{4,5},{5,4},{6,7},{7,6},{8,9},{9,8},{10,11... | collective-permute-start | bytes 835592 | tf_op jit(solution)/shard_map/ppermute | solution.py:46
  494.1 14.8 %collective-permute-start.14 = (bf16[2,272,256]{2,1,0:T(8,128)(2,1)}, bf16[2,272,256]{2,1,0:T(8,128)(2,1)S(1)}, u32[]{:S(2)}, u32[]{:S(2)}) collective-permute-start(bf16[2,272,256]{2,1,0:T(8,128)(2,1)} %get-tuple-element.94), channel_id=1, source_target_pairs={{0,2},{1,3},{2,0},{3,1},{4,6},{5,7},{6,4},{7,5},{8,10},{9,11},{10,... | collective-permute-start | bytes 835592 | tf_op jit(solution)/shard_map/ppermute | solution.py:46
  495.6 13.3 %collective-permute-start.15 = (bf16[2,272,256]{2,1,0:T(8,128)(2,1)S(1)}, bf16[2,272,256]{2,1,0:T(8,128)(2,1)S(1)}, u32[]{:S(2)}, u32[]{:S(2)}) collective-permute-start(bf16[2,272,256]{2,1,0:T(8,128)(2,1)S(1)} %copy-done.50), channel_id=1, source_target_pairs={{0,3},{1,2},{2,1},{3,0},{4,7},{5,6},{6,5},{7,4},{8,11},{9,10},{10,... | collective-permute-start | bytes 835592 | tf_op jit(solution)/shard_map/ppermute | solution.py:46
  541.5 104.3 %all-to-all-start.5 = ((bf16[8,4,32,1024]{3,2,1,0:T(8,128)(2,1)}), bf16[8,4,32,1024]{3,2,1,0:T(8,128)(2,1)}, u32[]{:S(2)}, u32[]{:S(2)}) async-start(bf16[8,4,32,1024]{3,2,1,0:T(8,128)(2,1)} %get-tuple-element.111), calls=%async_computation.5 | async-start | bytes 4194304 | tf_op jit(solution)/shard_map/all_to_all | solution.py:430
  545.9 15.7 %collective-permute-start.7 = (bf16[4,272,256]{2,1,0:T(8,128)(2,1)}, bf16[4,272,256]{2,1,0:T(8,128)(2,1)S(1)}, u32[]{:S(2)}, u32[]{:S(2)}) collective-permute-start(bf16[4,272,256]{2,1,0:T(8,128)(2,1)} %get-tuple-element.84), channel_id=1, source_target_pairs={{0,1},{1,0},{2,3},{3,2},{4,5},{5,4},{6,7},{7,6},{8,9},{9,8},{10,11... | collective-permute-start | bytes 1671176 | tf_op jit(solution)/shard_map/ppermute | solution.py:46
  547.4 25.6 %collective-permute-start.8 = (bf16[4,272,256]{2,1,0:T(8,128)(2,1)S(1)}, bf16[4,272,256]{2,1,0:T(8,128)(2,1)S(1)}, u32[]{:S(2)}, u32[]{:S(2)}) collective-permute-start(bf16[4,272,256]{2,1,0:T(8,128)(2,1)S(1)} %copy-done.46), channel_id=1, source_target_pairs={{0,2},{1,3},{2,0},{3,1},{4,6},{5,7},{6,4},{7,5},{8,10},{9,11},{10,... | collective-permute-start | bytes 1671176 | tf_op jit(solution)/shard_map/ppermute | solution.py:46
  548.9 25.5 %collective-permute-start.9 = (bf16[4,272,256]{2,1,0:T(8,128)(2,1)S(1)}, bf16[4,272,256]{2,1,0:T(8,128)(2,1)S(1)}, u32[]{:S(2)}, u32[]{:S(2)}) collective-permute-start(bf16[4,272,256]{2,1,0:T(8,128)(2,1)S(1)} %copy-done.45), channel_id=1, source_target_pairs={{0,3},{1,2},{2,1},{3,0},{4,7},{5,6},{6,5},{7,4},{8,11},{9,10},{10,... | collective-permute-start | bytes 1671176 | tf_op jit(solution)/shard_map/ppermute | solution.py:46
  549.4 42.1 %collective-permute-start.16 = (bf16[512,256]{1,0:T(8,128)(2,1)}, bf16[512,256]{1,0:T(8,128)(2,1)S(1)}, u32[]{:S(2)}, u32[]{:S(2)}) collective-permute-start(bf16[512,256]{1,0:T(8,128)(2,1)} %get-tuple-element.97), channel_id=1, source_target_pairs={{0,1},{1,0},{2,3},{3,2},{4,5},{5,4},{6,7},{7,6},{8,9},{9,8},{10,11... | collective-permute-start | bytes 786440 | tf_op jit(solution)/shard_map/ppermute | solution.py:46
  586.1 42.8 %collective-permute-start.10 = (bf16[1024,256]{1,0:T(8,128)(2,1)}, bf16[1024,256]{1,0:T(8,128)(2,1)S(1)}, u32[]{:S(2)}, u32[]{:S(2)}) collective-permute-start(bf16[1024,256]{1,0:T(8,128)(2,1)} %get-tuple-element.88), channel_id=1, source_target_pairs={{0,1},{1,0},{2,3},{3,2},{4,5},{5,4},{6,7},{7,6},{8,9},{9,8},{10,11... | collective-permute-start | bytes 1572872 | tf_op jit(solution)/shard_map/ppermute | solution.py:46
  587.7 41.3 %collective-permute-start.11 = (bf16[1024,256]{1,0:T(8,128)(2,1)}, bf16[1024,256]{1,0:T(8,128)(2,1)S(1)}, u32[]{:S(2)}, u32[]{:S(2)}) collective-permute-start(bf16[1024,256]{1,0:T(8,128)(2,1)} %get-tuple-element.89), channel_id=1, source_target_pairs={{0,2},{1,3},{2,0},{3,1},{4,6},{5,7},{6,4},{7,5},{8,10},{9,11},{10,... | collective-permute-start | bytes 1572872 | tf_op jit(solution)/shard_map/ppermute | solution.py:46
  588.2 40.7 %collective-permute-start.12 = (bf16[1024,256]{1,0:T(8,128)(2,1)}, bf16[1024,256]{1,0:T(8,128)(2,1)S(1)}, u32[]{:S(2)}, u32[]{:S(2)}) collective-permute-start(bf16[1024,256]{1,0:T(8,128)(2,1)} %get-tuple-element.90), channel_id=1, source_target_pairs={{0,3},{1,2},{2,1},{3,0},{4,7},{5,6},{6,5},{7,4},{8,11},{9,10},{10,... | collective-permute-start | bytes 1572872 | tf_op jit(solution)/shard_map/ppermute | solution.py:46
  589.7 33.2 %collective-permute-start.17 = (bf16[512,256]{1,0:T(8,128)(2,1)S(1)}, bf16[512,256]{1,0:T(8,128)(2,1)S(1)}, u32[]{:S(2)}, u32[]{:S(2)}) collective-permute-start(bf16[512,256]{1,0:T(8,128)(2,1)S(1)} %copy-done.53), channel_id=1, source_target_pairs={{0,2},{1,3},{2,0},{3,1},{4,6},{5,7},{6,4},{7,5},{8,10},{9,11},{10,... | collective-permute-start | bytes 786440 | tf_op jit(solution)/shard_map/ppermute | solution.py:46
  591.5 31.4 %collective-permute-start.18 = (bf16[512,256]{1,0:T(8,128)(2,1)S(1)}, bf16[512,256]{1,0:T(8,128)(2,1)S(1)}, u32[]{:S(2)}, u32[]{:S(2)}) collective-permute-start(bf16[512,256]{1,0:T(8,128)(2,1)S(1)} %copy-done.52), channel_id=1, source_target_pairs={{0,3},{1,2},{2,1},{3,0},{4,7},{5,6},{6,5},{7,4},{8,11},{9,10},{10,... | collective-permute-start | bytes 786440 | tf_op jit(solution)/shard_map/ppermute | solution.py:46
  645.8 45.7 %all-to-all-start.4 = ((bf16[8,2,32,1024]{3,2,1,0:T(8,128)(2,1)}), bf16[8,2,32,1024]{3,2,1,0:T(8,128)(2,1)S(1)}, u32[]{:S(2)}, u32[]{:S(2)}) async-start(bf16[8,2,32,1024]{3,2,1,0:T(8,128)(2,1)} %get-tuple-element.100), calls=%async_computation.4 | async-start | bytes 2097152 | tf_op jit(solution)/shard_map/all_to_all | solution.py:430
  650.5 15.6 %collective-permute-start.31 = (bf16[4,272,256]{2,1,0:T(8,128)(2,1)}, bf16[4,272,256]{2,1,0:T(8,128)(2,1)S(1)}, u32[]{:S(2)}, u32[]{:S(2)}) collective-permute-start(bf16[4,272,256]{2,1,0:T(8,128)(2,1)} %get-tuple-element.122), channel_id=1, source_target_pairs={{0,1},{1,0},{2,3},{3,2},{4,5},{5,4},{6,7},{7,6},{8,9},{9,8},{10,11... | collective-permute-start | bytes 1671176 | tf_op jit(solution)/shard_map/ppermute | solution.py:46
  651.1 27.5 %collective-permute-start.32 = (bf16[4,272,256]{2,1,0:T(8,128)(2,1)}, bf16[4,272,256]{2,1,0:T(8,128)(2,1)}, u32[]{:S(2)}, u32[]{:S(2)}) collective-permute-start(bf16[4,272,256]{2,1,0:T(8,128)(2,1)} %get-tuple-element.123), channel_id=1, source_target_pairs={{0,2},{1,3},{2,0},{3,1},{4,6},{5,7},{6,4},{7,5},{8,10},{9,11},{10,... | collective-permute-start | bytes 1671176 | tf_op jit(solution)/shard_map/ppermute | solution.py:46
  651.8 26.8 %collective-permute-start.33 = (bf16[4,272,256]{2,1,0:T(8,128)(2,1)}, bf16[4,272,256]{2,1,0:T(8,128)(2,1)}, u32[]{:S(2)}, u32[]{:S(2)}) collective-permute-start(bf16[4,272,256]{2,1,0:T(8,128)(2,1)} %get-tuple-element.124), channel_id=1, source_target_pairs={{0,3},{1,2},{2,1},{3,0},{4,7},{5,6},{6,5},{7,4},{8,11},{9,10},{10,... | collective-permute-start | bytes 1671176 | tf_op jit(solution)/shard_map/ppermute | solution.py:46
  662.8 35.4 %collective-permute-start.25 = (bf16[4,272,256]{2,1,0:T(8,128)(2,1)}, bf16[4,272,256]{2,1,0:T(8,128)(2,1)S(1)}, u32[]{:S(2)}, u32[]{:S(2)}) collective-permute-start(bf16[4,272,256]{2,1,0:T(8,128)(2,1)} %get-tuple-element.113), channel_id=1, source_target_pairs={{0,1},{1,0},{2,3},{3,2},{4,5},{5,4},{6,7},{7,6},{8,9},{9,8},{10,11... | collective-permute-start | bytes 1671176 | tf_op jit(solution)/shard_map/ppermute | solution.py:46
  663.3 38.5 %collective-permute-start.26 = (bf16[4,272,256]{2,1,0:T(8,128)(2,1)}, bf16[4,272,256]{2,1,0:T(8,128)(2,1)S(1)}, u32[]{:S(2)}, u32[]{:S(2)}) collective-permute-start(bf16[4,272,256]{2,1,0:T(8,128)(2,1)} %get-tuple-element.114), channel_id=1, source_target_pairs={{0,2},{1,3},{2,0},{3,1},{4,6},{5,7},{6,4},{7,5},{8,10},{9,11},{10,... | collective-permute-start | bytes 1671176 | tf_op jit(solution)/shard_map/ppermute | solution.py:46
  666.2 36.0 %collective-permute-start.27 = (bf16[4,272,256]{2,1,0:T(8,128)(2,1)}, bf16[4,272,256]{2,1,0:T(8,128)(2,1)}, u32[]{:S(2)}, u32[]{:S(2)}) collective-permute-start(bf16[4,272,256]{2,1,0:T(8,128)(2,1)} %get-tuple-element.115), channel_id=1, source_target_pairs={{0,3},{1,2},{2,1},{3,0},{4,7},{5,6},{6,5},{7,4},{8,11},{9,10},{10,... | collective-permute-start | bytes 1671176 | tf_op jit(solution)/shard_map/ppermute | solution.py:46
  689.4 26.9 %collective-permute-start.34 = (bf16[1024,256]{1,0:T(8,128)(2,1)}, bf16[1024,256]{1,0:T(8,128)(2,1)S(1)}, u32[]{:S(2)}, u32[]{:S(2)}) collective-permute-start(bf16[1024,256]{1,0:T(8,128)(2,1)} %get-tuple-element.126), channel_id=1, source_target_pairs={{0,1},{1,0},{2,3},{3,2},{4,5},{5,4},{6,7},{7,6},{8,9},{9,8},{10,11... | collective-permute-start | bytes 1572872 | tf_op jit(solution)/shard_map/ppermute | solution.py:46
  691.1 57.2 %collective-permute-start.35 = (bf16[1024,256]{1,0:T(8,128)(2,1)}, bf16[1024,256]{1,0:T(8,128)(2,1)S(1)}, u32[]{:S(2)}, u32[]{:S(2)}) collective-permute-start(bf16[1024,256]{1,0:T(8,128)(2,1)} %get-tuple-element.127), channel_id=1, source_target_pairs={{0,2},{1,3},{2,0},{3,1},{4,6},{5,7},{6,4},{7,5},{8,10},{9,11},{10,... | collective-permute-start | bytes 1572872 | tf_op jit(solution)/shard_map/ppermute | solution.py:46
  698.1 21.1 %collective-permute-start.19 = (bf16[2,272,256]{2,1,0:T(8,128)(2,1)}, bf16[2,272,256]{2,1,0:T(8,128)(2,1)S(1)}, u32[]{:S(2)}, u32[]{:S(2)}) collective-permute-start(bf16[2,272,256]{2,1,0:T(8,128)(2,1)} %get-tuple-element.102), channel_id=1, source_target_pairs={{0,1},{1,0},{2,3},{3,2},{4,5},{5,4},{6,7},{7,6},{8,9},{9,8},{10,11... | collective-permute-start | bytes 835592 | tf_op jit(solution)/shard_map/ppermute | solution.py:46
  701.8 34.2 %collective-permute-start.20 = (bf16[2,272,256]{2,1,0:T(8,128)(2,1)}, bf16[2,272,256]{2,1,0:T(8,128)(2,1)S(1)}, u32[]{:S(2)}, u32[]{:S(2)}) collective-permute-start(bf16[2,272,256]{2,1,0:T(8,128)(2,1)} %get-tuple-element.103), channel_id=1, source_target_pairs={{0,2},{1,3},{2,0},{3,1},{4,6},{5,7},{6,4},{7,5},{8,10},{9,11},{10,... | collective-permute-start | bytes 835592 | tf_op jit(solution)/shard_map/ppermute | solution.py:46
  702.6 34.1 %collective-permute-start.21 = (bf16[2,272,256]{2,1,0:T(8,128)(2,1)}, bf16[2,272,256]{2,1,0:T(8,128)(2,1)S(1)}, u32[]{:S(2)}, u32[]{:S(2)}) collective-permute-start(bf16[2,272,256]{2,1,0:T(8,128)(2,1)} %get-tuple-element.104), channel_id=1, source_target_pairs={{0,3},{1,2},{2,1},{3,0},{4,7},{5,6},{6,5},{7,4},{8,11},{9,10},{10,... | collective-permute-start | bytes 835592 | tf_op jit(solution)/shard_map/ppermute | solution.py:46
  716.3 32.4 %collective-permute-start.36 = (bf16[1024,256]{1,0:T(8,128)(2,1)}, bf16[1024,256]{1,0:T(8,128)(2,1)S(1)}, u32[]{:S(2)}, u32[]{:S(2)}) collective-permute-start(bf16[1024,256]{1,0:T(8,128)(2,1)} %get-tuple-element.128), channel_id=1, source_target_pairs={{0,3},{1,2},{2,1},{3,0},{4,7},{5,6},{6,5},{7,4},{8,11},{9,10},{10,... | collective-permute-start | bytes 1572872 | tf_op jit(solution)/shard_map/ppermute | solution.py:46
  720.0 29.0 %collective-permute-start.28 = (bf16[1024,256]{1,0:T(8,128)(2,1)}, bf16[1024,256]{1,0:T(8,128)(2,1)S(1)}, u32[]{:S(2)}, u32[]{:S(2)}) collective-permute-start(bf16[1024,256]{1,0:T(8,128)(2,1)} %get-tuple-element.117), channel_id=1, source_target_pairs={{0,1},{1,0},{2,3},{3,2},{4,5},{5,4},{6,7},{7,6},{8,9},{9,8},{10,11... | collective-permute-start | bytes 1572872 | tf_op jit(solution)/shard_map/ppermute | solution.py:46
  736.7 26.2 %collective-permute-start.29 = (bf16[1024,256]{1,0:T(8,128)(2,1)}, bf16[1024,256]{1,0:T(8,128)(2,1)S(1)}, u32[]{:S(2)}, u32[]{:S(2)}) collective-permute-start(bf16[1024,256]{1,0:T(8,128)(2,1)} %get-tuple-element.118), channel_id=1, source_target_pairs={{0,2},{1,3},{2,0},{3,1},{4,6},{5,7},{6,4},{7,5},{8,10},{9,11},{10,... | collective-permute-start | bytes 1572872 | tf_op jit(solution)/shard_map/ppermute | solution.py:46
  737.4 25.5 %collective-permute-start.30 = (bf16[1024,256]{1,0:T(8,128)(2,1)}, bf16[1024,256]{1,0:T(8,128)(2,1)S(1)}, u32[]{:S(2)}, u32[]{:S(2)}) collective-permute-start(bf16[1024,256]{1,0:T(8,128)(2,1)} %get-tuple-element.119), channel_id=1, source_target_pairs={{0,3},{1,2},{2,1},{3,0},{4,7},{5,6},{6,5},{7,4},{8,11},{9,10},{10,... | collective-permute-start | bytes 1572872 | tf_op jit(solution)/shard_map/ppermute | solution.py:46
  748.3 22.6 %collective-permute-start.22 = (bf16[512,256]{1,0:T(8,128)(2,1)}, bf16[512,256]{1,0:T(8,128)(2,1)S(1)}, u32[]{:S(2)}, u32[]{:S(2)}) collective-permute-start(bf16[512,256]{1,0:T(8,128)(2,1)} %get-tuple-element.106), channel_id=1, source_target_pairs={{0,1},{1,0},{2,3},{3,2},{4,5},{5,4},{6,7},{7,6},{8,9},{9,8},{10,11... | collective-permute-start | bytes 786440 | tf_op jit(solution)/shard_map/ppermute | solution.py:46
  748.7 24.5 %collective-permute-start.23 = (bf16[512,256]{1,0:T(8,128)(2,1)}, bf16[512,256]{1,0:T(8,128)(2,1)S(1)}, u32[]{:S(2)}, u32[]{:S(2)}) collective-permute-start(bf16[512,256]{1,0:T(8,128)(2,1)} %get-tuple-element.107), channel_id=1, source_target_pairs={{0,2},{1,3},{2,0},{3,1},{4,6},{5,7},{6,4},{7,5},{8,10},{9,11},{10,... | collective-permute-start | bytes 786440 | tf_op jit(solution)/shard_map/ppermute | solution.py:46
  749.0 24.2 %collective-permute-start.24 = (bf16[512,256]{1,0:T(8,128)(2,1)}, bf16[512,256]{1,0:T(8,128)(2,1)}, u32[]{:S(2)}, u32[]{:S(2)}) collective-permute-start(bf16[512,256]{1,0:T(8,128)(2,1)} %get-tuple-element.108), channel_id=1, source_target_pairs={{0,3},{1,2},{2,1},{3,0},{4,7},{5,6},{6,5},{7,4},{8,11},{9,10},{10,... | collective-permute-start | bytes 786440 | tf_op jit(solution)/shard_map/ppermute | solution.py:46
  (48 other events, 587.9 us)

commit v3 on v2

--- a/solution.py
+++ b/solution.py
@@ -15,7 +15,7 @@
 BF = jnp.bfloat16
 F32 = jnp.float32
 
-RETURN_SPLIT = (2, 4, 4, 4, 2)
+RETURN_SPLIT = (4, 4, 5, 3)
 
 
 def cost(flops, moved, exps=0):
@@ -47,6 +47,8 @@
 
 
 def exchange(pieces, name, size):
+    if len(pieces) != size:
+        return [lax.all_to_all(pieces[0], name, split_axis=0, concat_axis=0, tiled=True)]
     order = sorted(range(1, size), key=lambda d: -d)
     got = {d: swap(pieces[d], name, size, d) for d in order}
     return [pieces[0]] + [got[d] for d in range(1, size)]
@@ -146,7 +148,12 @@
     return iota((rows, cols), 0) == iota((rows, cols), 1) + first
 
 
-def mix_kernel(groups, pieces, tok, scale, gain, gain_two, back, up, mixed_out, *outs):
+def places(refs, groups, me):
+    return refs if len(refs) == groups else [refs[0].at[me[0] ^ d] for d in range(groups)]
+
+
+def mix_kernel(groups, me, pieces, tok, scale, gain, gain_two, back, up, mixed_out, *outs):
+    outs = places(outs, groups, me)
     block, chans = tok.shape
     conv = dot(back[...], pieces[...].reshape(block, chans))
     wide = tok[...].astype(F32)
@@ -169,7 +176,22 @@
         outs[d][0, block:] = tail.astype(BF)
 
 
-def mix(home, tokens, scale, gain, gain_two, back, up, row, groups):
+def fan(shape, index, groups, stacked):
+    if stacked:
+        return [pl.BlockSpec((groups,) + shape, lambda t: (0,) + index(t))]
+    return [pl.BlockSpec(shape, index) for _ in range(groups)]
+
+
+def fan_out(shape, groups, stacked):
+    if stacked:
+        return [jax.ShapeDtypeStruct((groups,) + shape, BF)]
+    return [jax.ShapeDtypeStruct(shape, BF) for _ in range(groups)]
+
+
+SCALAR = pl.BlockSpec(memory_space=pltpu.SMEM)
+
+
+def mix(me, home, tokens, scale, gain, gain_two, back, up, row, groups, stacked):
     parts, size, ql, chans = home.shape
     block = ql * parts
     count = size * block
@@ -178,6 +200,7 @@
         lambda *refs: mix_kernel(groups, *refs),
         grid=(size,),
         in_specs=[
+            SCALAR,
             pl.BlockSpec((parts, 1, ql, chans), lambda r: (0, r, 0, 0)),
             pl.BlockSpec((block, chans), lambda r: (r + row, 0)),
             pl.BlockSpec((block, 1), lambda r: (r + row, 0)),
@@ -187,18 +210,17 @@
             whole(up.shape),
         ],
         out_specs=[pl.BlockSpec((block, chans), lambda r: (r, 0))]
-        + [pl.BlockSpec((1, block + TAIL, width), lambda r: (r, 0, 0)) for _ in range(groups)],
+        + fan((1, block + TAIL, width), lambda r: (r, 0, 0), groups, stacked),
         out_shape=[jax.ShapeDtypeStruct((count, chans), F32)]
-        + [jax.ShapeDtypeStruct((size, block + TAIL, width), BF) for _ in range(groups)],
+        + fan_out((size, block + TAIL, width), groups, stacked),
         cost_estimate=cost(2 * count * chans * (block + up.shape[1]), 10 * count * chans, count * chans),
         name="mix_tokens",
-    )(home, tokens, scale, gain, gain_two, back, up)
-
-
-def hidden_kernel(groups, total, halves, *refs):
-    pieces = refs[:groups]
-    up, down = refs[groups : groups + 2]
-    outs = refs[groups + 2 :]
+    )(me, home, tokens, scale, gain, gain_two, back, up)
+
+
+def hidden_kernel(groups, total, halves, me, up, down, *refs):
+    pieces = places(refs[: len(refs) // 2], groups, me)
+    outs = places(refs[len(refs) // 2 :], groups, me)
     width = pieces[0].shape[2]
     block = pieces[0].shape[1] - TAIL
     tail = sum(p[0, block:].astype(F32) for p in pieces)
@@ -222,39 +244,38 @@
             outs[d][:, h * step : (h + 1) * step] = reduced[:, d * step : (d + 1) * step]
 
 
-def hidden(pieces, up, down, total, halves):
-    groups = len(pieces)
-    size, tall, width = pieces[0].shape
+def hidden(me, pieces, up, down, total, halves, groups):
+    stacked = len(pieces) != groups
+    size, tall, width = pieces[0].shape[-3:]
     block = tall - TAIL
     count = size * block
     step = down.shape[1] // groups
     return pl.pallas_call(
         lambda *refs: hidden_kernel(groups, total, halves, *refs),
         grid=(size,),
-        in_specs=[pl.BlockSpec((1, tall, width), lambda t: (t, 0, 0)) for _ in range(groups)]
-        + [whole(up.shape), whole(down.shape)],
-        out_specs=[pl.BlockSpec((block, step), lambda t: (t, 0)) for _ in range(groups)],
-        out_shape=[jax.ShapeDtypeStruct((count, step), BF) for _ in range(groups)],
+        in_specs=[SCALAR, whole(up.shape), whole(down.shape)]
+        + fan((1, tall, width), lambda t: (t, 0, 0), groups, stacked),
+        out_specs=fan((block, step), lambda t: (t, 0), groups, stacked),
+        out_shape=fan_out((count, step), groups, stacked),
         cost_estimate=cost(
             2 * count * up.shape[1] * (up.shape[0] + down.shape[1]) // halves,
             2 * groups * count * (width + step),
             count * up.shape[1],
         ),
         name="hidden_units",
-    )(*pieces, up, down)
-
-
-def final_kernel(groups, *refs):
-    pieces = refs[:groups]
-    mixed, left = refs[groups : groups + 2]
+    )(me, up, down, *pieces)
+
+
+def final_kernel(groups, me, mixed, left, *refs):
+    pieces = places(refs[: 1 if len(refs) < groups else groups], groups, me)
     out = refs[-1]
     x = jnp.concatenate([p[...] for p in pieces], axis=1)
     out[...] = (mixed[...] + dot(x, left[...])).astype(BF)
 
 
-def final(pieces, mixed, left, row, count_all, carried):
-    groups = len(pieces)
-    count, step = pieces[0].shape
+def final(me, pieces, mixed, left, row, count_all, carried, groups):
+    stacked = len(pieces) != groups
+    count, step = pieces[0].shape[-2:]
     chans = mixed.shape[1]
     tb = min(ROWS, count)
     first = row // tb
@@ -262,15 +283,15 @@
     return pl.pallas_call(
         lambda *refs: final_kernel(groups, *refs),
         grid=(count // tb,),
-        in_specs=[pl.BlockSpec((tb, step), lambda t: (t, 0)) for _ in range(groups)]
-        + [pl.BlockSpec((tb, chans), lambda t: (t, 0)), whole(left.shape)]
+        in_specs=[SCALAR, pl.BlockSpec((tb, chans), lambda t: (t, 0)), whole(left.shape)]
+        + fan((tb, step), lambda t: (t, 0), groups, stacked)
         + [pl.BlockSpec(memory_space=pl.ANY) for _ in extra],
         out_specs=pl.BlockSpec((tb, chans), lambda t: (t + first, 0)),
         out_shape=jax.ShapeDtypeStruct((count_all, chans), BF),
-        input_output_aliases={groups + 2: 0} if extra else {},
+        input_output_aliases={3 + len(pieces): 0} if extra else {},
         cost_estimate=cost(2 * count * groups * step * chans, 8 * count * chans),
         name="block_out",
-    )(*pieces, mixed, left, *extra)
+    )(me, mixed, left, *pieces, *extra)
 
 
 def iota(shape, axis):
@@ -406,40 +427,57 @@
         kern = after(kern, up_one, up_two, down_one, down_two, turn)
         backed = outer(pieces, kern, fwd, back, turn, sizes)
         chunks = len(sizes)
+        place = me.astype(jnp.int32).reshape(1)
         starts = [sum(sizes[:j]) for j in range(chunks)]
-        mixed, ups, downs, done = {}, {}, {}, {}
-        out = None
+        mixed, ups, downs, done, outs = {}, {}, {}, {}, {-1: None}
 
         def hide(j):
-            downs[j] = hidden(ups[j], up_two, down_one, total, halves)
-            done[j] = downs[j][0]
-            downs[j] = exchange(downs[j], "hid", groups)
-
-        def finish(j, out):
-            return final(downs[j], mixed[j], down_two, starts[j] * block, count, out)
+            pieces = ups[j]
+            if 1 <= j < chunks - 1:
+                pieces = after(pieces, mixed[j + 1])
+            if j >= 1:
+                pieces = after(pieces, downs[j - 1])
+            pieces = hidden(place, pieces, up_two, down_one, total, halves, groups)
+            done[j] = pieces
+            downs[j] = exchange(pieces, "hid", groups)
+
+        def finish(j):
+            outs[j] = final(
+                place, downs[j], mixed[j], down_two, starts[j] * block, count, outs[j - 1], groups
+            )
 
         for j in range(chunks):
             needed = []
             if j >= 2:
-                needed.append(mixed[j - 2])
+                needed.append(ups[j - 2])
             if j >= 3:
                 needed.append(done[j - 3])
             if j >= 4:
-                needed.append(out)
+                needed.append(outs[j - 4])
             sent = after(backed[j], *needed) if needed else backed[j]
             home = lax.all_to_all(sent, "ctx", split_axis=0, concat_axis=0, tiled=True)
             mixed[j], *pieces = mix(
-                home, tok, scale, gain, gain_two, inv_inner, up_one, starts[j], groups
+                place,
+                home,
+                tok,
+                scale,
+                gain,
+                gain_two,
+                inv_inner,
+                up_one,
+                starts[j],
+                groups,
+                j == chunks - 1,
             )
             ups[j] = exchange(pieces, "hid", groups)
             if j >= 1:
                 hide(j - 1)
             if j >= 2:
-                out = finish(j - 2, out)
+                finish(j - 2)
         hide(chunks - 1)
         for j in range(max(chunks - 2, 0), chunks):
-            out = finish(j, out)
-        return out.reshape(1, count, chans)
+            finish(j)
+        return outs[chunks - 1].reshape(1, count, chans)
 
     return shards
 

time: 786 us -> 749 us (0.953)
  waiting for transfers between devices: 394 us -> 365 us
  blocking collectives: 90.2 us -> 113 us
  Pallas kernels: 167 us -> 157 us
  starting transfers between devices: 67.7 us -> 59.4 us
    all_to_all x4 -> x3, waiting for transfers between devices: 58.6 us -> 34 us  [shards(): home = lax.all_to_all(sent, 'ctx', split_axis=0, concat_axis=0, tiled=True)]
    all_to_all x1, blocking collectives: 73.7 us -> 96.2 us  [shards(): home = lax.all_to_all(sent, 'ctx', split_axis=0, concat_axis=0, tiled=True)]
    ppermute x37 -> x25, starting transfers between devices: 44.9 us -> 33.5 us  [swap(): return lax.ppermute(x, name, [(i, i ^ d) for i in range(size)])]
    unnamed x116 -> x80, local copies, waits for them, and re-layouts: 23.1 us -> 15.8 us
    all_to_all x4 -> x3, starting transfers between devices: 16.3 us -> 11.8 us  [shards(): home = lax.all_to_all(sent, 'ctx', split_axis=0, concat_axis=0, tiled=True)]
    ppermute x37 -> x25, waiting for transfers between devices: 316 us -> 312 us  [swap(): return lax.ppermute(x, name, [(i, i ^ d) for i in range(size)])]
    pallas_call x5 -> x4, Pallas kernels: 47.8 us -> 43.7 us  [hidden(): pl.pallas_call(lambda *refs: hidden_kernel(groups, total, halves, *refs),...]
    pallas_call x5 -> x4, Pallas kernels: 37.5 us -> 34.7 us  [mix(): pl.pallas_call(lambda *refs: mix_kernel(groups, *refs), grid=(size,), in_...]
  transfers between devices with their start and end apart: 42 -> 31, of which waited for: 20 -> 20; matrix products, arithmetic and copies ran while one was open for 5% -> 5% of each run, Pallas kernels for 18% -> 16%
where the time goes in v3:
time: 749 us; the launch traced here: 747 us
  waiting for transfers between devices  365 us (49%)
  Pallas kernels  157 us (21%)
  blocking collectives  113 us (15%)
  starting transfers between devices  59.4 us (8%)
  local copies, waits for them, and re-layouts  24.9 us (3%)
  other arithmetic  13.9 us (2%)
  matrix products  13.6 us (2%)
    ppermute x25, waiting for transfers between devices, swap(): return lax.ppermute(x, name, [(i, i ^ d) for i in range(size)])  312 us
    all_to_all x1, blocking collectives, shards(): home = lax.all_to_all(sent, 'ctx', split_axis=0, concat_axis=0, tiled=True)  96.2 us
    pallas_call x4, Pallas kernels, hidden(): pl.pallas_call(lambda *refs: hidden_kernel(groups, total, halves, *refs),...  43.7 us
    pallas_call x4, Pallas kernels, mix(): pl.pallas_call(lambda *refs: mix_kernel(groups, *refs), grid=(size,), in_...  34.7 us
    all_to_all x3, waiting for transfers between devices, shards(): home = lax.all_to_all(sent, 'ctx', split_axis=0, concat_axis=0, tiled=True)  34 us
    ppermute x25, starting transfers between devices, swap(): return lax.ppermute(x, name, [(i, i ^ d) for i in range(size)])  33.5 us
    pallas_call x4, Pallas kernels, final(): pl.pallas_call(lambda *refs: final_kernel(groups, *refs), grid=(count //...  28 us
    pallas_call x1, Pallas kernels, inner(): pl.pallas_call(lambda *refs: inner_kernel(parts, *refs), grid=(chans // c...  26.3 us
  transfers between devices with their start and end apart: 31, of which 20 were waited for; matrix products, arithmetic and copies ran while one was open for 5% of the time, Pallas kernels for 16%

profile of v3, /device:TPU:0, one launch (start us, length us, event | category | flops | bytes accessed | tf_op | source)
XLA Modules:
  0.0 747.3 jit_solution(11326309580858822442)
XLA Ops:
  0.0 11.5 %copy.23 = bf16[16,256,1024]{2,0,1:T(8,128)(2,1)} copy(bf16[16,256,1024]{2,1,0:T(8,128)(2,1)} %param.21) | data formatting | bytes 16777216 | tf_op args[7]
  11.5 6.3 all-to-all-start
  17.9 5.1 multiply_reduce_fusion
  23.0 16.3 %psum.7 = f32[4096]{0:T(1024)S(1)} all-reduce(f32[4096]{0:T(1024)S(1)} %multiply_reduce_fusion), channel_id=1, replica_groups=mesh['ctx'=8,'hid'=4] {'hid'}, use_global_device_ids=true, to_apply=%region_1.0 | all-reduce | flops 4096 | bytes 32768 | tf_op jit(solution)/shard_map/psum | solution.py:403
  44.2 26.3 %inner_mix.1 = (bf16[32,16,1024]{2,1,0:T(8,128)(2,1)}, bf16[32,16,1024]{2,1,0:T(8,128)(2,1)}, bf16[32,16,1024]{2,1,0:T(8,128)(2,1)}, bf16[32,16,1024]{2,1,0:T(8,...) custom-call(bf16[4096,1024]{1,0:T(8,128)(2,1)} %bitcast.52, ...), custom_call_target="tpu_custom_call" | custom-call | flops 2147483648 | bytes 16777216 | tf_op jit(solution)/shard_map/inner_mix/pallas_call | solution.py:77
  72.6 2.6 collective-permute-start.3
  77.8 3.1 fusion.40
  81.0 3.7 fusion.9.refs_2_
  85.3 5.1 fusion.8.refs_1_
  96.1 3.1 fusion.31.refs_7_
  99.2 3.5 collective-permute-start.5
  102.7 73.9 %collective-permute-done.1.refs_2_ = bf16[32,16,1024]{2,1,0:T(8,128)(2,1)S(1)} collective-permute-done((bf16[32,16,1024]{2,1,0:T(8,128)(2,1)}, bf16[32,16,1024]{2,1,0:T(8,128)(2,1)S(1)}, u32[]{:S(2)}, u32[]{:S(2)}) %collective-permute-start.1) | collective-permute-done | bytes 1048608 | tf_op jit(solution)/shard_map/ppermute | solution.py:46
  176.6 2.6 collective-permute-start.6
  179.2 3.7 select_convert_fusion.refs_2_
  182.9 19.4 %all-to-all-done.refs_8_ = bf16[8,32,16,1024]{3,2,1,0:T(8,128)(2,1)} async-done(((bf16[8,32,16,1024]{3,2,1,0:T(8,128)(2,1)}), bf16[8,32,16,1024]{3,2,1,0:T(8,128)(2,1)}, u32[]{:S(2)}, u32[]{:S(2)}) %all-to-all-start) | async-done | bytes 8388640 | tf_op jit(solution)/shard_map/all_to_all | solution.py:400
  202.3 112.3 %collective-permute-done.3.refs_4_ = bf16[32,16,1024]{2,1,0:T(8,128)(2,1)} collective-permute-done((bf16[32,16,1024]{2,1,0:T(8,128)(2,1)}, bf16[32,16,1024]{2,1,0:T(8,128)(2,1)}, u32[]{:S(2)}, u32[]{:S(2)}) %collective-permute-start.3) | collective-permute-done | bytes 1048608 | tf_op jit(solution)/shard_map/ppermute | solution.py:46
  314.7 21.5 %collective-permute-done.4.refs_5_ = bf16[32,16,1024]{2,1,0:T(8,128)(2,1)} collective-permute-done((bf16[32,16,1024]{2,1,0:T(8,128)(2,1)}, bf16[32,16,1024]{2,1,0:T(8,128)(2,1)}, u32[]{:S(2)}, u32[]{:S(2)}) %collective-permute-start.4) | collective-permute-done | bytes 1048608 | tf_op jit(solution)/shard_map/ppermute | solution.py:46
  336.2 24.8 %outer_mix.1 = (bf16[8,4,32,1024]{3,2,1,0:T(8,128)(2,1)}, bf16[8,4,32,1024]{3,2,1,0:T(8,128)(2,1)}, bf16[8,5,32,1024]{3,2,1,0:T(8,128)(2,1)}, bf16[8,3,32,1024]{3,2,1,0:T(8,128)(2,1)}) custom-call(bf16[32,16,1024]{2,1,0:T(8,128)(2,1)} %get-tuple-element.66.refs_0_, bf16[32,16,1024]{2,1,0:T(8,128)(2,1)} %copy-done.7, bf16[32,16,1024]{2,1,0:T(8,128)(2,1)} %copy-done.8, ...), custom_call_target="tpu_custom_call" | custom-call | flops 4294967296 | bytes 25165824 | tf_op jit(solution)/shard_map/outer_mix/pallas_call | solution.py:129
  361.1 96.2 %all_to_all.35.refs_1_ = bf16[8,4,32,1024]{3,2,1,0:T(8,128)(2,1)} all-to-all(bf16[8,4,32,1024]{3,2,1,0:T(8,128)(2,1)} %get-tuple-element.81), channel_id=1, replica_groups=mesh['ctx'=8,'hid'=4] {'ctx'}, dimensions={0} | all-to-all | bytes 4194304 | tf_op jit(solution)/shard_map/all_to_all | solution.py:458
  457.3 3.6 all-to-all-start.1
  460.9 8.7 %mix_tokens.5 = (f32[1024,1024]{1,0:T(8,128)}, bf16[4,272,256]{2,1,0:T(8,128)(2,1)}, bf16[4,272,256]{2,1,0:T(8,128)(2,1)}, bf16[4,272,256]{2,1,0:T(8,128)(2,1)}, bf16[4,272,256]{2,1,0:T(8,128)(2,1)}) custom-call(s32[1]{0:T(128)} %bitcast.refs_0_, bf16[8,4,32,1024]{3,2,1,0:T(8,128)(2,1)} %all_to_all.35.refs_1_, bf16[4096,1024]{1,0:T(8,128)(2,1)} %bitcast.53, ...), custom_call_target="tpu_custom_call" | custom-call | flops 2684354560 | bytes 10485760 | tf_op jit(solution)/shard_map/mix_tokens/pallas_call | solution.py:199
  473.1 12.2 %collective-permute-done.10.refs_4_ = bf16[4,272,256]{2,1,0:T(8,128)(2,1)S(1)} collective-permute-done((bf16[4,272,256]{2,1,0:T(8,128)(2,1)}, bf16[4,272,256]{2,1,0:T(8,128)(2,1)S(1)}, u32[]{:S(2)}, u32[]{:S(2)}) %collective-permute-start.10) | collective-permute-done | bytes 557088 | tf_op jit(solution)/shard_map/ppermute | solution.py:46
  485.3 12.6 %collective-permute-done.11.refs_5_ = bf16[4,272,256]{2,1,0:T(8,128)(2,1)S(1)} collective-permute-done((bf16[4,272,256]{2,1,0:T(8,128)(2,1)}, bf16[4,272,256]{2,1,0:T(8,128)(2,1)S(1)}, u32[]{:S(2)}, u32[]{:S(2)}) %collective-permute-start.11) | collective-permute-done | bytes 557088 | tf_op jit(solution)/shard_map/ppermute | solution.py:46
  498.9 11.0 %all-to-all-done.1.refs_1_ = bf16[8,4,32,1024]{3,2,1,0:T(8,128)(2,1)S(1)} async-done(((bf16[8,4,32,1024]{3,2,1,0:T(8,128)(2,1)}), bf16[8,4,32,1024]{3,2,1,0:T(8,128)(2,1)S(1)}, u32[]{:S(2)}, u32[]{:S(2)}) %all-to-all-start.1) | async-done | bytes 2097184 | tf_op jit(solution)/shard_map/all_to_all | solution.py:458
  511.2 3.6 all-to-all-start.5
  514.8 8.8 %mix_tokens.4 = (f32[1024,1024]{1,0:T(8,128)}, bf16[4,272,256]{2,1,0:T(8,128)(2,1)}, bf16[4,272,256]{2,1,0:T(8,128)(2,1)}, bf16[4,272,256]{2,1,0:T(8,128)(2,1)}, bf16[4,272,256]{2,1,0:T(8,128)(2,1)}) custom-call(s32[1]{0:T(128)} %bitcast.refs_0_, bf16[8,4,32,1024]{3,2,1,0:T(8,128)(2,1)} %copy-done.3, bf16[4096,1024]{1,0:T(8,128)(2,1)} %bitcast.54, ...), custom_call_target="tpu_custom_call" | custom-call | flops 2684354560 | bytes 10485760 | tf_op jit(solution)/shard_map/mix_tokens/pallas_call | solution.py:199
  527.2 10.8 %hidden_units.4 = (bf16[1024,256]{1,0:T(8,128)(2,1)}, bf16[1024,256]{1,0:T(8,128)(2,1)}, bf16[1024,256]{1,0:T(8,128)(2,1)}, bf16[1024,256]{1,0:T(8,128)(2,1)}) custom-call(s32[1]{0:T(128)} %bitcast.refs_0_, bf16[1024,2048]{1,0:T(8,128)(2,1)} %fusion.8.refs_1_, bf16[2048,1024]{1,0:T(8,128)(2,1)} %fusion.9.refs_2_, ...), custom_call_target="tpu_custom_call" | custom-call | flops 4294967296 | bytes 4194304 | tf_op jit(solution)/shard_map/hidden_units/pallas_call | solution.py:253
  539.3 12.7 %collective-permute-done.8.refs_5_ = bf16[4,272,256]{2,1,0:T(8,128)(2,1)} collective-permute-done((bf16[4,272,256]{2,1,0:T(8,128)(2,1)}, bf16[4,272,256]{2,1,0:T(8,128)(2,1)}, u32[]{:S(2)}, u32[]{:S(2)}) %collective-permute-start.8) | collective-permute-done | bytes 557088 | tf_op jit(solution)/shard_map/ppermute | solution.py:46
  552.0 23.0 %all-to-all-done.5.refs_1_ = bf16[8,5,32,1024]{3,2,1,0:T(8,128)(2,1)S(1)} async-done(((bf16[8,5,32,1024]{3,2,1,0:T(8,128)(2,1)}), bf16[8,5,32,1024]{3,2,1,0:T(8,128)(2,1)S(1)}, u32[]{:S(2)}, u32[]{:S(2)}) %all-to-all-start.5) | async-done | bytes 2621472 | tf_op jit(solution)/shard_map/all_to_all | solution.py:458
  575.0 4.6 all-to-all-start.3
  583.2 10.3 %mix_tokens.7 = (f32[1280,1024]{1,0:T(8,128)}, bf16[5,272,256]{2,1,0:T(8,128)(2,1)}, bf16[5,272,256]{2,1,0:T(8,128)(2,1)}, bf16[5,272,256]{2,1,0:T(8,128)(2,1)}, bf16[5,272,256]{2,1,0:T(8,128)(2,1)}) custom-call(s32[1]{0:T(128)} %bitcast.refs_0_, bf16[8,5,32,1024]{3,2,1,0:T(8,128)(2,1)} %copy-done.2, bf16[4096,1024]{1,0:T(8,128)(2,1)} %bitcast.55, ...), custom_call_target="tpu_custom_call" | custom-call | flops 3355443200 | bytes 13107200 | tf_op jit(solution)/shard_map/mix_tokens/pallas_call | solution.py:199
  597.1 9.3 %collective-permute-done.17.refs_5_ = bf16[1024,256]{1,0:T(8,128)(2,1)} collective-permute-done((bf16[1024,256]{1,0:T(8,128)(2,1)}, bf16[1024,256]{1,0:T(8,128)(2,1)}, u32[]{:S(2)}, u32[]{:S(2)}) %collective-permute-start.17) | collective-permute-done | bytes 524320 | tf_op jit(solution)/shard_map/ppermute | solution.py:46
  607.0 10.8 %hidden_units.5 = (bf16[1024,256]{1,0:T(8,128)(2,1)}, bf16[1024,256]{1,0:T(8,128)(2,1)}, bf16[1024,256]{1,0:T(8,128)(2,1)}, bf16[1024,256]{1,0:T(8,128)(2,1)}) custom-call(s32[1]{0:T(128)} %bitcast.refs_0_, bf16[1024,2048]{1,0:T(8,128)(2,1)} %fusion.8.refs_1_, bf16[2048,1024]{1,0:T(8,128)(2,1)} %fusion.9.refs_2_, ...), custom_call_target="tpu_custom_call" | custom-call | flops 4294967296 | bytes 4194304 | tf_op jit(solution)/shard_map/hidden_units/pallas_call | solution.py:253
  620.9 2.4 collective-permute-start.21
  623.3 6.9 mix_tokens.6
  630.2 3.6 all-to-all-start.4
  633.8 2.5 collective-permute-done.14.refs_5_
  636.9 10.2 %collective-permute-done.19.refs_4_ = bf16[1024,256]{1,0:T(8,128)(2,1)S(1)} collective-permute-done((bf16[1024,256]{1,0:T(8,128)(2,1)}, bf16[1024,256]{1,0:T(8,128)(2,1)S(1)}, u32[]{:S(2)}, u32[]{:S(2)}) %collective-permute-start.19) | collective-permute-done | bytes 524320 | tf_op jit(solution)/shard_map/ppermute | solution.py:46
  647.1 20.7 %collective-permute-done.20.refs_5_ = bf16[1024,256]{1,0:T(8,128)(2,1)S(1)} collective-permute-done((bf16[1024,256]{1,0:T(8,128)(2,1)}, bf16[1024,256]{1,0:T(8,128)(2,1)S(1)}, u32[]{:S(2)}, u32[]{:S(2)}) %collective-permute-start.20) | collective-permute-done | bytes 524320 | tf_op jit(solution)/shard_map/ppermute | solution.py:46
  667.7 12.7 %hidden_units.6 = (bf16[1280,256]{1,0:T(8,128)(2,1)}, bf16[1280,256]{1,0:T(8,128)(2,1)}, bf16[1280,256]{1,0:T(8,128)(2,1)}, bf16[1280,256]{1,0:T(8,128)(2,1)}) custom-call(s32[1]{0:T(128)} %bitcast.refs_0_, bf16[1024,2048]{1,0:T(8,128)(2,1)} %fusion.8.refs_1_, bf16[2048,1024]{1,0:T(8,128)(2,1)} %fusion.9.refs_2_, ...), custom_call_target="tpu_custom_call" | custom-call | flops 5368709120 | bytes 5242880 | tf_op jit(solution)/shard_map/hidden_units/pallas_call | solution.py:253
  684.4 12.1 %collective-permute-done.22.refs_4_ = bf16[1280,256]{1,0:T(8,128)(2,1)S(1)} collective-permute-done((bf16[1280,256]{1,0:T(8,128)(2,1)}, bf16[1280,256]{1,0:T(8,128)(2,1)S(1)}, u32[]{:S(2)}, u32[]{:S(2)}) %collective-permute-start.22) | collective-permute-done | bytes 655392 | tf_op jit(solution)/shard_map/ppermute | solution.py:46
  696.5 7.2 collective-permute-done.23.refs_5_
  704.6 9.3 %hidden_units.7 = bf16[4,768,256]{2,1,0:T(8,128)(2,1)} custom-call(s32[1]{0:T(128)} %bitcast.refs_0_, bf16[1024,2048]{1,0:T(8,128)(2,1)} %fusion.8.refs_1_, bf16[2048,1024]{1,0:T(8,128)(2,1)} %fusion.9.refs_2_, bf16[4,3,272,256]{3,2,1,0:T(8,128)(2,1)} %copy-done.6), custom_call_target="tpu_custom_call" | custom-call | flops 3221225472 | bytes 3145728 | tf_op jit(solution)/shard_map/hidden_units/pallas_call | solution.py:253
  714.0 4.2 all-to-all-start.6
  718.1 6.9 block_out.4.refs_7_
  725.0 6.9 block_out.5.refs_7_
  731.9 8.3 %block_out.6.refs_4_ = bf16[4096,1024]{1,0:T(8,128)(2,1)} custom-call(s32[1]{0:T(128)} %bitcast.refs_0_, f32[1280,1024]{1,0:T(8,128)} %get-tuple-element.103.refs_1_, bf16[1024,1024]{1,0:T(8,128)(2,1)} %select_convert_fusion.refs_2_, bf16[1280,256]{1,0:T(8,128)(2,1)} %get-tuple-element.120.refs_3_, ...), custom_call_target="tpu_custom_call", output_to_operand_aliasing={{}: (7, {})} | custom-call | flops 2684354560 | bytes 10485760 | tf_op jit(solution)/shard_map/block_out/pallas_call | solution.py:283
  741.4 5.9 block_out.7
  (145 shorter events, 43.9 us)
Async XLA Ops:
  0.0 80.9 %copy-start = (bf16[16,128,64]{1,2,0:T(8,128)(2,1)S(1)}, bf16[16,128,64]{1,2,0:T(8,128)(2,1)}, u32[]{:S(2)}) copy-start(bf16[16,128,64]{1,2,0:T(8,128)(2,1)} %param.26) | copy-start | bytes 786436
  11.5 190.8 %all-to-all-start = ((bf16[8,32,16,1024]{3,2,1,0:T(8,128)(2,1)}), bf16[8,32,16,1024]{3,2,1,0:T(8,128)(2,1)}, u32[]{:S(2)}, u32[]{:S(2)}) async-start(bf16[8,32,16,1024]{3,2,1,0:T(8,128)(2,1)} %bitcast.57), calls=%async_computation | async-start | bytes 16777216 | tf_op jit(solution)/shard_map/all_to_all | solution.py:400
  17.9 23.4 %copy-start.16 = (f32[16,256]{1,0:T(8,128)S(1)}, f32[16,256]{1,0:T(8,128)}, u32[]{:S(2)}) copy-start(f32[16,256]{1,0:T(8,128)} %param.19) | copy-start | bytes 49156
  23.0 20.4 %copy-start.23 = (bf16[256,256]{1,0:T(8,128)(2,1)S(1)}, bf16[256,256]{1,0:T(8,128)(2,1)}, u32[]{:S(2)}) copy-start(bf16[256,256]{1,0:T(8,128)(2,1)} %param.15) | copy-start | bytes 393220
  44.2 32.8 %copy-start.5 = (bf16[128,128]{1,0:T(8,128)(2,1)S(1)}, bf16[128,128]{1,0:T(8,128)(2,1)}, u32[]{:S(2)}) copy-start(bf16[128,128]{1,0:T(8,128)(2,1)} %param.16) | copy-start | bytes 98308
  70.5 28.7 %collective-permute-start = (bf16[32,16,1024]{2,1,0:T(8,128)(2,1)}, bf16[32,16,1024]{2,1,0:T(8,128)(2,1)S(1)}, u32[]{:S(2)}, u32[]{:S(2)}) collective-permute-start(bf16[32,16,1024]{2,1,0:T(8,128)(2,1)} %get-tuple-element.67), channel_id=1, source_target_pairs={{0,4},{4,0},{8,12},{12,8},{16,20},{20,16},{24,28},{28,24},{1,5},{5... | collective-permute-start | bytes 3145736 | tf_op jit(solution)/shard_map/ppermute | solution.py:46
  70.5 106.1 %collective-permute-start.1 = (bf16[32,16,1024]{2,1,0:T(8,128)(2,1)}, bf16[32,16,1024]{2,1,0:T(8,128)(2,1)S(1)}, u32[]{:S(2)}, u32[]{:S(2)}) collective-permute-start(bf16[32,16,1024]{2,1,0:T(8,128)(2,1)} %get-tuple-element.68), channel_id=1, source_target_pairs={{0,8},{4,12},{8,0},{12,4},{16,24},{20,28},{24,16},{28,20},{1,9},{5... | collective-permute-start | bytes 3145736 | tf_op jit(solution)/shard_map/ppermute | solution.py:46
  72.5 129.8 %collective-permute-start.2 = (bf16[32,16,1024]{2,1,0:T(8,128)(2,1)}, bf16[32,16,1024]{2,1,0:T(8,128)(2,1)S(1)}, u32[]{:S(2)}, u32[]{:S(2)}) collective-permute-start(bf16[32,16,1024]{2,1,0:T(8,128)(2,1)} %get-tuple-element.69), channel_id=1, source_target_pairs={{0,12},{4,8},{8,4},{12,0},{16,28},{20,24},{24,20},{28,16},{1,13},{... | collective-permute-start | bytes 3145736 | tf_op jit(solution)/shard_map/ppermute | solution.py:46
  72.6 242.1 %collective-permute-start.3 = (bf16[32,16,1024]{2,1,0:T(8,128)(2,1)}, bf16[32,16,1024]{2,1,0:T(8,128)(2,1)}, u32[]{:S(2)}, u32[]{:S(2)}) collective-permute-start(bf16[32,16,1024]{2,1,0:T(8,128)(2,1)} %get-tuple-element.70), channel_id=1, source_target_pairs={{0,16},{4,20},{8,24},{12,28},{16,0},{20,4},{24,8},{28,12},{1,17},{... | collective-permute-start | bytes 3145736 | tf_op jit(solution)/shard_map/ppermute | solution.py:46
  75.2 261.0 %collective-permute-start.4 = (bf16[32,16,1024]{2,1,0:T(8,128)(2,1)}, bf16[32,16,1024]{2,1,0:T(8,128)(2,1)}, u32[]{:S(2)}, u32[]{:S(2)}) collective-permute-start(bf16[32,16,1024]{2,1,0:T(8,128)(2,1)} %get-tuple-element.71), channel_id=1, source_target_pairs={{0,20},{4,16},{8,28},{12,24},{16,4},{20,0},{24,12},{28,8},{1,21},{... | collective-permute-start | bytes 3145736 | tf_op jit(solution)/shard_map/ppermute | solution.py:46
  96.1 83.1 %copy-start.26 = (pred[1024]{0:T(1024)(128)(4,1)S(1)}, pred[1024]{0:T(1024)(128)(4,1)}, u32[]{:S(2)}) copy-start(pred[1024]{0:T(1024)(128)(4,1)} %get-tuple-element.147) | copy-start | bytes 3076
  96.1 83.1 %copy-start.27 = (pred[1024]{0:T(1024)(128)(4,1)S(1)}, pred[1024]{0:T(1024)(128)(4,1)}, u32[]{:S(2)}) copy-start(pred[1024]{0:T(1024)(128)(4,1)} %get-tuple-element.148) | copy-start | bytes 3076
  96.1 83.1 %copy-start.28 = (pred[1024]{0:T(1024)(128)(4,1)S(1)}, pred[1024]{0:T(1024)(128)(4,1)}, u32[]{:S(2)}) copy-start(pred[1024]{0:T(1024)(128)(4,1)} %get-tuple-element.149) | copy-start | bytes 3076
  96.1 83.1 %copy-start.29 = (pred[1024]{0:T(1024)(128)(4,1)S(1)}, pred[1024]{0:T(1024)(128)(4,1)}, u32[]{:S(2)}) copy-start(pred[1024]{0:T(1024)(128)(4,1)} %get-tuple-element.145) | copy-start | bytes 3076
  96.1 83.1 %copy-start.35 = (bf16[16,64,64]{2,1,0:T(8,128)(2,1)S(1)}, bf16[16,64,64]{2,1,0:T(8,128)(2,1)}, u32[]{:S(2)}) copy-start(bf16[16,64,64]{2,1,0:T(8,128)(2,1)} %param.27) | copy-start | bytes 393220
  99.2 83.7 %copy-start.7 = (bf16[32,16,1024]{2,1,0:T(8,128)(2,1)}, bf16[32,16,1024]{2,1,0:T(8,128)(2,1)S(1)}, u32[]{:S(2)}) copy-start(bf16[32,16,1024]{2,1,0:T(8,128)(2,1)S(1)} %collective-permute-done.refs_1_) | copy-start | bytes 3145732
  99.2 237.0 %collective-permute-start.5 = (bf16[32,16,1024]{2,1,0:T(8,128)(2,1)}, bf16[32,16,1024]{2,1,0:T(8,128)(2,1)}, u32[]{:S(2)}, u32[]{:S(2)}) collective-permute-start(bf16[32,16,1024]{2,1,0:T(8,128)(2,1)} %get-tuple-element.72), channel_id=1, source_target_pairs={{0,24},{4,28},{8,16},{12,20},{16,8},{20,12},{24,0},{28,4},{1,25},{... | collective-permute-start | bytes 3145736 | tf_op jit(solution)/shard_map/ppermute | solution.py:46
  176.6 159.6 %collective-permute-start.6 = (bf16[32,16,1024]{2,1,0:T(8,128)(2,1)}, bf16[32,16,1024]{2,1,0:T(8,128)(2,1)}, u32[]{:S(2)}, u32[]{:S(2)}) collective-permute-start(bf16[32,16,1024]{2,1,0:T(8,128)(2,1)} %get-tuple-element.73), channel_id=1, source_target_pairs={{0,28},{4,24},{8,20},{12,16},{16,12},{20,8},{24,4},{28,0},{1,29},{... | collective-permute-start | bytes 3145736 | tf_op jit(solution)/shard_map/ppermute | solution.py:46
  202.3 133.9 %copy-start.9 = (bf16[32,16,1024]{2,1,0:T(8,128)(2,1)}, bf16[32,16,1024]{2,1,0:T(8,128)(2,1)S(1)}, u32[]{:S(2)}) copy-start(bf16[32,16,1024]{2,1,0:T(8,128)(2,1)S(1)} %collective-permute-done.2.refs_3_) | copy-start | bytes 3145732
  457.3 52.6 %all-to-all-start.1 = ((bf16[8,4,32,1024]{3,2,1,0:T(8,128)(2,1)}), bf16[8,4,32,1024]{3,2,1,0:T(8,128)(2,1)S(1)}, u32[]{:S(2)}, u32[]{:S(2)}) async-start(bf16[8,4,32,1024]{3,2,1,0:T(8,128)(2,1)} %get-tuple-element.76), calls=%async_computation.1 | async-start | bytes 4194304 | tf_op jit(solution)/shard_map/all_to_all | solution.py:458
  469.6 15.7 %collective-permute-start.10 = (bf16[4,272,256]{2,1,0:T(8,128)(2,1)}, bf16[4,272,256]{2,1,0:T(8,128)(2,1)S(1)}, u32[]{:S(2)}, u32[]{:S(2)}) collective-permute-start(bf16[4,272,256]{2,1,0:T(8,128)(2,1)} %get-tuple-element.83), channel_id=1, source_target_pairs={{0,1},{1,0},{2,3},{3,2},{4,5},{5,4},{6,7},{7,6},{8,9},{9,8},{10,11... | collective-permute-start | bytes 1671176 | tf_op jit(solution)/shard_map/ppermute | solution.py:46
  471.1 26.8 %collective-permute-start.11 = (bf16[4,272,256]{2,1,0:T(8,128)(2,1)}, bf16[4,272,256]{2,1,0:T(8,128)(2,1)S(1)}, u32[]{:S(2)}, u32[]{:S(2)}) collective-permute-start(bf16[4,272,256]{2,1,0:T(8,128)(2,1)} %get-tuple-element.84), channel_id=1, source_target_pairs={{0,2},{1,3},{2,0},{3,1},{4,6},{5,7},{6,4},{7,5},{8,10},{9,11},{10,... | collective-permute-start | bytes 1671176 | tf_op jit(solution)/shard_map/ppermute | solution.py:46
  472.6 25.2 %collective-permute-start.12 = (bf16[4,272,256]{2,1,0:T(8,128)(2,1)}, bf16[4,272,256]{2,1,0:T(8,128)(2,1)S(1)}, u32[]{:S(2)}, u32[]{:S(2)}) collective-permute-start(bf16[4,272,256]{2,1,0:T(8,128)(2,1)} %get-tuple-element.85), channel_id=1, source_target_pairs={{0,3},{1,2},{2,1},{3,0},{4,7},{5,6},{6,5},{7,4},{8,11},{9,10},{10,... | collective-permute-start | bytes 1671176 | tf_op jit(solution)/shard_map/ppermute | solution.py:46
  511.2 63.9 %all-to-all-start.5 = ((bf16[8,5,32,1024]{3,2,1,0:T(8,128)(2,1)}), bf16[8,5,32,1024]{3,2,1,0:T(8,128)(2,1)S(1)}, u32[]{:S(2)}, u32[]{:S(2)}) async-start(bf16[8,5,32,1024]{3,2,1,0:T(8,128)(2,1)} %get-tuple-element.94), calls=%async_computation.5 | async-start | bytes 5242880 | tf_op jit(solution)/shard_map/all_to_all | solution.py:458
  523.6 15.7 %collective-permute-start.7 = (bf16[4,272,256]{2,1,0:T(8,128)(2,1)}, bf16[4,272,256]{2,1,0:T(8,128)(2,1)S(1)}, u32[]{:S(2)}, u32[]{:S(2)}) collective-permute-start(bf16[4,272,256]{2,1,0:T(8,128)(2,1)} %get-tuple-element.78), channel_id=1, source_target_pairs={{0,1},{1,0},{2,3},{3,2},{4,5},{5,4},{6,7},{7,6},{8,9},{9,8},{10,11... | collective-permute-start | bytes 1671176 | tf_op jit(solution)/shard_map/ppermute | solution.py:46
  525.2 26.9 %collective-permute-start.8 = (bf16[4,272,256]{2,1,0:T(8,128)(2,1)}, bf16[4,272,256]{2,1,0:T(8,128)(2,1)}, u32[]{:S(2)}, u32[]{:S(2)}) collective-permute-start(bf16[4,272,256]{2,1,0:T(8,128)(2,1)} %get-tuple-element.79), channel_id=1, source_target_pairs={{0,2},{1,3},{2,0},{3,1},{4,6},{5,7},{6,4},{7,5},{8,10},{9,11},{10,... | collective-permute-start | bytes 1671176 | tf_op jit(solution)/shard_map/ppermute | solution.py:46
  526.7 25.4 %collective-permute-start.9 = (bf16[4,272,256]{2,1,0:T(8,128)(2,1)}, bf16[4,272,256]{2,1,0:T(8,128)(2,1)}, u32[]{:S(2)}, u32[]{:S(2)}) collective-permute-start(bf16[4,272,256]{2,1,0:T(8,128)(2,1)} %get-tuple-element.80), channel_id=1, source_target_pairs={{0,3},{1,2},{2,1},{3,0},{4,7},{5,6},{6,5},{7,4},{8,11},{9,10},{10,... | collective-permute-start | bytes 1671176 | tf_op jit(solution)/shard_map/ppermute | solution.py:46
  539.3 35.7 %copy-start.31 = (bf16[4,272,256]{2,1,0:T(8,128)(2,1)}, bf16[4,272,256]{2,1,0:T(8,128)(2,1)S(1)}, u32[]{:S(2)}) copy-start(bf16[4,272,256]{2,1,0:T(8,128)(2,1)S(1)} %collective-permute-done.7.refs_4_) | copy-start | bytes 1671172
  575.0 48.3 %all-to-all-start.3 = ((bf16[8,3,32,1024]{3,2,1,0:T(8,128)(2,1)}), bf16[8,3,32,1024]{3,2,1,0:T(8,128)(2,1)}, u32[]{:S(2)}, u32[]{:S(2)}) async-start(bf16[8,3,32,1024]{3,2,1,0:T(8,128)(2,1)} %get-tuple-element.90), calls=%async_computation.3 | async-start | bytes 3145728 | tf_op jit(solution)/shard_map/all_to_all | solution.py:458
  579.6 16.8 %collective-permute-start.16 = (bf16[1024,256]{1,0:T(8,128)(2,1)}, bf16[1024,256]{1,0:T(8,128)(2,1)S(1)}, u32[]{:S(2)}, u32[]{:S(2)}) collective-permute-start(bf16[1024,256]{1,0:T(8,128)(2,1)} %get-tuple-element.87), channel_id=1, source_target_pairs={{0,1},{1,0},{2,3},{3,2},{4,5},{5,4},{6,7},{7,6},{8,9},{9,8},{10,11... | collective-permute-start | bytes 1572872 | tf_op jit(solution)/shard_map/ppermute | solution.py:46
  581.2 25.3 %collective-permute-start.17 = (bf16[1024,256]{1,0:T(8,128)(2,1)}, bf16[1024,256]{1,0:T(8,128)(2,1)}, u32[]{:S(2)}, u32[]{:S(2)}) collective-permute-start(bf16[1024,256]{1,0:T(8,128)(2,1)} %get-tuple-element.88), channel_id=1, source_target_pairs={{0,2},{1,3},{2,0},{3,1},{4,6},{5,7},{6,4},{7,5},{8,10},{9,11},{10,... | collective-permute-start | bytes 1572872 | tf_op jit(solution)/shard_map/ppermute | solution.py:46
  582.7 24.3 %collective-permute-start.18 = (bf16[1024,256]{1,0:T(8,128)(2,1)}, bf16[1024,256]{1,0:T(8,128)(2,1)}, u32[]{:S(2)}, u32[]{:S(2)}) collective-permute-start(bf16[1024,256]{1,0:T(8,128)(2,1)} %get-tuple-element.89), channel_id=1, source_target_pairs={{0,3},{1,2},{2,1},{3,0},{4,7},{5,6},{6,5},{7,4},{8,11},{9,10},{10,... | collective-permute-start | bytes 1572872 | tf_op jit(solution)/shard_map/ppermute | solution.py:46
  593.4 27.5 %collective-permute-start.13 = (bf16[5,272,256]{2,1,0:T(8,128)(2,1)}, bf16[5,272,256]{2,1,0:T(8,128)(2,1)S(1)}, u32[]{:S(2)}, u32[]{:S(2)}) collective-permute-start(bf16[5,272,256]{2,1,0:T(8,128)(2,1)} %get-tuple-element.96), channel_id=1, source_target_pairs={{0,1},{1,0},{2,3},{3,2},{4,5},{5,4},{6,7},{7,6},{8,9},{9,8},{10,11... | collective-permute-start | bytes 2088968 | tf_op jit(solution)/shard_map/ppermute | solution.py:46
  594.9 41.4 %collective-permute-start.14 = (bf16[5,272,256]{2,1,0:T(8,128)(2,1)}, bf16[5,272,256]{2,1,0:T(8,128)(2,1)}, u32[]{:S(2)}, u32[]{:S(2)}) collective-permute-start(bf16[5,272,256]{2,1,0:T(8,128)(2,1)} %get-tuple-element.97), channel_id=1, source_target_pairs={{0,2},{1,3},{2,0},{3,1},{4,6},{5,7},{6,4},{7,5},{8,10},{9,11},{10,... | collective-permute-start | bytes 2088968 | tf_op jit(solution)/shard_map/ppermute | solution.py:46
  596.4 21.4 %copy-start.12 = (bf16[1024,256]{1,0:T(8,128)(2,1)}, bf16[1024,256]{1,0:T(8,128)(2,1)S(1)}, u32[]{:S(2)}) copy-start(bf16[1024,256]{1,0:T(8,128)(2,1)S(1)} %collective-permute-done.16.refs_4_) | copy-start | bytes 1572868
  596.4 40.5 %collective-permute-start.15 = (bf16[5,272,256]{2,1,0:T(8,128)(2,1)}, bf16[5,272,256]{2,1,0:T(8,128)(2,1)}, u32[]{:S(2)}, u32[]{:S(2)}) collective-permute-start(bf16[5,272,256]{2,1,0:T(8,128)(2,1)} %get-tuple-element.98), channel_id=1, source_target_pairs={{0,3},{1,2},{2,1},{3,0},{4,7},{5,6},{6,5},{7,4},{8,11},{9,10},{10,... | collective-permute-start | bytes 2088968 | tf_op jit(solution)/shard_map/ppermute | solution.py:46
  617.8 29.2 %collective-permute-start.19 = (bf16[1024,256]{1,0:T(8,128)(2,1)}, bf16[1024,256]{1,0:T(8,128)(2,1)S(1)}, u32[]{:S(2)}, u32[]{:S(2)}) collective-permute-start(bf16[1024,256]{1,0:T(8,128)(2,1)} %get-tuple-element.113), channel_id=1, source_target_pairs={{0,1},{1,0},{2,3},{3,2},{4,5},{5,4},{6,7},{7,6},{8,9},{9,8},{10,11... | collective-permute-start | bytes 1572872 | tf_op jit(solution)/shard_map/ppermute | solution.py:46
  619.4 48.3 %collective-permute-start.20 = (bf16[1024,256]{1,0:T(8,128)(2,1)}, bf16[1024,256]{1,0:T(8,128)(2,1)S(1)}, u32[]{:S(2)}, u32[]{:S(2)}) collective-permute-start(bf16[1024,256]{1,0:T(8,128)(2,1)} %get-tuple-element.114), channel_id=1, source_target_pairs={{0,2},{1,3},{2,0},{3,1},{4,6},{5,7},{6,4},{7,5},{8,10},{9,11},{10,... | collective-permute-start | bytes 1572872 | tf_op jit(solution)/shard_map/ppermute | solution.py:46
  620.9 46.9 %collective-permute-start.21 = (bf16[1024,256]{1,0:T(8,128)(2,1)}, bf16[1024,256]{1,0:T(8,128)(2,1)S(1)}, u32[]{:S(2)}, u32[]{:S(2)}) collective-permute-start(bf16[1024,256]{1,0:T(8,128)(2,1)} %get-tuple-element.115), channel_id=1, source_target_pairs={{0,3},{1,2},{2,1},{3,0},{4,7},{5,6},{6,5},{7,4},{8,11},{9,10},{10,... | collective-permute-start | bytes 1572872 | tf_op jit(solution)/shard_map/ppermute | solution.py:46
  630.2 54.1 %all-to-all-start.4 = ((bf16[4,3,272,256]{3,2,1,0:T(8,128)(2,1)}), bf16[4,3,272,256]{3,2,1,0:T(8,128)(2,1)S(1)}, u32[]{:S(2)}, u32[]{:S(2)}) async-start(bf16[4,3,272,256]{3,2,1,0:T(8,128)(2,1)} %get-tuple-element.92), calls=%async_computation.4 | async-start | bytes 3342336 | tf_op jit(solution)/shard_map/all_to_all | solution.py:51
  647.1 33.4 %copy-start.13 = (bf16[1024,256]{1,0:T(8,128)(2,1)}, bf16[1024,256]{1,0:T(8,128)(2,1)S(1)}, u32[]{:S(2)}) copy-start(bf16[1024,256]{1,0:T(8,128)(2,1)S(1)} %collective-permute-done.19.refs_4_) | copy-start | bytes 1572868
  667.7 12.7 %copy-start.15 = (bf16[1024,256]{1,0:T(8,128)(2,1)}, bf16[1024,256]{1,0:T(8,128)(2,1)S(1)}, u32[]{:S(2)}) copy-start(bf16[1024,256]{1,0:T(8,128)(2,1)S(1)} %collective-permute-done.21.refs_6_) | copy-start | bytes 1572868
  680.5 16.0 %collective-permute-start.22 = (bf16[1280,256]{1,0:T(8,128)(2,1)}, bf16[1280,256]{1,0:T(8,128)(2,1)S(1)}, u32[]{:S(2)}, u32[]{:S(2)}) collective-permute-start(bf16[1280,256]{1,0:T(8,128)(2,1)} %get-tuple-element.121), channel_id=1, source_target_pairs={{0,1},{1,0},{2,3},{3,2},{4,5},{5,4},{6,7},{7,6},{8,9},{9,8},{10,11... | collective-permute-start | bytes 1966088 | tf_op jit(solution)/shard_map/ppermute | solution.py:46
  680.5 23.1 %collective-permute-start.23 = (bf16[1280,256]{1,0:T(8,128)(2,1)}, bf16[1280,256]{1,0:T(8,128)(2,1)S(1)}, u32[]{:S(2)}, u32[]{:S(2)}) collective-permute-start(bf16[1280,256]{1,0:T(8,128)(2,1)} %get-tuple-element.122), channel_id=1, source_target_pairs={{0,2},{1,3},{2,0},{3,1},{4,6},{5,7},{6,4},{7,5},{8,10},{9,11},{10,... | collective-permute-start | bytes 1966088 | tf_op jit(solution)/shard_map/ppermute | solution.py:46
  683.0 21.6 %collective-permute-start.24 = (bf16[1280,256]{1,0:T(8,128)(2,1)}, bf16[1280,256]{1,0:T(8,128)(2,1)}, u32[]{:S(2)}, u32[]{:S(2)}) collective-permute-start(bf16[1280,256]{1,0:T(8,128)(2,1)} %get-tuple-element.123), channel_id=1, source_target_pairs={{0,3},{1,2},{2,1},{3,0},{4,7},{5,6},{6,5},{7,4},{8,11},{9,10},{10,... | collective-permute-start | bytes 1966088 | tf_op jit(solution)/shard_map/ppermute | solution.py:46
  684.4 20.3 %copy-start.6 = (bf16[4,3,272,256]{3,2,1,0:T(8,128)(2,1)}, bf16[4,3,272,256]{3,2,1,0:T(8,128)(2,1)S(1)}, u32[]{:S(2)}) copy-start(bf16[4,3,272,256]{3,2,1,0:T(8,128)(2,1)S(1)} %all-to-all-done.4.refs_3_) | copy-start | bytes 5013508
  696.5 17.5 %copy-start.10 = (bf16[1280,256]{1,0:T(8,128)(2,1)}, bf16[1280,256]{1,0:T(8,128)(2,1)S(1)}, u32[]{:S(2)}) copy-start(bf16[1280,256]{1,0:T(8,128)(2,1)S(1)} %collective-permute-done.22.refs_4_) | copy-start | bytes 1966084
  714.0 26.3 %all-to-all-start.6 = ((bf16[4,768,256]{2,1,0:T(8,128)(2,1)}), bf16[4,768,256]{2,1,0:T(8,128)(2,1)S(1)}, u32[]{:S(2)}, u32[]{:S(2)}) async-start(bf16[4,768,256]{2,1,0:T(8,128)(2,1)} %hidden_units.7), calls=%async_computation.6 | async-start | bytes 3145728 | tf_op jit(solution)/shard_map/all_to_all | solution.py:51
  (19 other events, 122.1 us)

commit v4 on v3

--- a/solution.py
+++ b/solution.py
@@ -68,19 +68,20 @@
             outs[d][q] = rows_of[pl.ds(d * ql + q, al, stride=block), :].astype(BF)
 
 
-def inner(tokens, scale, gain, mix, twiddle, parts):
-    count, chans = tokens.shape
+def inner(tokens, scale, gain, mix, twiddle, parts, start, chans):
+    count = tokens.shape[0]
     block = mix.shape[0]
     al = count // block
     ql = block // parts
     cb = LANES
+    first = start // cb
     return pl.pallas_call(
         lambda *refs: inner_kernel(parts, *refs),
         grid=(chans // cb,),
         in_specs=[
-            pl.BlockSpec((count, cb), lambda c: (0, c)),
+            pl.BlockSpec((count, cb), lambda c: (0, c + first)),
             whole((count, 1)),
-            pl.BlockSpec((1, cb), lambda c: (0, c)),
+            pl.BlockSpec((1, cb), lambda c: (0, c + first)),
             whole((block, block)),
             whole((al, block, 1)),
         ],
@@ -95,7 +96,7 @@
 def outer_kernel(parts, sizes, *refs):
     pieces = refs[:parts]
     kern, fwd, back, twiddle = refs[parts : parts + 4]
-    outs, rows_of = refs[parts + 4 : -1], refs[-1]
+    outs, rows_of = refs[-1 - len(sizes) : -1], refs[-1]
     width = kern.shape[-1]
     side = twiddle.shape[1]
     pair = fwd.shape[0] // side
@@ -121,27 +122,31 @@
                 r += 1
 
 
-def outer(pieces, kern, fwd, back, twiddle, sizes):
+def outer(pieces, kern, fwd, back, twiddle, sizes, start, chans, carried):
     parts = len(pieces)
-    ql, al, chans = pieces[0].shape
+    ql, al, width = pieces[0].shape
     side = parts * al
-    cb = 256
+    cb = math.gcd(width, 256)
+    first = start // cb
+    extra = carried or []
     return pl.pallas_call(
         lambda *refs: outer_kernel(parts, sizes, *refs),
-        grid=(chans // cb, ql // G),
+        grid=(width // cb, ql // G),
         in_specs=[pl.BlockSpec((G, al, cb), lambda c, q: (q, 0, c)) for _ in range(parts)]
         + [
             pl.BlockSpec((parts, G, al, cb), lambda c, q: (0, q, 0, c)),
             whole(fwd.shape),
             whole(back.shape),
             pl.BlockSpec((G, side, 1), lambda c, q: (q, 0, 0)),
-        ],
-        out_specs=[pl.BlockSpec((parts, size, G, cb), lambda c, q: (0, 0, q, c)) for size in sizes],
+        ]
+        + [pl.BlockSpec(memory_space=pl.ANY) for _ in extra],
+        out_specs=[pl.BlockSpec((parts, size, G, cb), lambda c, q: (0, 0, q, c + first)) for size in sizes],
         out_shape=[jax.ShapeDtypeStruct((parts, size, ql, chans), BF) for size in sizes],
         scratch_shapes=[pltpu.VMEM((cb // LANES, G * side, LANES), F32)],
-        cost_estimate=cost(8 * side * side * ql * chans, 6 * side * ql * chans),
+        input_output_aliases={parts + 4 + i: i for i in range(len(extra))},
+        cost_estimate=cost(8 * side * side * ql * width, 6 * side * ql * width),
         name="outer_mix",
-    )(*pieces, kern, fwd, back, twiddle)
+    )(*pieces, kern, fwd, back, twiddle, *extra)
 
 
 def eye_at(rows, cols, first):
@@ -396,8 +401,12 @@
         me = lax.axis_index("hid")
         tok = tokens.reshape(count, chans)
 
-        sent = freq_kernel.reshape(al, parts, ql, chans).transpose(1, 2, 0, 3)
-        kern = lax.all_to_all(sent, "ctx", split_axis=0, concat_axis=0, tiled=True)
+        split = chans // 2 if chans % 512 == 0 else chans
+        chan_starts = range(0, chans, split)
+        kerns = []
+        for c in chan_starts:
+            sent = freq_kernel[:, :, c : c + split].reshape(al, parts, ql, split).transpose(1, 2, 0, 3)
+            kerns.append(lax.all_to_all(sent, "ctx", split_axis=0, concat_axis=0, tiled=True))
 
         wide = tok.astype(F32)
         sums = lax.psum(jnp.sum(wide * wide, axis=1), "hid")
@@ -405,27 +414,26 @@
         gain = first_gain.reshape(1, chans)
         gain_two = second_gain.reshape(1, chans)
 
-        pieces = inner(
-            tok,
-            scale,
-            gain,
-            xor_blocks(seq_inner, 0, at, parts),
-            xor_blocks(twiddle_in, 1, at, parts).reshape(al, block, 1),
-            parts,
-        )
+        rows_in = xor_blocks(seq_inner, 0, at, parts)
+        turn_in = xor_blocks(twiddle_in, 1, at, parts).reshape(al, block, 1)
+        waves = [inner(tok, scale, gain, rows_in, turn_in, parts, c, split) for c in chan_starts]
         fwd = repeat_block(xor_blocks(seq_outer, 1, at, parts), 2)
         back = repeat_block(inv_outer, 2)
         turn = twiddle_out.T.reshape(ql, al * parts, 1)
         sizes = splits_of(al, RETURN_SPLIT)
-        pieces = exchange(pieces, "ctx", parts)
+        waves = [exchange(wave, "ctx", parts) for wave in waves]
 
         lanes = right_up.shape[0] * left_up.shape[0]
         halves = lanes // 128 if lanes % 128 == 0 else 1
         up_one, up_two, down_one, down_two = expand_factors(
             right_up, left_up, right_down, left_down, me, groups, halves
         )
-        kern = after(kern, up_one, up_two, down_one, down_two, turn)
-        backed = outer(pieces, kern, fwd, back, turn, sizes)
+        kerns[0] = after(kerns[0], up_one, up_two, down_one, down_two, turn)
+        backed = None
+        for f, c in enumerate(chan_starts):
+            if f + 1 < len(waves):
+                kerns[f] = after(kerns[f], waves[f + 1][-1])
+            backed = outer(waves[f], kerns[f], fwd, back, turn, sizes, c, chans, backed)
         chunks = len(sizes)
         place = me.astype(jnp.int32).reshape(1)
         starts = [sum(sizes[:j]) for j in range(chunks)]

time: 749 us -> 746 us (level)
  blocking collectives: 113 us -> 78.9 us
  starting transfers between devices: 59.4 us -> 91.8 us
  waiting for transfers between devices: 365 us -> 354 us
    all_to_all x1, blocking collectives: 96.2 us -> 62.1 us  [shards(): home = lax.all_to_all(sent, 'ctx', split_axis=0, concat_axis=0, tiled=True)]
    ppermute x25 -> x32, starting transfers between devices: 33.5 us -> 61.6 us  [swap(): return lax.ppermute(x, name, [(i, i ^ d) for i in range(size)])]
    ppermute x25 -> x32, waiting for transfers between devices: 312 us -> 285 us  [swap(): return lax.ppermute(x, name, [(i, i ^ d) for i in range(size)])]
    slice x0 -> x3, local copies, waits for them, and re-layouts: none -> 16.2 us  [shards(): freq_kernel[:, :, c:c + split].reshape(al, parts, ql, split)]
    all_to_all x1 -> x2, waiting for transfers between devices: 19.4 us -> 34.4 us  [shards(): lax.all_to_all(sent, 'ctx', split_axis=0, concat_axis=0, tiled=True)]
    unnamed x80 -> x77, local copies, waits for them, and re-layouts: 15.8 us -> 5.02 us
    pallas_call x1 -> x2, Pallas kernels: 26.3 us -> 29.7 us  [inner(): pl.pallas_call(lambda *refs: inner_kernel(parts, *refs), grid=(chans // c...]
    pallas_call x1 -> x2, Pallas kernels: 24.8 us -> 27.7 us  [outer(): pl.pallas_call(lambda *refs: outer_kernel(parts, sizes, *refs), grid=(wid...]
  transfers between devices with their start and end apart: 31 -> 39, of which waited for: 20 -> 21; matrix products, arithmetic and copies ran while one was open for 5% -> 5% of each run, Pallas kernels for 16% -> 18%
where the time goes in v4:
time: 746 us; the launch traced here: 741 us
  waiting for transfers between devices  354 us (47%)
  Pallas kernels  164 us (22%)
  starting transfers between devices  91.8 us (12%)
  blocking collectives  78.9 us (11%)
  local copies, waits for them, and re-layouts  28.4 us (4%)
  matrix products  12.6 us (2%)
  other arithmetic  11.1 us (1%)
    ppermute x32, waiting for transfers between devices, swap(): return lax.ppermute(x, name, [(i, i ^ d) for i in range(size)])  285 us
    all_to_all x1, blocking collectives, shards(): home = lax.all_to_all(sent, 'ctx', split_axis=0, concat_axis=0, tiled=True)  62.1 us
    ppermute x32, starting transfers between devices, swap(): return lax.ppermute(x, name, [(i, i ^ d) for i in range(size)])  61.6 us
    pallas_call x4, Pallas kernels, hidden(): pl.pallas_call(lambda *refs: hidden_kernel(groups, total, halves, *refs),...  43.7 us
    pallas_call x4, Pallas kernels, mix(): pl.pallas_call(lambda *refs: mix_kernel(groups, *refs), grid=(size,), in_...  34.5 us
    all_to_all x2, waiting for transfers between devices, shards(): lax.all_to_all(sent, 'ctx', split_axis=0, concat_axis=0, tiled=True)  34.4 us
    all_to_all x3, waiting for transfers between devices, shards(): home = lax.all_to_all(sent, 'ctx', split_axis=0, concat_axis=0, tiled=True)  34.1 us
    pallas_call x2, Pallas kernels, inner(): pl.pallas_call(lambda *refs: inner_kernel(parts, *refs), grid=(chans // c...  29.7 us
  transfers between devices with their start and end apart: 39, of which 21 were waited for; matrix products, arithmetic and copies ran while one was open for 5% of the time, Pallas kernels for 18%

profile of v4, /device:TPU:0, one launch (start us, length us, event | category | flops | bytes accessed | tf_op | source)
XLA Modules:
  0.0 741.0 jit_solution(2300176548167664422)
XLA Ops:
  0.0 5.2 fusion.202
  5.2 4.4 copy.31
  9.6 6.3 all-to-all-start.1
  16.0 5.1 multiply_reduce_fusion
  21.1 16.8 %psum.7 = f32[4096]{0:T(1024)S(1)} all-reduce(f32[4096]{0:T(1024)S(1)} %multiply_reduce_fusion), channel_id=1, replica_groups=mesh['ctx'=8,'hid'=4] {'hid'}, use_global_device_ids=true, to_apply=%region_1.0 | all-reduce | flops 4096 | bytes 32768 | tf_op jit(solution)/shard_map/psum | solution.py:412
  42.9 14.9 %inner_mix.2 = (bf16[32,16,512]{2,1,0:T(8,128)(2,1)}, bf16[32,16,512]{2,1,0:T(8,128)(2,1)}, bf16[32,16,512]{2,1,0:T(8,128)(2,1)}, bf16[32,16,512]{2,1,0:T(8,128)...) custom-call(bf16[4096,1024]{1,0:T(8,128)(2,1)} %bitcast.55, ...), custom_call_target="tpu_custom_call" | custom-call | flops 1073741824 | bytes 8388608 | tf_op jit(solution)/shard_map/inner_mix/pallas_call | solution.py:78
  57.8 3.9 collective-permute-start.6
  61.7 14.8 %inner_mix.3 = (bf16[32,16,512]{2,1,0:T(8,128)(2,1)}, bf16[32,16,512]{2,1,0:T(8,128)(2,1)}, bf16[32,16,512]{2,1,0:T(8,128)(2,1)}, bf16[32,16,512]{2,1,0:T(8,128)...) custom-call(bf16[4096,1024]{1,0:T(8,128)(2,1)} %bitcast.56, ...), custom_call_target="tpu_custom_call" | custom-call | flops 1073741824 | bytes 8388608 | tf_op jit(solution)/shard_map/inner_mix/pallas_call | solution.py:78
  78.5 6.5 copy.28
  87.4 34.4 %all-to-all-done.1.refs_8_ = bf16[8,32,16,512]{3,2,1,0:T(8,128)(2,1)} async-done(((bf16[8,32,16,512]{3,2,1,0:T(8,128)(2,1)}), bf16[8,32,16,512]{3,2,1,0:T(8,128)(2,1)}, u32[]{:S(2)}, u32[]{:S(2)}) %all-to-all-start.1) | async-done | bytes 4194336 | tf_op jit(solution)/shard_map/all_to_all | solution.py:409
  121.8 4.7 all-to-all-start
  126.6 3.8 fusion.9.refs_2_
  130.9 5.0 fusion.8.refs_1_
  135.9 3.7 select_convert_fusion.refs_2_
  150.9 128.1 %collective-permute-done.10.refs_4_ = bf16[32,16,512]{2,1,0:T(8,128)(2,1)S(1)} collective-permute-done((bf16[32,16,512]{2,1,0:T(8,128)(2,1)}, bf16[32,16,512]{2,1,0:T(8,128)(2,1)S(1)}, u32[]{:S(2)}, u32[]{:S(2)}) %collective-permute-start.10) | collective-permute-done | bytes 524320 | tf_op jit(solution)/shard_map/ppermute | solution.py:46
  279.0 10.5 %collective-permute-done.11.refs_5_ = bf16[32,16,512]{2,1,0:T(8,128)(2,1)} collective-permute-done((bf16[32,16,512]{2,1,0:T(8,128)(2,1)}, bf16[32,16,512]{2,1,0:T(8,128)(2,1)}, u32[]{:S(2)}, u32[]{:S(2)}) %collective-permute-start.11) | collective-permute-done | bytes 524320 | tf_op jit(solution)/shard_map/ppermute | solution.py:46
  289.9 22.5 %collective-permute-start.4 = (bf16[32,16,512]{2,1,0:T(8,128)(2,1)}, bf16[32,16,512]{2,1,0:T(8,128)(2,1)S(1)}, u32[]{:S(2)}, u32[]{:S(2)}) collective-permute-start(bf16[32,16,512]{2,1,0:T(8,128)(2,1)} %get-tuple-element.84), channel_id=1, source_target_pairs={{0,20},{4,16},{8,28},{12,24},{16,4},{20,0},{24,12},{28,8},{1,21},{... | collective-permute-start | bytes 1572872 | tf_op jit(solution)/shard_map/ppermute | solution.py:46
  317.6 13.8 %outer_mix.2 = (bf16[8,4,32,1024]{3,2,1,0:T(8,128)(2,1)}, bf16[8,4,32,1024]{3,2,1,0:T(8,128)(2,1)}, bf16[8,5,32,1024]{3,2,1,0:T(8,128)(2,1)}, bf16[8,3,32,1024]{3,2,1,0:T(8,128)(2,1)}) custom-call(bf16[32,16,512]{2,1,0:T(8,128)(2,1)} %get-tuple-element.87.refs_0_, bf16[32,16,512]{2,1,0:T(8,128)(2,1)} %copy-done.20, bf16[32,16,512]{2,1,0:T(8,128)(2,1)} %copy-done.21, ...), custom_call_target="tpu_custom_call" | custom-call | flops 2147483648 | bytes 12582912 | tf_op jit(solution)/shard_map/outer_mix/pallas_call | solution.py:132
  331.4 26.3 %collective-permute-done.3.refs_4_ = bf16[32,16,512]{2,1,0:T(8,128)(2,1)S(1)} collective-permute-done((bf16[32,16,512]{2,1,0:T(8,128)(2,1)}, bf16[32,16,512]{2,1,0:T(8,128)(2,1)S(1)}, u32[]{:S(2)}, u32[]{:S(2)}) %collective-permute-start.3) | collective-permute-done | bytes 524320 | tf_op jit(solution)/shard_map/ppermute | solution.py:46
  357.7 10.3 %collective-permute-done.4.refs_5_ = bf16[32,16,512]{2,1,0:T(8,128)(2,1)S(1)} collective-permute-done((bf16[32,16,512]{2,1,0:T(8,128)(2,1)}, bf16[32,16,512]{2,1,0:T(8,128)(2,1)S(1)}, u32[]{:S(2)}, u32[]{:S(2)}) %collective-permute-start.4) | collective-permute-done | bytes 524320 | tf_op jit(solution)/shard_map/ppermute | solution.py:46
  368.8 13.8 %outer_mix.3 = (bf16[8,4,32,1024]{3,2,1,0:T(8,128)(2,1)}, bf16[8,4,32,1024]{3,2,1,0:T(8,128)(2,1)}, bf16[8,5,32,1024]{3,2,1,0:T(8,128)(2,1)}, bf16[8,3,32,1024]{3,2,1,0:T(8,128)(2,1)}) custom-call(bf16[32,16,512]{2,1,0:T(8,128)(2,1)} %get-tuple-element.79.refs_0_, ...), custom_call_target="tpu_custom_call", output_to_operand_aliasing={{0}: (12, {}), {1}: (13, {}), {2}: (14, {}), {3}: (15, {})} | custom-call | flops 2147483648 | bytes 12582912 | tf_op jit(solution)/shard_map/outer_mix/pallas_call | solution.py:132
  382.6 62.1 %all_to_all.40.refs_1_ = bf16[8,4,32,1024]{3,2,1,0:T(8,128)(2,1)} all-to-all(bf16[8,4,32,1024]{3,2,1,0:T(8,128)(2,1)} %get-tuple-element.107), channel_id=1, replica_groups=mesh['ctx'=8,'hid'=4] {'ctx'}, dimensions={0} | all-to-all | bytes 4194304 | tf_op jit(solution)/shard_map/all_to_all | solution.py:466
  444.7 3.8 all-to-all-start.2
  448.5 8.6 %mix_tokens.5 = (f32[1024,1024]{1,0:T(8,128)}, bf16[4,272,256]{2,1,0:T(8,128)(2,1)}, bf16[4,272,256]{2,1,0:T(8,128)(2,1)}, bf16[4,272,256]{2,1,0:T(8,128)(2,1)}, bf16[4,272,256]{2,1,0:T(8,128)(2,1)}) custom-call(s32[1]{0:T(128)} %bitcast.refs_0_, bf16[8,4,32,1024]{3,2,1,0:T(8,128)(2,1)} %all_to_all.40.refs_1_, bf16[4096,1024]{1,0:T(8,128)(2,1)} %bitcast.57, ...), custom_call_target="tpu_custom_call" | custom-call | flops 2684354560 | bytes 10485760 | tf_op jit(solution)/shard_map/mix_tokens/pallas_call | solution.py:204
  460.7 12.2 %collective-permute-done.17.refs_4_ = bf16[4,272,256]{2,1,0:T(8,128)(2,1)S(1)} collective-permute-done((bf16[4,272,256]{2,1,0:T(8,128)(2,1)}, bf16[4,272,256]{2,1,0:T(8,128)(2,1)S(1)}, u32[]{:S(2)}, u32[]{:S(2)}) %collective-permute-start.17) | collective-permute-done | bytes 557088 | tf_op jit(solution)/shard_map/ppermute | solution.py:46
  472.8 12.7 %collective-permute-done.18.refs_5_ = bf16[4,272,256]{2,1,0:T(8,128)(2,1)S(1)} collective-permute-done((bf16[4,272,256]{2,1,0:T(8,128)(2,1)}, bf16[4,272,256]{2,1,0:T(8,128)(2,1)S(1)}, u32[]{:S(2)}, u32[]{:S(2)}) %collective-permute-start.18) | collective-permute-done | bytes 557088 | tf_op jit(solution)/shard_map/ppermute | solution.py:46
  486.5 11.0 %all-to-all-done.2.refs_1_ = bf16[8,4,32,1024]{3,2,1,0:T(8,128)(2,1)S(1)} async-done(((bf16[8,4,32,1024]{3,2,1,0:T(8,128)(2,1)}), bf16[8,4,32,1024]{3,2,1,0:T(8,128)(2,1)S(1)}, u32[]{:S(2)}, u32[]{:S(2)}) %all-to-all-start.2) | async-done | bytes 2097184 | tf_op jit(solution)/shard_map/all_to_all | solution.py:466
  498.8 3.6 all-to-all-start.6
  502.5 8.7 %mix_tokens.4 = (f32[1024,1024]{1,0:T(8,128)}, bf16[4,272,256]{2,1,0:T(8,128)(2,1)}, bf16[4,272,256]{2,1,0:T(8,128)(2,1)}, bf16[4,272,256]{2,1,0:T(8,128)(2,1)}, bf16[4,272,256]{2,1,0:T(8,128)(2,1)}) custom-call(s32[1]{0:T(128)} %bitcast.refs_0_, bf16[8,4,32,1024]{3,2,1,0:T(8,128)(2,1)} %copy-done.3, bf16[4096,1024]{1,0:T(8,128)(2,1)} %bitcast.58, ...), custom_call_target="tpu_custom_call" | custom-call | flops 2684354560 | bytes 10485760 | tf_op jit(solution)/shard_map/mix_tokens/pallas_call | solution.py:204
  514.7 10.8 %hidden_units.4 = (bf16[1024,256]{1,0:T(8,128)(2,1)}, bf16[1024,256]{1,0:T(8,128)(2,1)}, bf16[1024,256]{1,0:T(8,128)(2,1)}, bf16[1024,256]{1,0:T(8,128)(2,1)}) custom-call(s32[1]{0:T(128)} %bitcast.refs_0_, bf16[1024,2048]{1,0:T(8,128)(2,1)} %fusion.8.refs_1_, bf16[2048,1024]{1,0:T(8,128)(2,1)} %fusion.9.refs_2_, ...), custom_call_target="tpu_custom_call" | custom-call | flops 4294967296 | bytes 4194304 | tf_op jit(solution)/shard_map/hidden_units/pallas_call | solution.py:258
  526.9 12.7 %collective-permute-done.15.refs_5_ = bf16[4,272,256]{2,1,0:T(8,128)(2,1)} collective-permute-done((bf16[4,272,256]{2,1,0:T(8,128)(2,1)}, bf16[4,272,256]{2,1,0:T(8,128)(2,1)}, u32[]{:S(2)}, u32[]{:S(2)}) %collective-permute-start.15) | collective-permute-done | bytes 557088 | tf_op jit(solution)/shard_map/ppermute | solution.py:46
  539.6 23.1 %all-to-all-done.6.refs_1_ = bf16[8,5,32,1024]{3,2,1,0:T(8,128)(2,1)S(1)} async-done(((bf16[8,5,32,1024]{3,2,1,0:T(8,128)(2,1)}), bf16[8,5,32,1024]{3,2,1,0:T(8,128)(2,1)S(1)}, u32[]{:S(2)}, u32[]{:S(2)}) %all-to-all-start.6) | async-done | bytes 2621472 | tf_op jit(solution)/shard_map/all_to_all | solution.py:466
  562.7 4.3 all-to-all-start.4
  570.5 10.3 %mix_tokens.7 = (f32[1280,1024]{1,0:T(8,128)}, bf16[5,272,256]{2,1,0:T(8,128)(2,1)}, bf16[5,272,256]{2,1,0:T(8,128)(2,1)}, bf16[5,272,256]{2,1,0:T(8,128)(2,1)}, bf16[5,272,256]{2,1,0:T(8,128)(2,1)}) custom-call(s32[1]{0:T(128)} %bitcast.refs_0_, bf16[8,5,32,1024]{3,2,1,0:T(8,128)(2,1)} %copy-done.2, bf16[4096,1024]{1,0:T(8,128)(2,1)} %bitcast.59, ...), custom_call_target="tpu_custom_call" | custom-call | flops 3355443200 | bytes 13107200 | tf_op jit(solution)/shard_map/mix_tokens/pallas_call | solution.py:204
  584.5 9.5 %collective-permute-done.24.refs_5_ = bf16[1024,256]{1,0:T(8,128)(2,1)} collective-permute-done((bf16[1024,256]{1,0:T(8,128)(2,1)}, bf16[1024,256]{1,0:T(8,128)(2,1)}, u32[]{:S(2)}, u32[]{:S(2)}) %collective-permute-start.24) | collective-permute-done | bytes 524320 | tf_op jit(solution)/shard_map/ppermute | solution.py:46
  594.4 10.8 %hidden_units.5 = (bf16[1024,256]{1,0:T(8,128)(2,1)}, bf16[1024,256]{1,0:T(8,128)(2,1)}, bf16[1024,256]{1,0:T(8,128)(2,1)}, bf16[1024,256]{1,0:T(8,128)(2,1)}) custom-call(s32[1]{0:T(128)} %bitcast.refs_0_, bf16[1024,2048]{1,0:T(8,128)(2,1)} %fusion.8.refs_1_, bf16[2048,1024]{1,0:T(8,128)(2,1)} %fusion.9.refs_2_, ...), custom_call_target="tpu_custom_call" | custom-call | flops 4294967296 | bytes 4194304 | tf_op jit(solution)/shard_map/hidden_units/pallas_call | solution.py:258
  610.7 6.9 mix_tokens.6
  617.6 3.8 all-to-all-start.5
  624.2 10.2 %collective-permute-done.26.refs_4_ = bf16[1024,256]{1,0:T(8,128)(2,1)S(1)} collective-permute-done((bf16[1024,256]{1,0:T(8,128)(2,1)}, bf16[1024,256]{1,0:T(8,128)(2,1)S(1)}, u32[]{:S(2)}, u32[]{:S(2)}) %collective-permute-start.26) | collective-permute-done | bytes 524320 | tf_op jit(solution)/shard_map/ppermute | solution.py:46
  634.4 20.8 %collective-permute-done.27.refs_5_ = bf16[1024,256]{1,0:T(8,128)(2,1)S(1)} collective-permute-done((bf16[1024,256]{1,0:T(8,128)(2,1)}, bf16[1024,256]{1,0:T(8,128)(2,1)S(1)}, u32[]{:S(2)}, u32[]{:S(2)}) %collective-permute-start.27) | collective-permute-done | bytes 524320 | tf_op jit(solution)/shard_map/ppermute | solution.py:46
  655.2 12.7 %hidden_units.6 = (bf16[1280,256]{1,0:T(8,128)(2,1)}, bf16[1280,256]{1,0:T(8,128)(2,1)}, bf16[1280,256]{1,0:T(8,128)(2,1)}, bf16[1280,256]{1,0:T(8,128)(2,1)}) custom-call(s32[1]{0:T(128)} %bitcast.refs_0_, bf16[1024,2048]{1,0:T(8,128)(2,1)} %fusion.8.refs_1_, bf16[2048,1024]{1,0:T(8,128)(2,1)} %fusion.9.refs_2_, ...), custom_call_target="tpu_custom_call" | custom-call | flops 5368709120 | bytes 5242880 | tf_op jit(solution)/shard_map/hidden_units/pallas_call | solution.py:258
  671.9 13.0 %collective-permute-done.29.refs_4_ = bf16[1280,256]{1,0:T(8,128)(2,1)S(1)} collective-permute-done((bf16[1280,256]{1,0:T(8,128)(2,1)}, bf16[1280,256]{1,0:T(8,128)(2,1)S(1)}, u32[]{:S(2)}, u32[]{:S(2)}) %collective-permute-start.29) | collective-permute-done | bytes 655392 | tf_op jit(solution)/shard_map/ppermute | solution.py:46
  684.9 12.0 %collective-permute-done.30.refs_5_ = bf16[1280,256]{1,0:T(8,128)(2,1)S(1)} collective-permute-done((bf16[1280,256]{1,0:T(8,128)(2,1)}, bf16[1280,256]{1,0:T(8,128)(2,1)S(1)}, u32[]{:S(2)}, u32[]{:S(2)}) %collective-permute-start.30) | collective-permute-done | bytes 655392 | tf_op jit(solution)/shard_map/ppermute | solution.py:46
  698.7 9.3 %hidden_units.7 = bf16[4,768,256]{2,1,0:T(8,128)(2,1)} custom-call(s32[1]{0:T(128)} %bitcast.refs_0_, bf16[1024,2048]{1,0:T(8,128)(2,1)} %fusion.8.refs_1_, bf16[2048,1024]{1,0:T(8,128)(2,1)} %fusion.9.refs_2_, bf16[4,3,272,256]{3,2,1,0:T(8,128)(2,1)} %copy-done.6), custom_call_target="tpu_custom_call" | custom-call | flops 3221225472 | bytes 3145728 | tf_op jit(solution)/shard_map/hidden_units/pallas_call | solution.py:258
  711.6 6.9 block_out.4.refs_7_
  718.5 6.9 block_out.5.refs_7_
  725.4 8.3 %block_out.6.refs_4_ = bf16[4096,1024]{1,0:T(8,128)(2,1)} custom-call(s32[1]{0:T(128)} %bitcast.refs_0_, f32[1280,1024]{1,0:T(8,128)} %get-tuple-element.129.refs_1_, bf16[1024,1024]{1,0:T(8,128)(2,1)} %select_convert_fusion.refs_2_, bf16[1280,256]{1,0:T(8,128)(2,1)} %get-tuple-element.146.refs_3_, ...), custom_call_target="tpu_custom_call", output_to_operand_aliasing={{}: (7, {})} | custom-call | flops 2684354560 | bytes 10485760 | tf_op jit(solution)/shard_map/block_out/pallas_call | solution.py:288
  734.9 5.9 block_out.7
  (163 shorter events, 64.4 us)
Async XLA Ops:
  0.0 126.5 %copy-start = (bf16[16,128,64]{1,2,0:T(8,128)(2,1)S(1)}, bf16[16,128,64]{1,2,0:T(8,128)(2,1)}, u32[]{:S(2)}) copy-start(bf16[16,128,64]{1,2,0:T(8,128)(2,1)} %param.26) | copy-start | bytes 786436
  9.6 112.2 %all-to-all-start.1 = ((bf16[8,32,16,512]{3,2,1,0:T(8,128)(2,1)}), bf16[8,32,16,512]{3,2,1,0:T(8,128)(2,1)}, u32[]{:S(2)}, u32[]{:S(2)}) async-start(bf16[8,32,16,512]{3,2,1,0:T(8,128)(2,1)} %bitcast.62), calls=%async_computation.1 | async-start | bytes 8388608 | tf_op jit(solution)/shard_map/all_to_all | solution.py:409
  57.7 83.9 %collective-permute-start = (bf16[32,16,512]{2,1,0:T(8,128)(2,1)}, bf16[32,16,512]{2,1,0:T(8,128)(2,1)S(1)}, u32[]{:S(2)}, u32[]{:S(2)}) collective-permute-start(bf16[32,16,512]{2,1,0:T(8,128)(2,1)} %get-tuple-element.80), channel_id=1, source_target_pairs={{0,4},{4,0},{8,12},{12,8},{16,20},{20,16},{24,28},{28,24},{1,5},{5... | collective-permute-start | bytes 1572872 | tf_op jit(solution)/shard_map/ppermute | solution.py:46
  57.8 86.7 %collective-permute-start.6 = (bf16[32,16,512]{2,1,0:T(8,128)(2,1)}, bf16[32,16,512]{2,1,0:T(8,128)(2,1)S(1)}, u32[]{:S(2)}, u32[]{:S(2)}) collective-permute-start(bf16[32,16,512]{2,1,0:T(8,128)(2,1)} %get-tuple-element.86), channel_id=1, source_target_pairs={{0,28},{4,24},{8,20},{12,16},{16,12},{20,8},{24,4},{28,0},{1,29},{... | collective-permute-start | bytes 1572872 | tf_op jit(solution)/shard_map/ppermute | solution.py:46
  76.6 69.2 %collective-permute-start.7 = (bf16[32,16,512]{2,1,0:T(8,128)(2,1)}, bf16[32,16,512]{2,1,0:T(8,128)(2,1)S(1)}, u32[]{:S(2)}, u32[]{:S(2)}) collective-permute-start(bf16[32,16,512]{2,1,0:T(8,128)(2,1)} %get-tuple-element.88), channel_id=1, source_target_pairs={{0,4},{4,0},{8,12},{12,8},{16,20},{20,16},{24,28},{28,24},{1,5},{5... | collective-permute-start | bytes 1572872 | tf_op jit(solution)/shard_map/ppermute | solution.py:46
  76.7 71.2 %collective-permute-start.8 = (bf16[32,16,512]{2,1,0:T(8,128)(2,1)}, bf16[32,16,512]{2,1,0:T(8,128)(2,1)S(1)}, u32[]{:S(2)}, u32[]{:S(2)}) collective-permute-start(bf16[32,16,512]{2,1,0:T(8,128)(2,1)} %get-tuple-element.89), channel_id=1, source_target_pairs={{0,8},{4,12},{8,0},{12,4},{16,24},{20,28},{24,16},{28,20},{1,9},{5... | collective-permute-start | bytes 1572872 | tf_op jit(solution)/shard_map/ppermute | solution.py:46
  76.7 74.1 %collective-permute-start.9 = (bf16[32,16,512]{2,1,0:T(8,128)(2,1)}, bf16[32,16,512]{2,1,0:T(8,128)(2,1)S(1)}, u32[]{:S(2)}, u32[]{:S(2)}) collective-permute-start(bf16[32,16,512]{2,1,0:T(8,128)(2,1)} %get-tuple-element.90), channel_id=1, source_target_pairs={{0,12},{4,8},{8,4},{12,0},{16,28},{20,24},{24,20},{28,16},{1,13},{... | collective-permute-start | bytes 1572872 | tf_op jit(solution)/shard_map/ppermute | solution.py:46
  121.8 246.2 %all-to-all-start = ((bf16[8,32,16,512]{3,2,1,0:T(8,128)(2,1)}), bf16[8,32,16,512]{3,2,1,0:T(8,128)(2,1)}, u32[]{:S(2)}, u32[]{:S(2)}) async-start(bf16[8,32,16,512]{3,2,1,0:T(8,128)(2,1)} %bitcast.61), calls=%async_computation | async-start | bytes 8388608 | tf_op jit(solution)/shard_map/all_to_all | solution.py:409
  141.6 175.9 %copy-start.10 = (bf16[32,16,512]{2,1,0:T(8,128)(2,1)}, bf16[32,16,512]{2,1,0:T(8,128)(2,1)S(1)}, u32[]{:S(2)}) copy-start(bf16[32,16,512]{2,1,0:T(8,128)(2,1)S(1)} %collective-permute-done.refs_1_) | copy-start | bytes 1572868
  141.6 137.4 %collective-permute-start.10 = (bf16[32,16,512]{2,1,0:T(8,128)(2,1)}, bf16[32,16,512]{2,1,0:T(8,128)(2,1)S(1)}, u32[]{:S(2)}, u32[]{:S(2)}) collective-permute-start(bf16[32,16,512]{2,1,0:T(8,128)(2,1)} %get-tuple-element.91), channel_id=1, source_target_pairs={{0,16},{4,20},{8,24},{12,28},{16,0},{20,4},{24,8},{28,12},{1,17},{... | collective-permute-start | bytes 1572872 | tf_op jit(solution)/shard_map/ppermute | solution.py:46
  144.5 173.0 %copy-start.11 = (bf16[32,16,512]{2,1,0:T(8,128)(2,1)}, bf16[32,16,512]{2,1,0:T(8,128)(2,1)S(1)}, u32[]{:S(2)}) copy-start(bf16[32,16,512]{2,1,0:T(8,128)(2,1)S(1)} %collective-permute-done.6.refs_7_) | copy-start | bytes 1572868
  144.5 145.0 %collective-permute-start.11 = (bf16[32,16,512]{2,1,0:T(8,128)(2,1)}, bf16[32,16,512]{2,1,0:T(8,128)(2,1)}, u32[]{:S(2)}, u32[]{:S(2)}) collective-permute-start(bf16[32,16,512]{2,1,0:T(8,128)(2,1)} %get-tuple-element.92), channel_id=1, source_target_pairs={{0,20},{4,16},{8,28},{12,24},{16,4},{20,0},{24,12},{28,8},{1,21},{... | collective-permute-start | bytes 1572872 | tf_op jit(solution)/shard_map/ppermute | solution.py:46
  145.8 144.1 %collective-permute-start.12 = (bf16[32,16,512]{2,1,0:T(8,128)(2,1)}, bf16[32,16,512]{2,1,0:T(8,128)(2,1)}, u32[]{:S(2)}, u32[]{:S(2)}) collective-permute-start(bf16[32,16,512]{2,1,0:T(8,128)(2,1)} %get-tuple-element.93), channel_id=1, source_target_pairs={{0,24},{4,28},{8,16},{12,20},{16,8},{20,12},{24,0},{28,4},{1,25},{... | collective-permute-start | bytes 1572872 | tf_op jit(solution)/shard_map/ppermute | solution.py:46
  147.8 131.2 %copy-start.21 = (bf16[32,16,512]{2,1,0:T(8,128)(2,1)}, bf16[32,16,512]{2,1,0:T(8,128)(2,1)S(1)}, u32[]{:S(2)}) copy-start(bf16[32,16,512]{2,1,0:T(8,128)(2,1)S(1)} %collective-permute-done.8.refs_2_) | copy-start | bytes 1572868
  147.8 164.6 %collective-permute-start.13 = (bf16[32,16,512]{2,1,0:T(8,128)(2,1)}, bf16[32,16,512]{2,1,0:T(8,128)(2,1)}, u32[]{:S(2)}, u32[]{:S(2)}) collective-permute-start(bf16[32,16,512]{2,1,0:T(8,128)(2,1)} %get-tuple-element.94), channel_id=1, source_target_pairs={{0,28},{4,24},{8,20},{12,16},{16,12},{20,8},{24,4},{28,0},{1,29},{... | collective-permute-start | bytes 1572872 | tf_op jit(solution)/shard_map/ppermute | solution.py:46
  150.8 138.7 %copy-start.22 = (bf16[32,16,512]{2,1,0:T(8,128)(2,1)}, bf16[32,16,512]{2,1,0:T(8,128)(2,1)S(1)}, u32[]{:S(2)}) copy-start(bf16[32,16,512]{2,1,0:T(8,128)(2,1)S(1)} %collective-permute-done.9.refs_3_) | copy-start | bytes 1572868
  150.8 180.6 %collective-permute-start.1 = (bf16[32,16,512]{2,1,0:T(8,128)(2,1)}, bf16[32,16,512]{2,1,0:T(8,128)(2,1)S(1)}, u32[]{:S(2)}, u32[]{:S(2)}) collective-permute-start(bf16[32,16,512]{2,1,0:T(8,128)(2,1)} %get-tuple-element.81), channel_id=1, source_target_pairs={{0,8},{4,12},{8,0},{12,4},{16,24},{20,28},{24,16},{28,20},{1,9},{5... | collective-permute-start | bytes 1572872 | tf_op jit(solution)/shard_map/ppermute | solution.py:46
  279.0 52.4 %collective-permute-start.2 = (bf16[32,16,512]{2,1,0:T(8,128)(2,1)}, bf16[32,16,512]{2,1,0:T(8,128)(2,1)S(1)}, u32[]{:S(2)}, u32[]{:S(2)}) collective-permute-start(bf16[32,16,512]{2,1,0:T(8,128)(2,1)} %get-tuple-element.82), channel_id=1, source_target_pairs={{0,12},{4,8},{8,4},{12,0},{16,28},{20,24},{24,20},{28,16},{1,13},{... | collective-permute-start | bytes 1572872 | tf_op jit(solution)/shard_map/ppermute | solution.py:46
  289.5 68.2 %collective-permute-start.3 = (bf16[32,16,512]{2,1,0:T(8,128)(2,1)}, bf16[32,16,512]{2,1,0:T(8,128)(2,1)S(1)}, u32[]{:S(2)}, u32[]{:S(2)}) collective-permute-start(bf16[32,16,512]{2,1,0:T(8,128)(2,1)} %get-tuple-element.83), channel_id=1, source_target_pairs={{0,16},{4,20},{8,24},{12,28},{16,0},{20,4},{24,8},{28,12},{1,17},{... | collective-permute-start | bytes 1572872 | tf_op jit(solution)/shard_map/ppermute | solution.py:46
  289.9 78.0 %collective-permute-start.4 = (bf16[32,16,512]{2,1,0:T(8,128)(2,1)}, bf16[32,16,512]{2,1,0:T(8,128)(2,1)S(1)}, u32[]{:S(2)}, u32[]{:S(2)}) collective-permute-start(bf16[32,16,512]{2,1,0:T(8,128)(2,1)} %get-tuple-element.84), channel_id=1, source_target_pairs={{0,20},{4,16},{8,28},{12,24},{16,4},{20,0},{24,12},{28,8},{1,21},{... | collective-permute-start | bytes 1572872 | tf_op jit(solution)/shard_map/ppermute | solution.py:46
  312.4 55.6 %collective-permute-start.5 = (bf16[32,16,512]{2,1,0:T(8,128)(2,1)}, bf16[32,16,512]{2,1,0:T(8,128)(2,1)}, u32[]{:S(2)}, u32[]{:S(2)}) collective-permute-start(bf16[32,16,512]{2,1,0:T(8,128)(2,1)} %get-tuple-element.85), channel_id=1, source_target_pairs={{0,24},{4,28},{8,16},{12,20},{16,8},{20,12},{24,0},{28,4},{1,25},{... | collective-permute-start | bytes 1572872 | tf_op jit(solution)/shard_map/ppermute | solution.py:46
  331.4 36.6 %copy-start.15 = (bf16[32,16,512]{2,1,0:T(8,128)(2,1)}, bf16[32,16,512]{2,1,0:T(8,128)(2,1)S(1)}, u32[]{:S(2)}) copy-start(bf16[32,16,512]{2,1,0:T(8,128)(2,1)S(1)} %collective-permute-done.1.refs_2_) | copy-start | bytes 1572868
  331.4 36.6 %copy-start.17 = (bf16[32,16,512]{2,1,0:T(8,128)(2,1)}, bf16[32,16,512]{2,1,0:T(8,128)(2,1)S(1)}, u32[]{:S(2)}) copy-start(bf16[32,16,512]{2,1,0:T(8,128)(2,1)S(1)} %collective-permute-done.2.refs_3_) | copy-start | bytes 1572868
  444.7 52.8 %all-to-all-start.2 = ((bf16[8,4,32,1024]{3,2,1,0:T(8,128)(2,1)}), bf16[8,4,32,1024]{3,2,1,0:T(8,128)(2,1)S(1)}, u32[]{:S(2)}, u32[]{:S(2)}) async-start(bf16[8,4,32,1024]{3,2,1,0:T(8,128)(2,1)} %get-tuple-element.102), calls=%async_computation.2 | async-start | bytes 4194304 | tf_op jit(solution)/shard_map/all_to_all | solution.py:466
  457.2 15.7 %collective-permute-start.17 = (bf16[4,272,256]{2,1,0:T(8,128)(2,1)}, bf16[4,272,256]{2,1,0:T(8,128)(2,1)S(1)}, u32[]{:S(2)}, u32[]{:S(2)}) collective-permute-start(bf16[4,272,256]{2,1,0:T(8,128)(2,1)} %get-tuple-element.109), channel_id=1, source_target_pairs={{0,1},{1,0},{2,3},{3,2},{4,5},{5,4},{6,7},{7,6},{8,9},{9,8},{10,11... | collective-permute-start | bytes 1671176 | tf_op jit(solution)/shard_map/ppermute | solution.py:46
  458.7 26.8 %collective-permute-start.18 = (bf16[4,272,256]{2,1,0:T(8,128)(2,1)}, bf16[4,272,256]{2,1,0:T(8,128)(2,1)S(1)}, u32[]{:S(2)}, u32[]{:S(2)}) collective-permute-start(bf16[4,272,256]{2,1,0:T(8,128)(2,1)} %get-tuple-element.110), channel_id=1, source_target_pairs={{0,2},{1,3},{2,0},{3,1},{4,6},{5,7},{6,4},{7,5},{8,10},{9,11},{10,... | collective-permute-start | bytes 1671176 | tf_op jit(solution)/shard_map/ppermute | solution.py:46
  460.2 25.3 %collective-permute-start.19 = (bf16[4,272,256]{2,1,0:T(8,128)(2,1)}, bf16[4,272,256]{2,1,0:T(8,128)(2,1)S(1)}, u32[]{:S(2)}, u32[]{:S(2)}) collective-permute-start(bf16[4,272,256]{2,1,0:T(8,128)(2,1)} %get-tuple-element.111), channel_id=1, source_target_pairs={{0,3},{1,2},{2,1},{3,0},{4,7},{5,6},{6,5},{7,4},{8,11},{9,10},{10,... | collective-permute-start | bytes 1671176 | tf_op jit(solution)/shard_map/ppermute | solution.py:46
  498.8 63.9 %all-to-all-start.6 = ((bf16[8,5,32,1024]{3,2,1,0:T(8,128)(2,1)}), bf16[8,5,32,1024]{3,2,1,0:T(8,128)(2,1)S(1)}, u32[]{:S(2)}, u32[]{:S(2)}) async-start(bf16[8,5,32,1024]{3,2,1,0:T(8,128)(2,1)} %get-tuple-element.120), calls=%async_computation.6 | async-start | bytes 5242880 | tf_op jit(solution)/shard_map/all_to_all | solution.py:466
  511.2 15.7 %collective-permute-start.14 = (bf16[4,272,256]{2,1,0:T(8,128)(2,1)}, bf16[4,272,256]{2,1,0:T(8,128)(2,1)S(1)}, u32[]{:S(2)}, u32[]{:S(2)}) collective-permute-start(bf16[4,272,256]{2,1,0:T(8,128)(2,1)} %get-tuple-element.104), channel_id=1, source_target_pairs={{0,1},{1,0},{2,3},{3,2},{4,5},{5,4},{6,7},{7,6},{8,9},{9,8},{10,11... | collective-permute-start | bytes 1671176 | tf_op jit(solution)/shard_map/ppermute | solution.py:46
  512.7 26.9 %collective-permute-start.15 = (bf16[4,272,256]{2,1,0:T(8,128)(2,1)}, bf16[4,272,256]{2,1,0:T(8,128)(2,1)}, u32[]{:S(2)}, u32[]{:S(2)}) collective-permute-start(bf16[4,272,256]{2,1,0:T(8,128)(2,1)} %get-tuple-element.105), channel_id=1, source_target_pairs={{0,2},{1,3},{2,0},{3,1},{4,6},{5,7},{6,4},{7,5},{8,10},{9,11},{10,... | collective-permute-start | bytes 1671176 | tf_op jit(solution)/shard_map/ppermute | solution.py:46
  514.2 25.3 %collective-permute-start.16 = (bf16[4,272,256]{2,1,0:T(8,128)(2,1)}, bf16[4,272,256]{2,1,0:T(8,128)(2,1)}, u32[]{:S(2)}, u32[]{:S(2)}) collective-permute-start(bf16[4,272,256]{2,1,0:T(8,128)(2,1)} %get-tuple-element.106), channel_id=1, source_target_pairs={{0,3},{1,2},{2,1},{3,0},{4,7},{5,6},{6,5},{7,4},{8,11},{9,10},{10,... | collective-permute-start | bytes 1671176 | tf_op jit(solution)/shard_map/ppermute | solution.py:46
  526.9 35.8 %copy-start.29 = (bf16[4,272,256]{2,1,0:T(8,128)(2,1)}, bf16[4,272,256]{2,1,0:T(8,128)(2,1)S(1)}, u32[]{:S(2)}) copy-start(bf16[4,272,256]{2,1,0:T(8,128)(2,1)S(1)} %collective-permute-done.14.refs_4_) | copy-start | bytes 1671172
  562.7 48.0 %all-to-all-start.4 = ((bf16[8,3,32,1024]{3,2,1,0:T(8,128)(2,1)}), bf16[8,3,32,1024]{3,2,1,0:T(8,128)(2,1)}, u32[]{:S(2)}, u32[]{:S(2)}) async-start(bf16[8,3,32,1024]{3,2,1,0:T(8,128)(2,1)} %get-tuple-element.116), calls=%async_computation.4 | async-start | bytes 3145728 | tf_op jit(solution)/shard_map/all_to_all | solution.py:466
  567.0 16.8 %collective-permute-start.23 = (bf16[1024,256]{1,0:T(8,128)(2,1)}, bf16[1024,256]{1,0:T(8,128)(2,1)S(1)}, u32[]{:S(2)}, u32[]{:S(2)}) collective-permute-start(bf16[1024,256]{1,0:T(8,128)(2,1)} %get-tuple-element.113), channel_id=1, source_target_pairs={{0,1},{1,0},{2,3},{3,2},{4,5},{5,4},{6,7},{7,6},{8,9},{9,8},{10,11... | collective-permute-start | bytes 1572872 | tf_op jit(solution)/shard_map/ppermute | solution.py:46
  568.5 25.4 %collective-permute-start.24 = (bf16[1024,256]{1,0:T(8,128)(2,1)}, bf16[1024,256]{1,0:T(8,128)(2,1)}, u32[]{:S(2)}, u32[]{:S(2)}) collective-permute-start(bf16[1024,256]{1,0:T(8,128)(2,1)} %get-tuple-element.114), channel_id=1, source_target_pairs={{0,2},{1,3},{2,0},{3,1},{4,6},{5,7},{6,4},{7,5},{8,10},{9,11},{10,... | collective-permute-start | bytes 1572872 | tf_op jit(solution)/shard_map/ppermute | solution.py:46
  570.1 24.3 %collective-permute-start.25 = (bf16[1024,256]{1,0:T(8,128)(2,1)}, bf16[1024,256]{1,0:T(8,128)(2,1)}, u32[]{:S(2)}, u32[]{:S(2)}) collective-permute-start(bf16[1024,256]{1,0:T(8,128)(2,1)} %get-tuple-element.115), channel_id=1, source_target_pairs={{0,3},{1,2},{2,1},{3,0},{4,7},{5,6},{6,5},{7,4},{8,11},{9,10},{10,... | collective-permute-start | bytes 1572872 | tf_op jit(solution)/shard_map/ppermute | solution.py:46
  580.8 27.4 %collective-permute-start.20 = (bf16[5,272,256]{2,1,0:T(8,128)(2,1)}, bf16[5,272,256]{2,1,0:T(8,128)(2,1)S(1)}, u32[]{:S(2)}, u32[]{:S(2)}) collective-permute-start(bf16[5,272,256]{2,1,0:T(8,128)(2,1)} %get-tuple-element.122), channel_id=1, source_target_pairs={{0,1},{1,0},{2,3},{3,2},{4,5},{5,4},{6,7},{7,6},{8,9},{9,8},{10,11... | collective-permute-start | bytes 2088968 | tf_op jit(solution)/shard_map/ppermute | solution.py:46
  582.3 41.5 %collective-permute-start.21 = (bf16[5,272,256]{2,1,0:T(8,128)(2,1)}, bf16[5,272,256]{2,1,0:T(8,128)(2,1)}, u32[]{:S(2)}, u32[]{:S(2)}) collective-permute-start(bf16[5,272,256]{2,1,0:T(8,128)(2,1)} %get-tuple-element.123), channel_id=1, source_target_pairs={{0,2},{1,3},{2,0},{3,1},{4,6},{5,7},{6,4},{7,5},{8,10},{9,11},{10,... | collective-permute-start | bytes 2088968 | tf_op jit(solution)/shard_map/ppermute | solution.py:46
  583.8 40.4 %collective-permute-start.22 = (bf16[5,272,256]{2,1,0:T(8,128)(2,1)}, bf16[5,272,256]{2,1,0:T(8,128)(2,1)}, u32[]{:S(2)}, u32[]{:S(2)}) collective-permute-start(bf16[5,272,256]{2,1,0:T(8,128)(2,1)} %get-tuple-element.124), channel_id=1, source_target_pairs={{0,3},{1,2},{2,1},{3,0},{4,7},{5,6},{6,5},{7,4},{8,11},{9,10},{10,... | collective-permute-start | bytes 2088968 | tf_op jit(solution)/shard_map/ppermute | solution.py:46
  605.2 29.2 %collective-permute-start.26 = (bf16[1024,256]{1,0:T(8,128)(2,1)}, bf16[1024,256]{1,0:T(8,128)(2,1)S(1)}, u32[]{:S(2)}, u32[]{:S(2)}) collective-permute-start(bf16[1024,256]{1,0:T(8,128)(2,1)} %get-tuple-element.139), channel_id=1, source_target_pairs={{0,1},{1,0},{2,3},{3,2},{4,5},{5,4},{6,7},{7,6},{8,9},{9,8},{10,11... | collective-permute-start | bytes 1572872 | tf_op jit(solution)/shard_map/ppermute | solution.py:46
  606.7 48.4 %collective-permute-start.27 = (bf16[1024,256]{1,0:T(8,128)(2,1)}, bf16[1024,256]{1,0:T(8,128)(2,1)S(1)}, u32[]{:S(2)}, u32[]{:S(2)}) collective-permute-start(bf16[1024,256]{1,0:T(8,128)(2,1)} %get-tuple-element.140), channel_id=1, source_target_pairs={{0,2},{1,3},{2,0},{3,1},{4,6},{5,7},{6,4},{7,5},{8,10},{9,11},{10,... | collective-permute-start | bytes 1572872 | tf_op jit(solution)/shard_map/ppermute | solution.py:46
  608.2 47.0 %collective-permute-start.28 = (bf16[1024,256]{1,0:T(8,128)(2,1)}, bf16[1024,256]{1,0:T(8,128)(2,1)S(1)}, u32[]{:S(2)}, u32[]{:S(2)}) collective-permute-start(bf16[1024,256]{1,0:T(8,128)(2,1)} %get-tuple-element.141), channel_id=1, source_target_pairs={{0,3},{1,2},{2,1},{3,0},{4,7},{5,6},{6,5},{7,4},{8,11},{9,10},{10,... | collective-permute-start | bytes 1572872 | tf_op jit(solution)/shard_map/ppermute | solution.py:46
  617.6 54.2 %all-to-all-start.5 = ((bf16[4,3,272,256]{3,2,1,0:T(8,128)(2,1)}), bf16[4,3,272,256]{3,2,1,0:T(8,128)(2,1)S(1)}, u32[]{:S(2)}, u32[]{:S(2)}) async-start(bf16[4,3,272,256]{3,2,1,0:T(8,128)(2,1)} %get-tuple-element.118), calls=%async_computation.5 | async-start | bytes 3342336 | tf_op jit(solution)/shard_map/all_to_all | solution.py:51
  634.4 33.5 %copy-start.13 = (bf16[1024,256]{1,0:T(8,128)(2,1)}, bf16[1024,256]{1,0:T(8,128)(2,1)S(1)}, u32[]{:S(2)}) copy-start(bf16[1024,256]{1,0:T(8,128)(2,1)S(1)} %collective-permute-done.26.refs_4_) | copy-start | bytes 1572868
  667.9 16.9 %collective-permute-start.29 = (bf16[1280,256]{1,0:T(8,128)(2,1)}, bf16[1280,256]{1,0:T(8,128)(2,1)S(1)}, u32[]{:S(2)}, u32[]{:S(2)}) collective-permute-start(bf16[1280,256]{1,0:T(8,128)(2,1)} %get-tuple-element.147), channel_id=1, source_target_pairs={{0,1},{1,0},{2,3},{3,2},{4,5},{5,4},{6,7},{7,6},{8,9},{9,8},{10,11... | collective-permute-start | bytes 1966088 | tf_op jit(solution)/shard_map/ppermute | solution.py:46
  668.0 28.8 %collective-permute-start.30 = (bf16[1280,256]{1,0:T(8,128)(2,1)}, bf16[1280,256]{1,0:T(8,128)(2,1)S(1)}, u32[]{:S(2)}, u32[]{:S(2)}) collective-permute-start(bf16[1280,256]{1,0:T(8,128)(2,1)} %get-tuple-element.148), channel_id=1, source_target_pairs={{0,2},{1,3},{2,0},{3,1},{4,6},{5,7},{6,4},{7,5},{8,10},{9,11},{10,... | collective-permute-start | bytes 1966088 | tf_op jit(solution)/shard_map/ppermute | solution.py:46
  670.5 28.2 %collective-permute-start.31 = (bf16[1280,256]{1,0:T(8,128)(2,1)}, bf16[1280,256]{1,0:T(8,128)(2,1)}, u32[]{:S(2)}, u32[]{:S(2)}) collective-permute-start(bf16[1280,256]{1,0:T(8,128)(2,1)} %get-tuple-element.149), channel_id=1, source_target_pairs={{0,3},{1,2},{2,1},{3,0},{4,7},{5,6},{6,5},{7,4},{8,11},{9,10},{10,... | collective-permute-start | bytes 1966088 | tf_op jit(solution)/shard_map/ppermute | solution.py:46
  708.0 25.7 %all-to-all-start.7 = ((bf16[4,768,256]{2,1,0:T(8,128)(2,1)}), bf16[4,768,256]{2,1,0:T(8,128)(2,1)S(1)}, u32[]{:S(2)}, u32[]{:S(2)}) async-start(bf16[4,768,256]{2,1,0:T(8,128)(2,1)} %hidden_units.7), calls=%async_computation.7 | async-start | bytes 3145728 | tf_op jit(solution)/shard_map/all_to_all | solution.py:51
  (26 other events, 263.5 us)

commit v5 on v4

--- a/solution.py
+++ b/solution.py
@@ -15,7 +15,7 @@
 BF = jnp.bfloat16
 F32 = jnp.float32
 
-RETURN_SPLIT = (4, 4, 5, 3)
+RETURN_SPLIT = (5, 4, 4, 3)
 
 
 def cost(flops, moved, exps=0):

time: 746 us -> 739 us (level)
  waiting for transfers between devices: 354 us -> 334 us
  blocking collectives: 78.9 us -> 90.1 us
    all_to_all x3, waiting for transfers between devices: 34.1 us -> 15.3 us  [shards(): home = lax.all_to_all(sent, 'ctx', split_axis=0, concat_axis=0, tiled=True)]
    all_to_all x1, blocking collectives: 62.1 us -> 73.3 us  [shards(): home = lax.all_to_all(sent, 'ctx', split_axis=0, concat_axis=0, tiled=True)]
  transfers between devices with their start and end apart: 39 -> 39, of which waited for: 21 -> 17; matrix products, arithmetic and copies ran while one was open for 5% -> 5% of each run, Pallas kernels for 18% -> 18%
where the time goes in v5:
time: 739 us; the launch traced here: 734 us
  waiting for transfers between devices  334 us (45%)
  Pallas kernels  164 us (22%)
  starting transfers between devices  92.5 us (13%)
  blocking collectives  90.1 us (12%)
  local copies, waits for them, and re-layouts  28.6 us (4%)
  matrix products  12.6 us (2%)
  other arithmetic  11.1 us (2%)
    ppermute x32, waiting for transfers between devices, swap(): return lax.ppermute(x, name, [(i, i ^ d) for i in range(size)])  284 us
    all_to_all x1, blocking collectives, shards(): home = lax.all_to_all(sent, 'ctx', split_axis=0, concat_axis=0, tiled=True)  73.3 us
    ppermute x32, starting transfers between devices, swap(): return lax.ppermute(x, name, [(i, i ^ d) for i in range(size)])  62.3 us
    pallas_call x4, Pallas kernels, hidden(): pl.pallas_call(lambda *refs: hidden_kernel(groups, total, halves, *refs),...  43.9 us
    pallas_call x4, Pallas kernels, mix(): pl.pallas_call(lambda *refs: mix_kernel(groups, *refs), grid=(size,), in_...  34.5 us
    all_to_all x2, waiting for transfers between devices, shards(): lax.all_to_all(sent, 'ctx', split_axis=0, concat_axis=0, tiled=True)  34.4 us
    pallas_call x2, Pallas kernels, inner(): pl.pallas_call(lambda *refs: inner_kernel(parts, *refs), grid=(chans // c...  29.7 us
    pallas_call x4, Pallas kernels, final(): pl.pallas_call(lambda *refs: final_kernel(groups, *refs), grid=(count //...  28 us
  transfers between devices with their start and end apart: 39, of which 17 were waited for; matrix products, arithmetic and copies ran while one was open for 5% of the time, Pallas kernels for 18%

profile of v5, /device:TPU:0, one launch (start us, length us, event | category | flops | bytes accessed | tf_op | source)
XLA Modules:
  0.0 733.6 jit_solution(9886562769377918901)
XLA Ops:
  0.0 5.2 fusion.202
  5.2 4.4 copy.31
  9.6 6.3 all-to-all-start.1
  16.0 5.1 multiply_reduce_fusion
  21.1 16.8 %psum.7 = f32[4096]{0:T(1024)S(1)} all-reduce(f32[4096]{0:T(1024)S(1)} %multiply_reduce_fusion), channel_id=1, replica_groups=mesh['ctx'=8,'hid'=4] {'hid'}, use_global_device_ids=true, to_apply=%region_1.0 | all-reduce | flops 4096 | bytes 32768 | tf_op jit(solution)/shard_map/psum | solution.py:412
  42.9 14.9 %inner_mix.2 = (bf16[32,16,512]{2,1,0:T(8,128)(2,1)}, bf16[32,16,512]{2,1,0:T(8,128)(2,1)}, bf16[32,16,512]{2,1,0:T(8,128)(2,1)}, bf16[32,16,512]{2,1,0:T(8,128)...) custom-call(bf16[4096,1024]{1,0:T(8,128)(2,1)} %bitcast.55, ...), custom_call_target="tpu_custom_call" | custom-call | flops 1073741824 | bytes 8388608 | tf_op jit(solution)/shard_map/inner_mix/pallas_call | solution.py:78
  57.8 3.9 collective-permute-start.6
  61.7 14.8 %inner_mix.3 = (bf16[32,16,512]{2,1,0:T(8,128)(2,1)}, bf16[32,16,512]{2,1,0:T(8,128)(2,1)}, bf16[32,16,512]{2,1,0:T(8,128)(2,1)}, bf16[32,16,512]{2,1,0:T(8,128)...) custom-call(bf16[4096,1024]{1,0:T(8,128)(2,1)} %bitcast.56, ...), custom_call_target="tpu_custom_call" | custom-call | flops 1073741824 | bytes 8388608 | tf_op jit(solution)/shard_map/inner_mix/pallas_call | solution.py:78
  78.5 6.5 copy.28
  87.4 34.4 %all-to-all-done.1.refs_8_ = bf16[8,32,16,512]{3,2,1,0:T(8,128)(2,1)} async-done(((bf16[8,32,16,512]{3,2,1,0:T(8,128)(2,1)}), bf16[8,32,16,512]{3,2,1,0:T(8,128)(2,1)}, u32[]{:S(2)}, u32[]{:S(2)}) %all-to-all-start.1) | async-done | bytes 4194336 | tf_op jit(solution)/shard_map/all_to_all | solution.py:409
  121.8 4.7 all-to-all-start
  126.6 3.8 fusion.9.refs_2_
  130.9 5.0 fusion.8.refs_1_
  135.9 3.7 select_convert_fusion.refs_2_
  150.9 128.1 %collective-permute-done.10.refs_4_ = bf16[32,16,512]{2,1,0:T(8,128)(2,1)S(1)} collective-permute-done((bf16[32,16,512]{2,1,0:T(8,128)(2,1)}, bf16[32,16,512]{2,1,0:T(8,128)(2,1)S(1)}, u32[]{:S(2)}, u32[]{:S(2)}) %collective-permute-start.10) | collective-permute-done | bytes 524320 | tf_op jit(solution)/shard_map/ppermute | solution.py:46
  279.0 10.5 %collective-permute-done.11.refs_5_ = bf16[32,16,512]{2,1,0:T(8,128)(2,1)} collective-permute-done((bf16[32,16,512]{2,1,0:T(8,128)(2,1)}, bf16[32,16,512]{2,1,0:T(8,128)(2,1)}, u32[]{:S(2)}, u32[]{:S(2)}) %collective-permute-start.11) | collective-permute-done | bytes 524320 | tf_op jit(solution)/shard_map/ppermute | solution.py:46
  289.9 22.5 %collective-permute-start.4 = (bf16[32,16,512]{2,1,0:T(8,128)(2,1)}, bf16[32,16,512]{2,1,0:T(8,128)(2,1)S(1)}, u32[]{:S(2)}, u32[]{:S(2)}) collective-permute-start(bf16[32,16,512]{2,1,0:T(8,128)(2,1)} %get-tuple-element.84), channel_id=1, source_target_pairs={{0,20},{4,16},{8,28},{12,24},{16,4},{20,0},{24,12},{28,8},{1,21},{... | collective-permute-start | bytes 1572872 | tf_op jit(solution)/shard_map/ppermute | solution.py:46
  317.6 13.9 %outer_mix.2 = (bf16[8,5,32,1024]{3,2,1,0:T(8,128)(2,1)}, bf16[8,4,32,1024]{3,2,1,0:T(8,128)(2,1)}, bf16[8,4,32,1024]{3,2,1,0:T(8,128)(2,1)}, bf16[8,3,32,1024]{3,2,1,0:T(8,128)(2,1)}) custom-call(bf16[32,16,512]{2,1,0:T(8,128)(2,1)} %get-tuple-element.87.refs_0_, bf16[32,16,512]{2,1,0:T(8,128)(2,1)} %copy-done.21, bf16[32,16,512]{2,1,0:T(8,128)(2,1)} %copy-done.22, ...), custom_call_target="tpu_custom_call" | custom-call | flops 2147483648 | bytes 12582912 | tf_op jit(solution)/shard_map/outer_mix/pallas_call | solution.py:132
  331.5 26.2 %collective-permute-done.3.refs_4_ = bf16[32,16,512]{2,1,0:T(8,128)(2,1)S(1)} collective-permute-done((bf16[32,16,512]{2,1,0:T(8,128)(2,1)}, bf16[32,16,512]{2,1,0:T(8,128)(2,1)S(1)}, u32[]{:S(2)}, u32[]{:S(2)}) %collective-permute-start.3) | collective-permute-done | bytes 524320 | tf_op jit(solution)/shard_map/ppermute | solution.py:46
  357.7 10.3 %collective-permute-done.4.refs_5_ = bf16[32,16,512]{2,1,0:T(8,128)(2,1)S(1)} collective-permute-done((bf16[32,16,512]{2,1,0:T(8,128)(2,1)}, bf16[32,16,512]{2,1,0:T(8,128)(2,1)S(1)}, u32[]{:S(2)}, u32[]{:S(2)}) %collective-permute-start.4) | collective-permute-done | bytes 524320 | tf_op jit(solution)/shard_map/ppermute | solution.py:46
  368.8 13.9 %outer_mix.3 = (bf16[8,5,32,1024]{3,2,1,0:T(8,128)(2,1)}, bf16[8,4,32,1024]{3,2,1,0:T(8,128)(2,1)}, bf16[8,4,32,1024]{3,2,1,0:T(8,128)(2,1)}, bf16[8,3,32,1024]{3,2,1,0:T(8,128)(2,1)}) custom-call(bf16[32,16,512]{2,1,0:T(8,128)(2,1)} %get-tuple-element.79.refs_0_, ...), custom_call_target="tpu_custom_call", output_to_operand_aliasing={{0}: (12, {}), {1}: (13, {}), {2}: (14, {}), {3}: (15, {})} | custom-call | flops 2147483648 | bytes 12582912 | tf_op jit(solution)/shard_map/outer_mix/pallas_call | solution.py:132
  382.6 73.3 %all_to_all.40.refs_1_ = bf16[8,5,32,1024]{3,2,1,0:T(8,128)(2,1)} all-to-all(bf16[8,5,32,1024]{3,2,1,0:T(8,128)(2,1)} %get-tuple-element.107), channel_id=1, replica_groups=mesh['ctx'=8,'hid'=4] {'ctx'}, dimensions={0} | all-to-all | bytes 5242880 | tf_op jit(solution)/shard_map/all_to_all | solution.py:466
  456.0 3.8 all-to-all-start.2
  459.8 10.2 %mix_tokens.5 = (f32[1280,1024]{1,0:T(8,128)}, bf16[5,272,256]{2,1,0:T(8,128)(2,1)}, bf16[5,272,256]{2,1,0:T(8,128)(2,1)}, bf16[5,272,256]{2,1,0:T(8,128)(2,1)}, bf16[5,272,256]{2,1,0:T(8,128)(2,1)}) custom-call(s32[1]{0:T(128)} %bitcast.refs_0_, bf16[8,5,32,1024]{3,2,1,0:T(8,128)(2,1)} %all_to_all.40.refs_1_, bf16[4096,1024]{1,0:T(8,128)(2,1)} %bitcast.57, ...), custom_call_target="tpu_custom_call" | custom-call | flops 3355443200 | bytes 13107200 | tf_op jit(solution)/shard_map/mix_tokens/pallas_call | solution.py:204
  473.5 15.1 %collective-permute-done.17.refs_4_ = bf16[5,272,256]{2,1,0:T(8,128)(2,1)S(1)} collective-permute-done((bf16[5,272,256]{2,1,0:T(8,128)(2,1)}, bf16[5,272,256]{2,1,0:T(8,128)(2,1)S(1)}, u32[]{:S(2)}, u32[]{:S(2)}) %collective-permute-start.17) | collective-permute-done | bytes 696352 | tf_op jit(solution)/shard_map/ppermute | solution.py:46
  488.6 15.7 %collective-permute-done.18.refs_5_ = bf16[5,272,256]{2,1,0:T(8,128)(2,1)S(1)} collective-permute-done((bf16[5,272,256]{2,1,0:T(8,128)(2,1)}, bf16[5,272,256]{2,1,0:T(8,128)(2,1)S(1)}, u32[]{:S(2)}, u32[]{:S(2)}) %collective-permute-start.18) | collective-permute-done | bytes 696352 | tf_op jit(solution)/shard_map/ppermute | solution.py:46
  510.1 3.6 all-to-all-start.6
  513.8 8.7 %mix_tokens.4 = (f32[1024,1024]{1,0:T(8,128)}, bf16[4,272,256]{2,1,0:T(8,128)(2,1)}, bf16[4,272,256]{2,1,0:T(8,128)(2,1)}, bf16[4,272,256]{2,1,0:T(8,128)(2,1)}, bf16[4,272,256]{2,1,0:T(8,128)(2,1)}) custom-call(s32[1]{0:T(128)} %bitcast.refs_0_, bf16[8,4,32,1024]{3,2,1,0:T(8,128)(2,1)} %copy-done.3, bf16[4096,1024]{1,0:T(8,128)(2,1)} %bitcast.58, ...), custom_call_target="tpu_custom_call" | custom-call | flops 2684354560 | bytes 10485760 | tf_op jit(solution)/shard_map/mix_tokens/pallas_call | solution.py:204
  526.0 12.4 %hidden_units.4 = (bf16[1280,256]{1,0:T(8,128)(2,1)}, bf16[1280,256]{1,0:T(8,128)(2,1)}, bf16[1280,256]{1,0:T(8,128)(2,1)}, bf16[1280,256]{1,0:T(8,128)(2,1)}) custom-call(s32[1]{0:T(128)} %bitcast.refs_0_, bf16[1024,2048]{1,0:T(8,128)(2,1)} %fusion.8.refs_1_, bf16[2048,1024]{1,0:T(8,128)(2,1)} %fusion.9.refs_2_, ...), custom_call_target="tpu_custom_call" | custom-call | flops 5368709120 | bytes 5242880 | tf_op jit(solution)/shard_map/hidden_units/pallas_call | solution.py:258
  538.4 12.5 %collective-permute-done.15.refs_5_ = bf16[4,272,256]{2,1,0:T(8,128)(2,1)} collective-permute-done((bf16[4,272,256]{2,1,0:T(8,128)(2,1)}, bf16[4,272,256]{2,1,0:T(8,128)(2,1)}, u32[]{:S(2)}, u32[]{:S(2)}) %collective-permute-start.15) | collective-permute-done | bytes 557088 | tf_op jit(solution)/shard_map/ppermute | solution.py:46
  550.9 11.9 %all-to-all-done.6.refs_1_ = bf16[8,4,32,1024]{3,2,1,0:T(8,128)(2,1)S(1)} async-done(((bf16[8,4,32,1024]{3,2,1,0:T(8,128)(2,1)}), bf16[8,4,32,1024]{3,2,1,0:T(8,128)(2,1)S(1)}, u32[]{:S(2)}, u32[]{:S(2)}) %all-to-all-start.6) | async-done | bytes 2097184 | tf_op jit(solution)/shard_map/all_to_all | solution.py:466
  562.7 4.3 all-to-all-start.4
  570.6 8.7 %mix_tokens.7 = (f32[1024,1024]{1,0:T(8,128)}, bf16[4,272,256]{2,1,0:T(8,128)(2,1)}, bf16[4,272,256]{2,1,0:T(8,128)(2,1)}, bf16[4,272,256]{2,1,0:T(8,128)(2,1)}, bf16[4,272,256]{2,1,0:T(8,128)(2,1)}) custom-call(s32[1]{0:T(128)} %bitcast.refs_0_, bf16[8,4,32,1024]{3,2,1,0:T(8,128)(2,1)} %copy-done.2, bf16[4096,1024]{1,0:T(8,128)(2,1)} %bitcast.59, ...), custom_call_target="tpu_custom_call" | custom-call | flops 2684354560 | bytes 10485760 | tf_op jit(solution)/shard_map/mix_tokens/pallas_call | solution.py:204
  587.3 13.2 %collective-permute-done.24.refs_5_ = bf16[1280,256]{1,0:T(8,128)(2,1)} collective-permute-done((bf16[1280,256]{1,0:T(8,128)(2,1)}, bf16[1280,256]{1,0:T(8,128)(2,1)}, u32[]{:S(2)}, u32[]{:S(2)}) %collective-permute-start.24) | collective-permute-done | bytes 655392 | tf_op jit(solution)/shard_map/ppermute | solution.py:46
  600.6 10.8 %hidden_units.5 = (bf16[1024,256]{1,0:T(8,128)(2,1)}, bf16[1024,256]{1,0:T(8,128)(2,1)}, bf16[1024,256]{1,0:T(8,128)(2,1)}, bf16[1024,256]{1,0:T(8,128)(2,1)}) custom-call(s32[1]{0:T(128)} %bitcast.refs_0_, bf16[1024,2048]{1,0:T(8,128)(2,1)} %fusion.8.refs_1_, bf16[2048,1024]{1,0:T(8,128)(2,1)} %fusion.9.refs_2_, ...), custom_call_target="tpu_custom_call" | custom-call | flops 4294967296 | bytes 4194304 | tf_op jit(solution)/shard_map/hidden_units/pallas_call | solution.py:258
  615.0 6.9 mix_tokens.6
  621.9 3.8 all-to-all-start.5
  625.8 8.4 %collective-permute-done.26.refs_4_ = bf16[1024,256]{1,0:T(8,128)(2,1)S(1)} collective-permute-done((bf16[1024,256]{1,0:T(8,128)(2,1)}, bf16[1024,256]{1,0:T(8,128)(2,1)S(1)}, u32[]{:S(2)}, u32[]{:S(2)}) %collective-permute-start.26) | collective-permute-done | bytes 524320 | tf_op jit(solution)/shard_map/ppermute | solution.py:46
  634.1 20.8 %collective-permute-done.27.refs_5_ = bf16[1024,256]{1,0:T(8,128)(2,1)S(1)} collective-permute-done((bf16[1024,256]{1,0:T(8,128)(2,1)}, bf16[1024,256]{1,0:T(8,128)(2,1)S(1)}, u32[]{:S(2)}, u32[]{:S(2)}) %collective-permute-start.27) | collective-permute-done | bytes 524320 | tf_op jit(solution)/shard_map/ppermute | solution.py:46
  654.9 11.1 %hidden_units.6 = (bf16[1024,256]{1,0:T(8,128)(2,1)}, bf16[1024,256]{1,0:T(8,128)(2,1)}, bf16[1024,256]{1,0:T(8,128)(2,1)}, bf16[1024,256]{1,0:T(8,128)(2,1)}) custom-call(s32[1]{0:T(128)} %bitcast.refs_0_, bf16[1024,2048]{1,0:T(8,128)(2,1)} %fusion.8.refs_1_, bf16[2048,1024]{1,0:T(8,128)(2,1)} %fusion.9.refs_2_, ...), custom_call_target="tpu_custom_call" | custom-call | flops 4294967296 | bytes 4194304 | tf_op jit(solution)/shard_map/hidden_units/pallas_call | solution.py:258
  670.0 11.2 %collective-permute-done.29.refs_4_ = bf16[1024,256]{1,0:T(8,128)(2,1)S(1)} collective-permute-done((bf16[1024,256]{1,0:T(8,128)(2,1)}, bf16[1024,256]{1,0:T(8,128)(2,1)S(1)}, u32[]{:S(2)}, u32[]{:S(2)}) %collective-permute-start.29) | collective-permute-done | bytes 524320 | tf_op jit(solution)/shard_map/ppermute | solution.py:46
  682.8 8.3 %collective-permute-done.31.refs_6_ = bf16[1024,256]{1,0:T(8,128)(2,1)S(1)} collective-permute-done((bf16[1024,256]{1,0:T(8,128)(2,1)}, bf16[1024,256]{1,0:T(8,128)(2,1)S(1)}, u32[]{:S(2)}, u32[]{:S(2)}) %collective-permute-start.31) | collective-permute-done | bytes 524320 | tf_op jit(solution)/shard_map/ppermute | solution.py:46
  691.1 9.5 %hidden_units.7 = bf16[4,768,256]{2,1,0:T(8,128)(2,1)} custom-call(s32[1]{0:T(128)} %bitcast.refs_0_, bf16[1024,2048]{1,0:T(8,128)(2,1)} %fusion.8.refs_1_, bf16[2048,1024]{1,0:T(8,128)(2,1)} %fusion.9.refs_2_, bf16[4,3,272,256]{3,2,1,0:T(8,128)(2,1)} %copy-done.6), custom_call_target="tpu_custom_call" | custom-call | flops 3221225472 | bytes 3145728 | tf_op jit(solution)/shard_map/hidden_units/pallas_call | solution.py:258
  700.6 3.6 all-to-all-start.7
  704.2 8.3 %block_out.4.refs_7_ = bf16[4096,1024]{1,0:T(8,128)(2,1)} custom-call(s32[1]{0:T(128)} %bitcast.refs_0_, f32[1280,1024]{1,0:T(8,128)} %get-tuple-element.152.refs_1_, bf16[1024,1024]{1,0:T(8,128)(2,1)} %select_convert_fusion.refs_2_, bf16[1280,256]{1,0:T(8,128)(2,1)} %get-tuple-element.112.refs_3_, bf16[1280,256]{1,0:T(8,128)(2,1)} %copy-done.7, ...), custom_call_target="tpu_custom_call" | custom-call | flops 2684354560 | bytes 10485760 | tf_op jit(solution)/shard_map/block_out/pallas_call | solution.py:288
  712.5 6.9 block_out.5.refs_7_
  719.4 6.9 block_out.6.refs_4_
  727.5 5.9 block_out.7
  (163 shorter events, 62.0 us)
Async XLA Ops:
  0.0 126.5 %copy-start = (bf16[16,128,64]{1,2,0:T(8,128)(2,1)S(1)}, bf16[16,128,64]{1,2,0:T(8,128)(2,1)}, u32[]{:S(2)}) copy-start(bf16[16,128,64]{1,2,0:T(8,128)(2,1)} %param.26) | copy-start | bytes 786436
  9.6 112.2 %all-to-all-start.1 = ((bf16[8,32,16,512]{3,2,1,0:T(8,128)(2,1)}), bf16[8,32,16,512]{3,2,1,0:T(8,128)(2,1)}, u32[]{:S(2)}, u32[]{:S(2)}) async-start(bf16[8,32,16,512]{3,2,1,0:T(8,128)(2,1)} %bitcast.62), calls=%async_computation.1 | async-start | bytes 8388608 | tf_op jit(solution)/shard_map/all_to_all | solution.py:409
  57.7 83.9 %collective-permute-start = (bf16[32,16,512]{2,1,0:T(8,128)(2,1)}, bf16[32,16,512]{2,1,0:T(8,128)(2,1)S(1)}, u32[]{:S(2)}, u32[]{:S(2)}) collective-permute-start(bf16[32,16,512]{2,1,0:T(8,128)(2,1)} %get-tuple-element.80), channel_id=1, source_target_pairs={{0,4},{4,0},{8,12},{12,8},{16,20},{20,16},{24,28},{28,24},{1,5},{5... | collective-permute-start | bytes 1572872 | tf_op jit(solution)/shard_map/ppermute | solution.py:46
  57.8 86.7 %collective-permute-start.6 = (bf16[32,16,512]{2,1,0:T(8,128)(2,1)}, bf16[32,16,512]{2,1,0:T(8,128)(2,1)S(1)}, u32[]{:S(2)}, u32[]{:S(2)}) collective-permute-start(bf16[32,16,512]{2,1,0:T(8,128)(2,1)} %get-tuple-element.86), channel_id=1, source_target_pairs={{0,28},{4,24},{8,20},{12,16},{16,12},{20,8},{24,4},{28,0},{1,29},{... | collective-permute-start | bytes 1572872 | tf_op jit(solution)/shard_map/ppermute | solution.py:46
  76.6 69.2 %collective-permute-start.7 = (bf16[32,16,512]{2,1,0:T(8,128)(2,1)}, bf16[32,16,512]{2,1,0:T(8,128)(2,1)S(1)}, u32[]{:S(2)}, u32[]{:S(2)}) collective-permute-start(bf16[32,16,512]{2,1,0:T(8,128)(2,1)} %get-tuple-element.88), channel_id=1, source_target_pairs={{0,4},{4,0},{8,12},{12,8},{16,20},{20,16},{24,28},{28,24},{1,5},{5... | collective-permute-start | bytes 1572872 | tf_op jit(solution)/shard_map/ppermute | solution.py:46
  76.7 71.2 %collective-permute-start.8 = (bf16[32,16,512]{2,1,0:T(8,128)(2,1)}, bf16[32,16,512]{2,1,0:T(8,128)(2,1)S(1)}, u32[]{:S(2)}, u32[]{:S(2)}) collective-permute-start(bf16[32,16,512]{2,1,0:T(8,128)(2,1)} %get-tuple-element.89), channel_id=1, source_target_pairs={{0,8},{4,12},{8,0},{12,4},{16,24},{20,28},{24,16},{28,20},{1,9},{5... | collective-permute-start | bytes 1572872 | tf_op jit(solution)/shard_map/ppermute | solution.py:46
  76.7 74.1 %collective-permute-start.9 = (bf16[32,16,512]{2,1,0:T(8,128)(2,1)}, bf16[32,16,512]{2,1,0:T(8,128)(2,1)S(1)}, u32[]{:S(2)}, u32[]{:S(2)}) collective-permute-start(bf16[32,16,512]{2,1,0:T(8,128)(2,1)} %get-tuple-element.90), channel_id=1, source_target_pairs={{0,12},{4,8},{8,4},{12,0},{16,28},{20,24},{24,20},{28,16},{1,13},{... | collective-permute-start | bytes 1572872 | tf_op jit(solution)/shard_map/ppermute | solution.py:46
  121.8 246.2 %all-to-all-start = ((bf16[8,32,16,512]{3,2,1,0:T(8,128)(2,1)}), bf16[8,32,16,512]{3,2,1,0:T(8,128)(2,1)}, u32[]{:S(2)}, u32[]{:S(2)}) async-start(bf16[8,32,16,512]{3,2,1,0:T(8,128)(2,1)} %bitcast.61), calls=%async_computation | async-start | bytes 8388608 | tf_op jit(solution)/shard_map/all_to_all | solution.py:409
  141.6 175.9 %copy-start.9 = (bf16[32,16,512]{2,1,0:T(8,128)(2,1)}, bf16[32,16,512]{2,1,0:T(8,128)(2,1)S(1)}, u32[]{:S(2)}) copy-start(bf16[32,16,512]{2,1,0:T(8,128)(2,1)S(1)} %collective-permute-done.refs_1_) | copy-start | bytes 1572868
  141.6 137.4 %collective-permute-start.10 = (bf16[32,16,512]{2,1,0:T(8,128)(2,1)}, bf16[32,16,512]{2,1,0:T(8,128)(2,1)S(1)}, u32[]{:S(2)}, u32[]{:S(2)}) collective-permute-start(bf16[32,16,512]{2,1,0:T(8,128)(2,1)} %get-tuple-element.91), channel_id=1, source_target_pairs={{0,16},{4,20},{8,24},{12,28},{16,0},{20,4},{24,8},{28,12},{1,17},{... | collective-permute-start | bytes 1572872 | tf_op jit(solution)/shard_map/ppermute | solution.py:46
  144.5 173.0 %copy-start.10 = (bf16[32,16,512]{2,1,0:T(8,128)(2,1)}, bf16[32,16,512]{2,1,0:T(8,128)(2,1)S(1)}, u32[]{:S(2)}) copy-start(bf16[32,16,512]{2,1,0:T(8,128)(2,1)S(1)} %collective-permute-done.6.refs_7_) | copy-start | bytes 1572868
  144.5 145.0 %collective-permute-start.11 = (bf16[32,16,512]{2,1,0:T(8,128)(2,1)}, bf16[32,16,512]{2,1,0:T(8,128)(2,1)}, u32[]{:S(2)}, u32[]{:S(2)}) collective-permute-start(bf16[32,16,512]{2,1,0:T(8,128)(2,1)} %get-tuple-element.92), channel_id=1, source_target_pairs={{0,20},{4,16},{8,28},{12,24},{16,4},{20,0},{24,12},{28,8},{1,21},{... | collective-permute-start | bytes 1572872 | tf_op jit(solution)/shard_map/ppermute | solution.py:46
  145.8 144.1 %collective-permute-start.12 = (bf16[32,16,512]{2,1,0:T(8,128)(2,1)}, bf16[32,16,512]{2,1,0:T(8,128)(2,1)}, u32[]{:S(2)}, u32[]{:S(2)}) collective-permute-start(bf16[32,16,512]{2,1,0:T(8,128)(2,1)} %get-tuple-element.93), channel_id=1, source_target_pairs={{0,24},{4,28},{8,16},{12,20},{16,8},{20,12},{24,0},{28,4},{1,25},{... | collective-permute-start | bytes 1572872 | tf_op jit(solution)/shard_map/ppermute | solution.py:46
  147.8 131.2 %copy-start.22 = (bf16[32,16,512]{2,1,0:T(8,128)(2,1)}, bf16[32,16,512]{2,1,0:T(8,128)(2,1)S(1)}, u32[]{:S(2)}) copy-start(bf16[32,16,512]{2,1,0:T(8,128)(2,1)S(1)} %collective-permute-done.8.refs_2_) | copy-start | bytes 1572868
  147.8 164.6 %collective-permute-start.13 = (bf16[32,16,512]{2,1,0:T(8,128)(2,1)}, bf16[32,16,512]{2,1,0:T(8,128)(2,1)}, u32[]{:S(2)}, u32[]{:S(2)}) collective-permute-start(bf16[32,16,512]{2,1,0:T(8,128)(2,1)} %get-tuple-element.94), channel_id=1, source_target_pairs={{0,28},{4,24},{8,20},{12,16},{16,12},{20,8},{24,4},{28,0},{1,29},{... | collective-permute-start | bytes 1572872 | tf_op jit(solution)/shard_map/ppermute | solution.py:46
  150.8 138.7 %copy-start.23 = (bf16[32,16,512]{2,1,0:T(8,128)(2,1)}, bf16[32,16,512]{2,1,0:T(8,128)(2,1)S(1)}, u32[]{:S(2)}) copy-start(bf16[32,16,512]{2,1,0:T(8,128)(2,1)S(1)} %collective-permute-done.9.refs_3_) | copy-start | bytes 1572868
  150.8 180.6 %collective-permute-start.1 = (bf16[32,16,512]{2,1,0:T(8,128)(2,1)}, bf16[32,16,512]{2,1,0:T(8,128)(2,1)S(1)}, u32[]{:S(2)}, u32[]{:S(2)}) collective-permute-start(bf16[32,16,512]{2,1,0:T(8,128)(2,1)} %get-tuple-element.81), channel_id=1, source_target_pairs={{0,8},{4,12},{8,0},{12,4},{16,24},{20,28},{24,16},{28,20},{1,9},{5... | collective-permute-start | bytes 1572872 | tf_op jit(solution)/shard_map/ppermute | solution.py:46
  279.0 52.4 %collective-permute-start.2 = (bf16[32,16,512]{2,1,0:T(8,128)(2,1)}, bf16[32,16,512]{2,1,0:T(8,128)(2,1)S(1)}, u32[]{:S(2)}, u32[]{:S(2)}) collective-permute-start(bf16[32,16,512]{2,1,0:T(8,128)(2,1)} %get-tuple-element.82), channel_id=1, source_target_pairs={{0,12},{4,8},{8,4},{12,0},{16,28},{20,24},{24,20},{28,16},{1,13},{... | collective-permute-start | bytes 1572872 | tf_op jit(solution)/shard_map/ppermute | solution.py:46
  289.5 68.2 %collective-permute-start.3 = (bf16[32,16,512]{2,1,0:T(8,128)(2,1)}, bf16[32,16,512]{2,1,0:T(8,128)(2,1)S(1)}, u32[]{:S(2)}, u32[]{:S(2)}) collective-permute-start(bf16[32,16,512]{2,1,0:T(8,128)(2,1)} %get-tuple-element.83), channel_id=1, source_target_pairs={{0,16},{4,20},{8,24},{12,28},{16,0},{20,4},{24,8},{28,12},{1,17},{... | collective-permute-start | bytes 1572872 | tf_op jit(solution)/shard_map/ppermute | solution.py:46
  289.9 78.0 %collective-permute-start.4 = (bf16[32,16,512]{2,1,0:T(8,128)(2,1)}, bf16[32,16,512]{2,1,0:T(8,128)(2,1)S(1)}, u32[]{:S(2)}, u32[]{:S(2)}) collective-permute-start(bf16[32,16,512]{2,1,0:T(8,128)(2,1)} %get-tuple-element.84), channel_id=1, source_target_pairs={{0,20},{4,16},{8,28},{12,24},{16,4},{20,0},{24,12},{28,8},{1,21},{... | collective-permute-start | bytes 1572872 | tf_op jit(solution)/shard_map/ppermute | solution.py:46
  312.4 55.6 %collective-permute-start.5 = (bf16[32,16,512]{2,1,0:T(8,128)(2,1)}, bf16[32,16,512]{2,1,0:T(8,128)(2,1)}, u32[]{:S(2)}, u32[]{:S(2)}) collective-permute-start(bf16[32,16,512]{2,1,0:T(8,128)(2,1)} %get-tuple-element.85), channel_id=1, source_target_pairs={{0,24},{4,28},{8,16},{12,20},{16,8},{20,12},{24,0},{28,4},{1,25},{... | collective-permute-start | bytes 1572872 | tf_op jit(solution)/shard_map/ppermute | solution.py:46
  331.4 36.6 %copy-start.13 = (bf16[32,16,512]{2,1,0:T(8,128)(2,1)}, bf16[32,16,512]{2,1,0:T(8,128)(2,1)S(1)}, u32[]{:S(2)}) copy-start(bf16[32,16,512]{2,1,0:T(8,128)(2,1)S(1)} %collective-permute-done.1.refs_2_) | copy-start | bytes 1572868
  331.4 36.6 %copy-start.15 = (bf16[32,16,512]{2,1,0:T(8,128)(2,1)}, bf16[32,16,512]{2,1,0:T(8,128)(2,1)S(1)}, u32[]{:S(2)}) copy-start(bf16[32,16,512]{2,1,0:T(8,128)(2,1)S(1)} %collective-permute-done.2.refs_3_) | copy-start | bytes 1572868
  456.0 52.8 %all-to-all-start.2 = ((bf16[8,4,32,1024]{3,2,1,0:T(8,128)(2,1)}), bf16[8,4,32,1024]{3,2,1,0:T(8,128)(2,1)S(1)}, u32[]{:S(2)}, u32[]{:S(2)}) async-start(bf16[8,4,32,1024]{3,2,1,0:T(8,128)(2,1)} %get-tuple-element.102), calls=%async_computation.2 | async-start | bytes 4194304 | tf_op jit(solution)/shard_map/all_to_all | solution.py:466
  469.9 18.6 %collective-permute-start.17 = (bf16[5,272,256]{2,1,0:T(8,128)(2,1)}, bf16[5,272,256]{2,1,0:T(8,128)(2,1)S(1)}, u32[]{:S(2)}, u32[]{:S(2)}) collective-permute-start(bf16[5,272,256]{2,1,0:T(8,128)(2,1)} %get-tuple-element.109), channel_id=1, source_target_pairs={{0,1},{1,0},{2,3},{3,2},{4,5},{5,4},{6,7},{7,6},{8,9},{9,8},{10,11... | collective-permute-start | bytes 2088968 | tf_op jit(solution)/shard_map/ppermute | solution.py:46
  471.5 32.8 %collective-permute-start.18 = (bf16[5,272,256]{2,1,0:T(8,128)(2,1)}, bf16[5,272,256]{2,1,0:T(8,128)(2,1)S(1)}, u32[]{:S(2)}, u32[]{:S(2)}) collective-permute-start(bf16[5,272,256]{2,1,0:T(8,128)(2,1)} %get-tuple-element.110), channel_id=1, source_target_pairs={{0,2},{1,3},{2,0},{3,1},{4,6},{5,7},{6,4},{7,5},{8,10},{9,11},{10,... | collective-permute-start | bytes 2088968 | tf_op jit(solution)/shard_map/ppermute | solution.py:46
  473.0 31.3 %collective-permute-start.19 = (bf16[5,272,256]{2,1,0:T(8,128)(2,1)}, bf16[5,272,256]{2,1,0:T(8,128)(2,1)S(1)}, u32[]{:S(2)}, u32[]{:S(2)}) collective-permute-start(bf16[5,272,256]{2,1,0:T(8,128)(2,1)} %get-tuple-element.111), channel_id=1, source_target_pairs={{0,3},{1,2},{2,1},{3,0},{4,7},{5,6},{6,5},{7,4},{8,11},{9,10},{10,... | collective-permute-start | bytes 2088968 | tf_op jit(solution)/shard_map/ppermute | solution.py:46
  488.6 37.4 %copy-start.29 = (bf16[5,272,256]{2,1,0:T(8,128)(2,1)}, bf16[5,272,256]{2,1,0:T(8,128)(2,1)S(1)}, u32[]{:S(2)}) copy-start(bf16[5,272,256]{2,1,0:T(8,128)(2,1)S(1)} %collective-permute-done.17.refs_4_) | copy-start | bytes 2088964
  510.1 52.6 %all-to-all-start.6 = ((bf16[8,4,32,1024]{3,2,1,0:T(8,128)(2,1)}), bf16[8,4,32,1024]{3,2,1,0:T(8,128)(2,1)S(1)}, u32[]{:S(2)}, u32[]{:S(2)}) async-start(bf16[8,4,32,1024]{3,2,1,0:T(8,128)(2,1)} %get-tuple-element.120), calls=%async_computation.6 | async-start | bytes 4194304 | tf_op jit(solution)/shard_map/all_to_all | solution.py:466
  522.5 15.9 %collective-permute-start.14 = (bf16[4,272,256]{2,1,0:T(8,128)(2,1)}, bf16[4,272,256]{2,1,0:T(8,128)(2,1)}, u32[]{:S(2)}, u32[]{:S(2)}) collective-permute-start(bf16[4,272,256]{2,1,0:T(8,128)(2,1)} %get-tuple-element.104), channel_id=1, source_target_pairs={{0,1},{1,0},{2,3},{3,2},{4,5},{5,4},{6,7},{7,6},{8,9},{9,8},{10,11... | collective-permute-start | bytes 1671176 | tf_op jit(solution)/shard_map/ppermute | solution.py:46
  524.0 26.9 %collective-permute-start.15 = (bf16[4,272,256]{2,1,0:T(8,128)(2,1)}, bf16[4,272,256]{2,1,0:T(8,128)(2,1)}, u32[]{:S(2)}, u32[]{:S(2)}) collective-permute-start(bf16[4,272,256]{2,1,0:T(8,128)(2,1)} %get-tuple-element.105), channel_id=1, source_target_pairs={{0,2},{1,3},{2,0},{3,1},{4,6},{5,7},{6,4},{7,5},{8,10},{9,11},{10,... | collective-permute-start | bytes 1671176 | tf_op jit(solution)/shard_map/ppermute | solution.py:46
  525.5 25.4 %collective-permute-start.16 = (bf16[4,272,256]{2,1,0:T(8,128)(2,1)}, bf16[4,272,256]{2,1,0:T(8,128)(2,1)}, u32[]{:S(2)}, u32[]{:S(2)}) collective-permute-start(bf16[4,272,256]{2,1,0:T(8,128)(2,1)} %get-tuple-element.106), channel_id=1, source_target_pairs={{0,3},{1,2},{2,1},{3,0},{4,7},{5,6},{6,5},{7,4},{8,11},{9,10},{10,... | collective-permute-start | bytes 1671176 | tf_op jit(solution)/shard_map/ppermute | solution.py:46
  562.7 52.2 %all-to-all-start.4 = ((bf16[8,3,32,1024]{3,2,1,0:T(8,128)(2,1)}), bf16[8,3,32,1024]{3,2,1,0:T(8,128)(2,1)}, u32[]{:S(2)}, u32[]{:S(2)}) async-start(bf16[8,3,32,1024]{3,2,1,0:T(8,128)(2,1)} %get-tuple-element.116), calls=%async_computation.4 | async-start | bytes 3145728 | tf_op jit(solution)/shard_map/all_to_all | solution.py:466
  567.0 17.8 %collective-permute-start.23 = (bf16[1280,256]{1,0:T(8,128)(2,1)}, bf16[1280,256]{1,0:T(8,128)(2,1)S(1)}, u32[]{:S(2)}, u32[]{:S(2)}) collective-permute-start(bf16[1280,256]{1,0:T(8,128)(2,1)} %get-tuple-element.113), channel_id=1, source_target_pairs={{0,1},{1,0},{2,3},{3,2},{4,5},{5,4},{6,7},{7,6},{8,9},{9,8},{10,11... | collective-permute-start | bytes 1966088 | tf_op jit(solution)/shard_map/ppermute | solution.py:46
  568.6 32.0 %collective-permute-start.24 = (bf16[1280,256]{1,0:T(8,128)(2,1)}, bf16[1280,256]{1,0:T(8,128)(2,1)}, u32[]{:S(2)}, u32[]{:S(2)}) collective-permute-start(bf16[1280,256]{1,0:T(8,128)(2,1)} %get-tuple-element.114), channel_id=1, source_target_pairs={{0,2},{1,3},{2,0},{3,1},{4,6},{5,7},{6,4},{7,5},{8,10},{9,11},{10,... | collective-permute-start | bytes 1966088 | tf_op jit(solution)/shard_map/ppermute | solution.py:46
  570.1 30.4 %collective-permute-start.25 = (bf16[1280,256]{1,0:T(8,128)(2,1)}, bf16[1280,256]{1,0:T(8,128)(2,1)}, u32[]{:S(2)}, u32[]{:S(2)}) collective-permute-start(bf16[1280,256]{1,0:T(8,128)(2,1)} %get-tuple-element.115), channel_id=1, source_target_pairs={{0,3},{1,2},{2,1},{3,0},{4,7},{5,6},{6,5},{7,4},{8,11},{9,10},{10,... | collective-permute-start | bytes 1966088 | tf_op jit(solution)/shard_map/ppermute | solution.py:46
  579.3 34.2 %collective-permute-start.20 = (bf16[4,272,256]{2,1,0:T(8,128)(2,1)}, bf16[4,272,256]{2,1,0:T(8,128)(2,1)S(1)}, u32[]{:S(2)}, u32[]{:S(2)}) collective-permute-start(bf16[4,272,256]{2,1,0:T(8,128)(2,1)} %get-tuple-element.122), channel_id=1, source_target_pairs={{0,1},{1,0},{2,3},{3,2},{4,5},{5,4},{6,7},{7,6},{8,9},{9,8},{10,11... | collective-permute-start | bytes 1671176 | tf_op jit(solution)/shard_map/ppermute | solution.py:46
  580.8 45.0 %collective-permute-start.21 = (bf16[4,272,256]{2,1,0:T(8,128)(2,1)}, bf16[4,272,256]{2,1,0:T(8,128)(2,1)}, u32[]{:S(2)}, u32[]{:S(2)}) collective-permute-start(bf16[4,272,256]{2,1,0:T(8,128)(2,1)} %get-tuple-element.123), channel_id=1, source_target_pairs={{0,2},{1,3},{2,0},{3,1},{4,6},{5,7},{6,4},{7,5},{8,10},{9,11},{10,... | collective-permute-start | bytes 1671176 | tf_op jit(solution)/shard_map/ppermute | solution.py:46
  584.9 40.9 %collective-permute-start.22 = (bf16[4,272,256]{2,1,0:T(8,128)(2,1)}, bf16[4,272,256]{2,1,0:T(8,128)(2,1)}, u32[]{:S(2)}, u32[]{:S(2)}) collective-permute-start(bf16[4,272,256]{2,1,0:T(8,128)(2,1)} %get-tuple-element.124), channel_id=1, source_target_pairs={{0,3},{1,2},{2,1},{3,0},{4,7},{5,6},{6,5},{7,4},{8,11},{9,10},{10,... | collective-permute-start | bytes 1671176 | tf_op jit(solution)/shard_map/ppermute | solution.py:46
  611.4 22.7 %collective-permute-start.26 = (bf16[1024,256]{1,0:T(8,128)(2,1)}, bf16[1024,256]{1,0:T(8,128)(2,1)S(1)}, u32[]{:S(2)}, u32[]{:S(2)}) collective-permute-start(bf16[1024,256]{1,0:T(8,128)(2,1)} %get-tuple-element.139), channel_id=1, source_target_pairs={{0,1},{1,0},{2,3},{3,2},{4,5},{5,4},{6,7},{7,6},{8,9},{9,8},{10,11... | collective-permute-start | bytes 1572872 | tf_op jit(solution)/shard_map/ppermute | solution.py:46
  612.4 42.5 %collective-permute-start.27 = (bf16[1024,256]{1,0:T(8,128)(2,1)}, bf16[1024,256]{1,0:T(8,128)(2,1)S(1)}, u32[]{:S(2)}, u32[]{:S(2)}) collective-permute-start(bf16[1024,256]{1,0:T(8,128)(2,1)} %get-tuple-element.140), channel_id=1, source_target_pairs={{0,2},{1,3},{2,0},{3,1},{4,6},{5,7},{6,4},{7,5},{8,10},{9,11},{10,... | collective-permute-start | bytes 1572872 | tf_op jit(solution)/shard_map/ppermute | solution.py:46
  613.5 41.4 %collective-permute-start.28 = (bf16[1024,256]{1,0:T(8,128)(2,1)}, bf16[1024,256]{1,0:T(8,128)(2,1)S(1)}, u32[]{:S(2)}, u32[]{:S(2)}) collective-permute-start(bf16[1024,256]{1,0:T(8,128)(2,1)} %get-tuple-element.141), channel_id=1, source_target_pairs={{0,3},{1,2},{2,1},{3,0},{4,7},{5,6},{6,5},{7,4},{8,11},{9,10},{10,... | collective-permute-start | bytes 1572872 | tf_op jit(solution)/shard_map/ppermute | solution.py:46
  621.9 48.1 %all-to-all-start.5 = ((bf16[4,3,272,256]{3,2,1,0:T(8,128)(2,1)}), bf16[4,3,272,256]{3,2,1,0:T(8,128)(2,1)S(1)}, u32[]{:S(2)}, u32[]{:S(2)}) async-start(bf16[4,3,272,256]{3,2,1,0:T(8,128)(2,1)} %get-tuple-element.118), calls=%async_computation.5 | async-start | bytes 3342336 | tf_op jit(solution)/shard_map/all_to_all | solution.py:51
  634.1 31.9 %copy-start.11 = (bf16[1024,256]{1,0:T(8,128)(2,1)}, bf16[1024,256]{1,0:T(8,128)(2,1)S(1)}, u32[]{:S(2)}) copy-start(bf16[1024,256]{1,0:T(8,128)(2,1)S(1)} %collective-permute-done.26.refs_4_) | copy-start | bytes 1572868
  666.1 15.1 %collective-permute-start.29 = (bf16[1024,256]{1,0:T(8,128)(2,1)}, bf16[1024,256]{1,0:T(8,128)(2,1)S(1)}, u32[]{:S(2)}, u32[]{:S(2)}) collective-permute-start(bf16[1024,256]{1,0:T(8,128)(2,1)} %get-tuple-element.147), channel_id=1, source_target_pairs={{0,1},{1,0},{2,3},{3,2},{4,5},{5,4},{6,7},{7,6},{8,9},{9,8},{10,11... | collective-permute-start | bytes 1572872 | tf_op jit(solution)/shard_map/ppermute | solution.py:46
  666.1 16.6 %collective-permute-start.30 = (bf16[1024,256]{1,0:T(8,128)(2,1)}, bf16[1024,256]{1,0:T(8,128)(2,1)S(1)}, u32[]{:S(2)}, u32[]{:S(2)}) collective-permute-start(bf16[1024,256]{1,0:T(8,128)(2,1)} %get-tuple-element.148), channel_id=1, source_target_pairs={{0,2},{1,3},{2,0},{3,1},{4,6},{5,7},{6,4},{7,5},{8,10},{9,11},{10,... | collective-permute-start | bytes 1572872 | tf_op jit(solution)/shard_map/ppermute | solution.py:46
  668.6 22.5 %collective-permute-start.31 = (bf16[1024,256]{1,0:T(8,128)(2,1)}, bf16[1024,256]{1,0:T(8,128)(2,1)S(1)}, u32[]{:S(2)}, u32[]{:S(2)}) collective-permute-start(bf16[1024,256]{1,0:T(8,128)(2,1)} %get-tuple-element.149), channel_id=1, source_target_pairs={{0,3},{1,2},{2,1},{3,0},{4,7},{5,6},{6,5},{7,4},{8,11},{9,10},{10,... | collective-permute-start | bytes 1572872 | tf_op jit(solution)/shard_map/ppermute | solution.py:46
  700.6 25.7 %all-to-all-start.7 = ((bf16[4,768,256]{2,1,0:T(8,128)(2,1)}), bf16[4,768,256]{2,1,0:T(8,128)(2,1)S(1)}, u32[]{:S(2)}, u32[]{:S(2)}) async-start(bf16[4,768,256]{2,1,0:T(8,128)(2,1)} %hidden_units.7), calls=%async_computation.7 | async-start | bytes 3145728 | tf_op jit(solution)/shard_map/all_to_all | solution.py:51
  (26 other events, 258.8 us)
